TPU v7x, 32 devices: a whole 2x2x4 slice. The times are simulated.
32 devices in a mesh: dp: 4 (over y, x), fsdp: 8 (over z, core).
Axes of the slice: x: 2, y: 2, z: 4, core: 2. Of those that a mesh axis runs over, the one named last changes fastest.
Arguments:
- tokens: bfloat16 [32, 256, 2048], P(None, ('dp', 'fsdp')), may hold values from -6 to 6
- cotangent: bfloat16 [32, 256, 2048], P(None, ('dp', 'fsdp')), may hold values from -6 to 6
- lengths: int32 [32], replicated, may hold values from 1 to 256, 6144 in all
- deal_order: int32 [32], replicated, may hold values from 0 to 31, each once
- norm_gain: float32 [2048], P(('dp', 'fsdp')), may hold values from 0.5 to 1.5
- in_weight: float32 [2048, 8192], P(('dp', 'fsdp')), may hold values from -0.125 to 0.125
- conv_weight: float32 [4096, 4], P(('dp', 'fsdp')), may hold values from -3 to 3
- conv_bias: float32 [4096], P(('dp', 'fsdp')), may hold values from -3 to 3
- x_weight: float32 [4096, 160], P(('dp', 'fsdp')), may hold values from -0.09375 to 0.09375
- dt_weight: float32 [4096, 128], P(('dp', 'fsdp')), may hold values from -0.5 to 0.5
- dt_bias: float32 [4096], P(('dp', 'fsdp')), may hold values from -6 to -2.5
- decay_log: float32 [4096, 16], P(('dp', 'fsdp')), may hold values from 0 to 2.77
- skip_gain: float32 [4096], P(('dp', 'fsdp')), may hold values from 0.5 to 1.5
- out_weight: float32 [4096, 2048], P(('dp', 'fsdp')), may hold values from -0.1875 to 0.1875
Outputs:
- output: bfloat16 [32, 256, 2048], P(None, ('dp', 'fsdp'))
- input_grad: bfloat16 [32, 256, 2048], P(None, ('dp', 'fsdp'))
- norm_gain_grad: float32 [2048], P(('dp', 'fsdp'))
- in_weight_grad: float32 [2048, 8192], P(('dp', 'fsdp'))
- conv_weight_grad: float32 [4096, 4], P(('dp', 'fsdp'))
- conv_bias_grad: float32 [4096], P(('dp', 'fsdp'))
- x_weight_grad: float32 [4096, 160], P(('dp', 'fsdp'))
- dt_weight_grad: float32 [4096, 128], P(('dp', 'fsdp'))
- dt_bias_grad: float32 [4096], P(('dp', 'fsdp'))
- decay_log_grad: float32 [4096, 16], P(('dp', 'fsdp'))
- skip_gain_grad: float32 [4096], P(('dp', 'fsdp'))
- out_weight_grad: float32 [4096, 2048], P(('dp', 'fsdp'))
Inputs may be any that keep to these rules, and one draw needn't show every extreme that they name: lengths[j] is the number of live tokens of sequence deal_order[j]; its other slots of 256 are padding; the largest is exactly 256 and they sum to 6144. `deal_order`: each sequence appears once.
All inputs are finite; a program needn't handle non-finite values.
Results may differ from a plain program's by a relative error of at most 0.0055.
The roundings to bfloat16 on the way count: a program that leaves them out, or rounds other values in their place, can miss the bound.
Values may be sent and summed in bfloat16 or wider, within the bound.
A program may use at most 320 MiB of HBM per device.

v0:
```python
import jax
import jax.numpy as jnp
from jax import lax
from jax.sharding import PartitionSpec as P

SPAN = 32


EPSILON = 1e-05


def for_sending(array):

    def short(part):
        return part.astype(jnp.bfloat16) if part.dtype == jnp.float32 else part

    return jax.tree.map(short, array)


def rms_scale(hidden, gain_vec):
    factor = lax.rsqrt(jnp.mean(hidden * hidden, axis=-1, keepdims=True) + EPSILON)
    return hidden * factor * gain_vec


def causal_conv(inner_part, kernel, shift_vec):
    kernel_width = kernel.shape[1]
    length = inner_part.shape[0]
    padded = jnp.pad(inner_part, ((kernel_width - 1, 0), (0, 0)))
    summed = jnp.zeros_like(inner_part) + shift_vec[None, :]
    for offset in range(kernel_width):
        summed = summed + kernel[:, offset][None, :] * padded[offset : offset + length]
    return jax.nn.silu(summed)


def span_pass(carried, pieces, decay_rate):
    delta_rate, drive_b, read_c, inputs = pieces
    results = []
    for position in range(delta_rate.shape[0]):
        factor = jnp.exp(delta_rate[position][None, :] * decay_rate)
        carried = (
            factor * carried
            + (delta_rate[position] * inputs[position])[None, :] * drive_b[position][:, None]
        )
        results.append(jnp.sum(carried * read_c[position][:, None], axis=0))
    return (carried, jnp.stack(results))


def selective_mix(dt_pre, dt_shift, log_rates, proj_bc, inputs, skip_vec, gate_pre):
    state_size = log_rates.shape[0]
    length, inner_dim = dt_pre.shape
    delta_rate = jax.nn.softplus(dt_pre + dt_shift[None, :])
    decay_rate = -jnp.exp(log_rates)
    blocks = length // SPAN

    def advance(carried, pieces):
        return span_pass(carried, pieces, decay_rate)

    advance = jax.checkpoint(advance)
    pieces = (
        delta_rate.reshape(blocks, SPAN, inner_dim),
        proj_bc[:, :state_size].reshape(blocks, SPAN, state_size),
        proj_bc[:, state_size:].reshape(blocks, SPAN, state_size),
        inputs.reshape(blocks, SPAN, inner_dim),
    )
    _, results = lax.scan(advance, jnp.zeros((state_size, inner_dim), jnp.float32), pieces)
    mixed_out = results.reshape(length, inner_dim) + skip_vec[None, :] * inputs
    return mixed_out * jax.nn.silu(gate_pre)


def body(
    tokens,
    cotangent,
    lengths,
    deal_order,
    norm_gain,
    in_weight,
    conv_weight,
    conv_bias,
    x_weight,
    dt_weight,
    dt_bias,
    decay_log,
    skip_gain,
    out_weight,
):
    masters = (
        norm_gain,
        in_weight,
        conv_weight,
        conv_bias,
        x_weight,
        dt_weight,
        dt_bias,
        decay_log,
        skip_gain,
        out_weight,
    )
    lowered = tuple((item.astype(jnp.bfloat16) for item in masters))
    gathered = jax.tree.map(
        lambda part, own: part.astype(own.dtype),
        lax.all_gather(for_sending(lowered), ("dp", "fsdp"), axis=0, tiled=True),
        lowered,
    )
    device = lax.axis_index(("dp", "fsdp"))
    seq_count = tokens.shape[0]
    slots = jnp.arange(seq_count, dtype=jnp.int32)
    picked_tokens = jnp.take(tokens, deal_order, axis=0)
    picked_grads = jnp.take(cotangent, deal_order, axis=0)
    arrived = (
        lax.all_to_all(picked_tokens, ("dp", "fsdp"), split_axis=0, concat_axis=1, tiled=True),
        lax.all_to_all(picked_grads, ("dp", "fsdp"), split_axis=0, concat_axis=1, tiled=True),
    )
    hidden = arrived[0][0].astype(jnp.float32)
    upstream = arrived[1][0].astype(jnp.float32)
    length = hidden.shape[0]
    live = jnp.sum(jnp.where(slots == device, lengths, 0))
    mask = (jnp.arange(length, dtype=jnp.int32) < live).astype(jnp.float32)[:, None]
    (
        gain_half,
        in_half,
        conv_half,
        shift_half,
        select_half,
        rank_half,
        bias_half,
        decay_half,
        skip_half,
        out_half,
    ) = gathered
    inner_dim = conv_half.shape[0]
    rank_dim = rank_half.shape[1]
    normed, norm_back = jax.vjp(rms_scale, hidden, gain_half.astype(jnp.float32))
    normed_low = normed.astype(jnp.bfloat16)
    both = jnp.dot(normed_low, in_half, preferred_element_type=jnp.float32)
    inputs, conv_back = jax.vjp(
        causal_conv,
        both[:, :inner_dim],
        conv_half.astype(jnp.float32),
        shift_half.astype(jnp.float32),
    )
    inputs_low = inputs.astype(jnp.bfloat16)
    projected = jnp.dot(inputs_low, select_half, preferred_element_type=jnp.float32)
    dt_low = projected[:, :rank_dim].astype(jnp.bfloat16)
    dt_pre = jnp.einsum("tr,er->te", dt_low, rank_half, preferred_element_type=jnp.float32)
    gated, mix_back = jax.vjp(
        selective_mix,
        dt_pre,
        bias_half.astype(jnp.float32),
        decay_half.astype(jnp.float32).T,
        projected[:, rank_dim:],
        inputs_low.astype(jnp.float32),
        skip_half.astype(jnp.float32),
        both[:, inner_dim:],
    )
    gated_low = gated.astype(jnp.bfloat16)
    branch = jnp.dot(gated_low, out_half, preferred_element_type=jnp.float32)
    result = (hidden + mask * branch).astype(jnp.bfloat16)
    again = jax.tree.map(
        lambda part, own: part.astype(own.dtype),
        lax.all_gather(for_sending(lowered), ("dp", "fsdp"), axis=0, tiled=True),
        lowered,
    )
    grad_branch = (upstream * mask).astype(jnp.bfloat16)
    grad_out = jnp.einsum("te,td->ed", gated_low, grad_branch, preferred_element_type=jnp.float32)
    grad_gated = jnp.einsum("td,ed->te", grad_branch, again[9], preferred_element_type=jnp.float32)
    grad_pre, grad_bias, grad_decay_rows, grad_bc, grad_inputs_scan, grad_skip, grad_gate = (
        mix_back(grad_gated)
    )
    grad_pre_low = grad_pre.astype(jnp.bfloat16)
    grad_rank = jnp.einsum("te,tr->er", grad_pre_low, dt_low, preferred_element_type=jnp.float32)
    grad_dt_low = jnp.dot(grad_pre_low, again[5], preferred_element_type=jnp.float32)
    grad_proj = jnp.concatenate([grad_dt_low, grad_bc], axis=1).astype(jnp.bfloat16)
    grad_select = jnp.einsum("te,tk->ek", inputs_low, grad_proj, preferred_element_type=jnp.float32)
    grad_inputs = grad_inputs_scan + jnp.einsum(
        "tk,ek->te", grad_proj, again[4], preferred_element_type=jnp.float32
    )
    grad_inner, grad_conv, grad_shift = conv_back(grad_inputs)
    grad_both = jnp.concatenate([grad_inner, grad_gate], axis=1).astype(jnp.bfloat16)
    grad_in = jnp.einsum("td,tf->df", normed_low, grad_both, preferred_element_type=jnp.float32)
    grad_normed = jnp.einsum("tf,df->td", grad_both, again[1], preferred_element_type=jnp.float32)
    grad_hidden, grad_gain = norm_back(grad_normed)
    grad_tokens = (upstream + grad_hidden).astype(jnp.bfloat16)
    summed = (
        lax.psum_scatter(grad_gain, ("dp", "fsdp"), scatter_dimension=0, tiled=True),
        lax.psum_scatter(grad_in, ("dp", "fsdp"), scatter_dimension=0, tiled=True),
        lax.psum_scatter(grad_conv, ("dp", "fsdp"), scatter_dimension=0, tiled=True),
        lax.psum_scatter(grad_shift, ("dp", "fsdp"), scatter_dimension=0, tiled=True),
        lax.psum_scatter(grad_select, ("dp", "fsdp"), scatter_dimension=0, tiled=True),
        lax.psum_scatter(grad_rank, ("dp", "fsdp"), scatter_dimension=0, tiled=True),
        lax.psum_scatter(grad_bias, ("dp", "fsdp"), scatter_dimension=0, tiled=True),
        lax.psum_scatter(grad_decay_rows.T, ("dp", "fsdp"), scatter_dimension=0, tiled=True),
        lax.psum_scatter(grad_skip, ("dp", "fsdp"), scatter_dimension=0, tiled=True),
        lax.psum_scatter(grad_out, ("dp", "fsdp"), scatter_dimension=0, tiled=True),
    )
    returned = (
        lax.all_to_all(result[None], ("dp", "fsdp"), split_axis=1, concat_axis=0, tiled=True),
        lax.all_to_all(grad_tokens[None], ("dp", "fsdp"), split_axis=1, concat_axis=0, tiled=True),
    )
    inverse = jnp.sum(jnp.where(deal_order[:, None] == slots[None, :], slots[:, None], 0), axis=0)
    out_rows = jnp.take(returned[0], inverse, axis=0)
    grad_rows = jnp.take(returned[1], inverse, axis=0)
    return (out_rows, grad_rows) + tuple(summed)


def solution(mesh):
    placed = (
        P(None, ("dp", "fsdp"), None),
        P(None, ("dp", "fsdp"), None),
        P(),
        P(),
        P(("dp", "fsdp")),
        P(("dp", "fsdp"), None),
        P(("dp", "fsdp"), None),
        P(("dp", "fsdp")),
        P(("dp", "fsdp"), None),
        P(("dp", "fsdp"), None),
        P(("dp", "fsdp")),
        P(("dp", "fsdp"), None),
        P(("dp", "fsdp")),
        P(("dp", "fsdp"), None),
    )
    return jax.shard_map(
        body,
        mesh=mesh,
        in_specs=placed,
        out_specs=(
            P(None, ("dp", "fsdp"), None),
            P(None, ("dp", "fsdp"), None),
            P(("dp", "fsdp")),
            P(("dp", "fsdp"), None),
            P(("dp", "fsdp"), None),
            P(("dp", "fsdp")),
            P(("dp", "fsdp"), None),
            P(("dp", "fsdp"), None),
            P(("dp", "fsdp")),
            P(("dp", "fsdp"), None),
            P(("dp", "fsdp")),
            P(("dp", "fsdp"), None),
        ),
        check_vma=False,
    )
```

profile of v0, /device:TPU:0, one launch (start us, length us, event | category | flops | bytes accessed | tf_op | source)
XLA Modules:
  0.0 2560.3 jit_solution(16101224027852184547)
XLA Ops:
  14.8 7.3 all-to-all-start
  23.2 68.1 %all-reduce.171 = bf16[2048]{0:T(1024)(128)(2,1)S(1)} all-reduce(bf16[2048]{0:T(1024)(128)(2,1)S(1)} %dynamic-update-slice), channel_id=1, replica_groups=mesh['dp'=4,'fsdp'=8] {'dp','fsdp'}, use_global_device_ids=true, to_apply=%add.171 | all-reduce | flops 2048 | bytes 8192
  91.3 41.8 %all_gather.35 = bf16[4096,4]{0,1:T(4,128)(2,1)S(1)} all-gather(bf16[128,4]{0,1:T(4,128)(2,1)S(1)} %convert_element_type.105), channel_id=1, replica_groups=mesh['dp'=4,'fsdp'=8] {'dp','fsdp'}, dimensions={0}, use_global_device_ids=true | all-gather | bytes 33792 | tf_op jit(solution)/shard_map/all_gather | solution.py:101
  133.1 37.0 %all-gather = bf16[32,1,128]{2,1,0:T(2,128)(2,1)S(1)} all-gather(bf16[1,1,128]{2,1,0:T(2,128)(2,1)S(1)} %convert_bitcast_fusion.3), channel_id=1, replica_groups=mesh['dp'=4,'fsdp'=8] {'dp','fsdp'}, dimensions={0}, use_global_device_ids=true | all-gather | bytes 8448 | tf_op jit(solution)/shard_map/all_gather | solution.py:101
  170.1 38.5 %all-gather.2 = bf16[32,1,128]{2,1,0:T(2,128)(2,1)S(1)} all-gather(bf16[1,1,128]{2,1,0:T(2,128)(2,1)S(1)} %convert_bitcast_fusion.1), channel_id=1, replica_groups=mesh['dp'=4,'fsdp'=8] {'dp','fsdp'}, dimensions={0}, use_global_device_ids=true | all-gather | bytes 8448 | tf_op jit(solution)/shard_map/all_gather | solution.py:101
  208.7 37.8 %all_gather.41 = bf16[4096,16]{0,1:T(8,128)(2,1)S(1)} all-gather(bf16[128,16]{0,1:T(8,128)(2,1)S(1)} %convert_element_type.117), channel_id=1, replica_groups=mesh['dp'=4,'fsdp'=8] {'dp','fsdp'}, dimensions={0}, use_global_device_ids=true | all-gather | bytes 135168 | tf_op jit(solution)/shard_map/all_gather | solution.py:101
  246.5 37.8 %all-gather.1 = bf16[32,1,128]{2,1,0:T(2,128)(2,1)S(1)} all-gather(bf16[1,1,128]{2,1,0:T(2,128)(2,1)S(1)} %convert_bitcast_fusion.2), channel_id=1, replica_groups=mesh['dp'=4,'fsdp'=8] {'dp','fsdp'}, dimensions={0}, use_global_device_ids=true | all-gather | bytes 8448 | tf_op jit(solution)/shard_map/all_gather | solution.py:101
  289.1 20.9 fusion.101
  314.7 22.3 all-to-all-done.2
  337.0 25.4 all-gather.14.cloned.1.call-done
  362.5 21.6 multiply_reduce_fusion.160
  386.7 27.9 %all-gather.10.cloned.1.call-done = bf16[4096,160]{0,1:T(8,128)(2,1)} async-done(((bf16[128,160]{0,1:T(8,128)(2,1)}), bf16[4096,160]{0,1:T(8,128)(2,1)}) %all-gather.10.cloned.1.call-update) | async-done | bytes 1310736 | tf_op jit(solution)/shard_map/all_gather | solution.py:101
  417.7 53.5 %all-gather.12.cloned.1.call-done = bf16[4096,128]{1,0:T(8,128)(2,1)} async-done(((bf16[128,128]{1,0:T(8,128)(2,1)}), bf16[4096,128]{1,0:T(8,128)(2,1)}) %all-gather.12.cloned.1.call-update) | async-done | bytes 1048592 | tf_op jit(solution)/shard_map/all_gather | solution.py:101
  471.1 6.9 compare_select_fusion.2
  480.4 156.4 %while.40 = (s32[]{:T(128)}, f32[16,4096]{1,0:T(8,128)S(1)}, f32[8,32,4096]{2,1,0:T(8,128)}, f32[8,16,4096]{2,1,0:T(8,128)}, f32[8,32,4096]{2,1,0:T(8,128)}, /*i...) while((s32[]{:T(128)}, f32[16,4096]{1,0:T(8,128)S(1)}, ...), condition=%wide.region_35.37_spmd.clone, body=%wide.region_2.36_spmd.clone.sunk | while | flops 18808864 | bytes 16497289 | solution.py:65
  643.1 257.9 %while.41 = (s32[]{:T(128)}, f32[16,4096]{1,0:T(8,128)S(1)}, f32[16,4096]{1,0:T(8,128)S(1)}, f32[8,32,4096]{2,1,0:T(8,128)}, f32[8,32,16]{2,1,0:T(8,128)}, /*ind...) while((s32[]{:T(128)}, f32[16,4096]{1,0:T(8,128)S(1)}, ...), condition=%wide.region_166.168_spmd.clone, body=%wide.region_37.167_spmd.clone.sunk | while | flops 80246784 | bytes 46582236 | solution.py:65
  903.0 6.5 bitcast_add_fusion
  914.8 20.3 multiply_reduce_fusion.163
  944.2 14.9 fusion.96
  959.2 9.2 fusion.73
  968.4 25.8 %fusion.75 = f32[2048,8192]{1,0:T(8,128)} fusion(bf16[256,4096]{1,0:T(8,128)(2,1)} %get-tuple-element.1179, bf16[256,4096]{1,0:T(8,128)(2,1)} %fusion.73, bf16[32,8,2048]{2,1,0:T(8,128)(2,1)S(1)} %copy-done.5, f32[2048]{0:T(1024)S(1)} %copy-done.19, f32[256]{0:T(256)S(1)} %copy-done.23), kind=kOutput, calls=%fused_computation.727 | convolution fusion | flops 8600420352 | bytes 72360960 | tf_op jit(solution)/shard_map/td,tf->df/dot_general | solution.py:179
  994.2 15.7 fusion.86
  1012.8 7.8 reduce.4
  1027.8 8.5 fusion.84
  1037.9 6.8 reduce.5
  1046.6 12.9 all-to-all-done.3
  1062.4 47.2 %all-reduce.176 = (f32[2048]{0:T(1024)S(1)}, f32[4096]{0:T(1024)S(1)}, f32[4096]{0:T(1024)S(1)}, f32[4096]{0:T(1024)S(1)}) all-reduce(f32[2048]{0:T(1024)S(1)} %get-tuple-element.716, f32[4096]{0:T(1024)S(1)} %get-tuple-element.714, f32[4096]{0:T(1024)S(1)} %get-tuple-element.805, ...), channel_id=2, replica_groups=mesh['dp'=4,'fsdp'=8] {'dp','fsdp'}, use_global_device_ids=true, to_apply=%region_169.171.clone | all-reduce | flops 14336 | bytes 114688
  1127.3 82.1 %reduce-scatter.15.cloned.1.call-done = f32[128,16]{0,1:T(8,128)} async-done(((f32[4096,16]{0,1:T(8,128)}), f32[128,16]{0,1:T(8,128)}) %reduce-scatter.15.cloned.1.call-update) | async-done | bytes 8208 | tf_op jit(solution)/shard_map/reduce_scatter | solution.py:191
  1209.4 135.9 %reduce-scatter.13.cloned.1.call-done = f32[128,128]{1,0:T(8,128)} async-done(((f32[4096,128]{1,0:T(8,128)}), f32[128,128]{1,0:T(8,128)}) %reduce-scatter.13.cloned.1.call-update) | async-done | bytes 65552 | tf_op jit(solution)/shard_map/reduce_scatter | solution.py:189
  1345.3 137.8 %reduce-scatter.11.cloned.1.call-done = f32[128,160]{0,1:T(8,128)} async-done(((f32[4096,160]{0,1:T(8,128)}), f32[128,160]{0,1:T(8,128)}) %reduce-scatter.11.cloned.1.call-update) | async-done | bytes 81936 | tf_op jit(solution)/shard_map/reduce_scatter | solution.py:188
  1483.1 361.3 %reduce-scatter.17.cloned.1.call-done = f32[128,2048]{1,0:T(8,128)} async-done(((f32[4096,2048]{1,0:T(8,128)}), f32[128,2048]{1,0:T(8,128)}) %reduce-scatter.17.cloned.1.call-update) | async-done | bytes 1048592 | tf_op jit(solution)/shard_map/reduce_scatter | solution.py:193
  1844.4 708.8 %reduce-scatter.9.cloned.1.call-done = f32[64,8192]{1,0:T(8,128)} async-done(((f32[2048,8192]{1,0:T(8,128)}), f32[64,8192]{1,0:T(8,128)}) %reduce-scatter.9.cloned.1.call-update) | async-done | bytes 2097168 | tf_op jit(solution)/shard_map/reduce_scatter | solution.py:185
  (993 shorter events, 491.0 us)
Async XLA Ops:
  7.2 281.9 %all-gather.8.cloned.1.call-start = ((), (), s32[]{:S(2)}) async-start(), calls=%async_computation.10 | async-start | bytes 34603008 | tf_op jit(solution)/shard_map/all_gather | solution.py:101
  10.1 352.3 %all-gather.14.cloned.1.call-start = ((), (), s32[]{:S(2)}) async-start(), calls=%async_computation.13 | async-start | bytes 17301504 | tf_op jit(solution)/shard_map/all_gather | solution.py:101
  11.1 403.5 %all-gather.10.cloned.1.call-start = ((), (), s32[]{:S(2)}) async-start(), calls=%async_computation.11 | async-start | bytes 1351680 | tf_op jit(solution)/shard_map/all_gather | solution.py:101
  12.5 78.8 %copy-start.38 = (f32[128,4]{0,1:T(4,128)S(1)}, f32[128,4]{0,1:T(4,128)}, u32[]{:S(2)}) copy-start(f32[128,4]{0,1:T(4,128)} %param.26) | copy-start | bytes 6148
  12.5 120.5 %copy-start.42 = (f32[128]{0:T(128)S(1)}, f32[128]{0:T(128)}, u32[]{:S(2)}) copy-start(f32[128]{0:T(128)} %param.27) | copy-start | bytes 1540
  12.6 157.6 %copy-start.43 = (f32[128]{0:T(128)S(1)}, f32[128]{0:T(128)}, u32[]{:S(2)}) copy-start(f32[128]{0:T(128)} %param.32) | copy-start | bytes 1540
  12.6 196.1 %copy-start.44 = (f32[128]{0:T(128)S(1)}, f32[128]{0:T(128)}, u32[]{:S(2)}) copy-start(f32[128]{0:T(128)} %param.30) | copy-start | bytes 1540
  12.6 196.1 %copy-start.37 = (f32[128,16]{0,1:T(8,128)S(1)}, f32[128,16]{0,1:T(8,128)}, u32[]{:S(2)}) copy-start(f32[128,16]{0,1:T(8,128)} %param.31) | copy-start | bytes 24580
  12.6 271.7 %copy-start.45 = (s32[32]{0:T(128)S(1)}, s32[32]{0:T(128)}, u32[]{:S(2)}) copy-start(s32[32]{0:T(128)} %param.22) | copy-start | bytes 388
  14.8 271.0 %all-to-all-start = ((bf16[32,8,2048]{2,1,0:T(8,128)(2,1)}), bf16[32,8,2048]{2,1,0:T(8,128)(2,1)S(1)}, u32[]{:S(2)}, u32[]{:S(2)}) async-start(bf16[32,8,2048]{2,1,0:T(8,128)(2,1)} %get-tuple-element.1192), calls=%async_computation | async-start | bytes 2097152 | tf_op jit(solution)/shard_map/all_to_all | solution.py:110
  22.1 449.0 %all-gather.12.cloned.1.call-start = ((), (), s32[]{:S(2)}) async-start(), calls=%async_computation.12 | async-start | bytes 1081344 | tf_op jit(solution)/shard_map/all_gather | solution.py:101
  91.3 218.8 %copy-start.18 = (f32[2048]{0:T(1024)}, f32[2048]{0:T(1024)S(1)}, u32[]{:S(2)}) copy-start(f32[2048]{0:T(1024)S(1)} %convert_element_type.109) | copy-start | bytes 24580
  246.5 63.6 %copy-start.13 = (bf16[4096,16]{0,1:T(8,128)(2,1)}, bf16[4096,16]{0,1:T(8,128)(2,1)S(1)}, u32[]{:S(2)}) copy-start(bf16[4096,16]{0,1:T(8,128)(2,1)S(1)} %all_gather.41) | copy-start | bytes 393220
  285.6 76.8 %copy-start.39 = (f32[256]{0:T(256)}, f32[256]{0:T(256)S(1)}, u32[]{:S(2)}) copy-start(f32[256]{0:T(256)S(1)} %compare_convert_fusion) | copy-start | bytes 3076
  285.7 76.8 %copy-start.27 = (f32[4096,1]{0,1:T(1,128)}, f32[4096,1]{0,1:T(1,128)S(1)}, u32[]{:S(2)}) copy-start(f32[4096,1]{0,1:T(1,128)S(1)} %get-tuple-element.1186) | copy-start | bytes 49156
  285.7 76.8 %copy-start.29 = (f32[4096,1]{0,1:T(1,128)}, f32[4096,1]{0,1:T(1,128)S(1)}, u32[]{:S(2)}) copy-start(f32[4096,1]{0,1:T(1,128)S(1)} %get-tuple-element.1187) | copy-start | bytes 49156
  285.7 76.8 %copy-start.31 = (f32[4096,1]{0,1:T(1,128)}, f32[4096,1]{0,1:T(1,128)S(1)}, u32[]{:S(2)}) copy-start(f32[4096,1]{0,1:T(1,128)S(1)} %get-tuple-element.1188) | copy-start | bytes 49156
  285.7 76.8 %copy-start.33 = (f32[4096,1]{0,1:T(1,128)}, f32[4096,1]{0,1:T(1,128)S(1)}, u32[]{:S(2)}) copy-start(f32[4096,1]{0,1:T(1,128)S(1)} %get-tuple-element.1189) | copy-start | bytes 49156
  285.8 51.2 %all-to-all-start.2 = ((bf16[32,8,2048]{2,1,0:T(8,128)(2,1)}), bf16[32,8,2048]{2,1,0:T(8,128)(2,1)S(1)}, u32[]{:S(2)}, u32[]{:S(2)}) async-start(bf16[32,8,2048]{2,1,0:T(8,128)(2,1)} %get-tuple-element.1193), calls=%async_computation.2 | async-start | bytes 2097152 | tf_op jit(solution)/shard_map/all_to_all | solution.py:111
  288.5 823.5 %reduce-scatter.19.cloned.1.call-start = ((), (), s32[]{:S(2)}) async-start(), calls=%async_computation.19 | async-start | bytes 2162688
  337.0 25.4 copy-start.7
  384.1 32.7 %copy-start.2 = (bf16[256,4096]{1,0:T(8,128)(2,1)}, bf16[256,4096]{1,0:T(8,128)(2,1)S(1)}, u32[]{:S(2)}) copy-start(bf16[256,4096]{1,0:T(8,128)(2,1)S(1)} %get-tuple-element.803) | copy-start | bytes 6291460
  416.8 61.2 %copy-start.20 = (f32[256,160]{0,1:T(8,128)}, f32[256,160]{0,1:T(8,128)S(1)}, u32[]{:S(2)}) copy-start(f32[256,160]{0,1:T(8,128)S(1)} %fusion.118) | copy-start | bytes 491524
  937.3 272.1 %reduce-scatter.15.cloned.1.call-start = ((), (), s32[]{:S(2)}) async-start(), calls=%async_computation.17 | async-start | bytes 270336 | tf_op jit(solution)/shard_map/reduce_scatter | solution.py:191
  938.1 407.1 %reduce-scatter.13.cloned.1.call-start = ((), (), s32[]{:S(2)}) async-start(), calls=%async_computation.16 | async-start | bytes 2162688 | tf_op jit(solution)/shard_map/reduce_scatter | solution.py:189
  940.4 542.7 %reduce-scatter.11.cloned.1.call-start = ((), (), s32[]{:S(2)}) async-start(), calls=%async_computation.15 | async-start | bytes 2703360 | tf_op jit(solution)/shard_map/reduce_scatter | solution.py:188
  944.1 900.2 %reduce-scatter.17.cloned.1.call-start = ((), (), s32[]{:S(2)}) async-start(), calls=%async_computation.18 | async-start | bytes 34603008 | tf_op jit(solution)/shard_map/reduce_scatter | solution.py:193
  959.1 1594.1 %reduce-scatter.9.cloned.1.call-start = ((), (), s32[]{:S(2)}) async-start(), calls=%async_computation.14 | async-start | bytes 69206016 | tf_op jit(solution)/shard_map/reduce_scatter | solution.py:185
  1023.6 35.9 %all-to-all-start.3 = ((bf16[32,2,8192]{2,1,0:T(2,128)(2,1)}), bf16[32,2,8192]{2,1,0:T(2,128)(2,1)}, u32[]{:S(2)}, u32[]{:S(2)}) async-start(bf16[32,2,8192]{2,1,0:T(2,128)(2,1)} %reshape.1755), calls=%async_computation.3 | async-start | bytes 2097152 | tf_op jit(solution)/shard_map/all_to_all | solution.py:197
  1037.9 24.5 copy-start.26
  1059.5 59.8 %all-to-all-start.1 = ((bf16[32,2,8192]{2,1,0:T(2,128)(2,1)}), bf16[32,2,8192]{2,1,0:T(2,128)(2,1)S(1)}, u32[]{:S(2)}, u32[]{:S(2)}) async-start(bf16[32,2,8192]{2,1,0:T(2,128)(2,1)} %reshape.1753), calls=%async_computation.1 | async-start | bytes 2097152 | tf_op jit(solution)/shard_map/all_to_all | solution.py:196
  1121.9 1431.2 %copy-start.1 = (bf16[32,8,2048]{2,1,0:T(8,128)(2,1)S(1)}, bf16[32,8,2048]{2,1,0:T(8,128)(2,1)}, u32[]{:S(2)}) copy-start(bf16[32,8,2048]{2,1,0:T(8,128)(2,1)} %param.20) | copy-start | bytes 3145732
  (30 other events, 248.1 us)
Sparse Core Ops, SparseCore 0:
  11.6 220.4 all-gather.7
  235.1 127.2 all-gather.13
  365.9 48.6 all-gather.9
  418.0 53.0 all-gather.11
  937.4 138.2 reduce-scatter.18
  1078.5 130.8 reduce-scatter.14
  1212.2 133.0 reduce-scatter.12
  1348.2 134.8 reduce-scatter.10
  1486.1 358.2 reduce-scatter.16
  1847.3 705.8 reduce-scatter.8
where the time goes:
time: 2570 us; the launch traced here: 2560 us
  waiting for transfers between devices  1570 us (61%)
  other arithmetic  314 us (12%)
  blocking collectives  308 us (12%)
  local copies, waits for them, and re-layouts  188 us (7%)
  matrix products  143 us (6%)
    reduce_scatter x1, waiting for transfers between devices, body(): lax.psum_scatter(grad_in, ('dp', 'fsdp'), scatter_dimension=0, tiled=True)  709 us
    reduce_scatter x1, waiting for transfers between devices, body(): lax.psum_scatter(grad_out, ('dp', 'fsdp'), scatter_dimension=0, tiled=True)  361 us
    all_gather x5, blocking collectives, body(): lax.all_gather(for_sending(lowered), ('dp', 'fsdp'), axis=0, tiled=True)  193 us
    reduce_scatter x1, waiting for transfers between devices, body(): lax.psum_scatter(grad_select, ('dp', 'fsdp'), scatter_dimension=0, tiled=...  138 us
    reduce_scatter x1, waiting for transfers between devices, body(): lax.psum_scatter(grad_rank, ('dp', 'fsdp'), scatter_dimension=0, tiled=True)  136 us
    unnamed x2, blocking collectives  115 us
    all_gather x4, waiting for transfers between devices, body(): lax.all_gather(for_sending(lowered), ('dp', 'fsdp'), axis=0, tiled=True)  107 us
    reduce_sum x136, other arithmetic, span_pass(): results.append(jnp.sum(carried * read_c[position][:, None], axis=0))  100 us
  transfers between devices with their start and end apart: 14, of which 10 were waited for; matrix products, arithmetic and copies ran while one was open for 7% of the time, Pallas kernels for 0%

commit v1 on v0

v1 whole, which is shorter than its diff:
```python
import functools
import jax
import jax.numpy as jnp
from jax import lax
from jax.experimental import pallas as pl
from jax.experimental.pallas import tpu as pltpu
from jax.sharding import PartitionSpec as P

EPSILON = 1e-05
STEPS = 32
LOG2E = 1.4426950408889634
BOTH = ("dp", "fsdp")
F32 = jnp.float32
BF16 = jnp.bfloat16
VMEM_BYTES = 60 * 1024 * 1024


def dot(a, b, dims=((1,), (0,))):
    return lax.dot_general(a, b, (dims, ((), ())), preferred_element_type=F32)


def sigmoid(v):
    return 1.0 / (1.0 + jnp.exp(-v))


def softplus(v):
    return jnp.maximum(v, 0.0) + jnp.log1p(jnp.exp(-jnp.abs(v)))


def rms_normed(x, gain):
    factor = lax.rsqrt(jnp.mean(x * x, axis=-1, keepdims=True) + EPSILON)
    return (x * factor * gain).astype(BF16)


def front_kernel(
    x_ref, gain_ref, win_ref, cw_ref, cb_ref, xw_ref, inner_ref, gate_ref, inp_ref, proj_ref, pad_ref, *, slots
):
    rows = x_ref.shape[0]
    width = inner_ref.shape[1]
    halo = 3 * slots
    normed = rms_normed(x_ref[...].astype(F32), gain_ref[...])
    both = dot(normed, win_ref[...])
    gate_ref[...] = both[:, width:]
    inner = both[:, :width]
    inner_ref[...] = inner

    @pl.when(pl.program_id(0) == 0)
    def _():
        pad_ref[0:halo, :] = jnp.zeros((halo, width), F32)

    pad_ref[halo : halo + rows, :] = inner
    total = jnp.broadcast_to(cb_ref[...], (rows, width))
    for tap in range(4):
        total = total + cw_ref[tap : tap + 1, :] * pad_ref[tap * slots : tap * slots + rows, :]
    inp = (total * sigmoid(total)).astype(BF16)
    inp_ref[...] = inp
    proj_ref[...] = dot(inp, xw_ref[...])
    pad_ref[0:halo, :] = pad_ref[rows : rows + halo, :]


def mix_kernel(
    dtl_ref, bc_ref, inp_ref, gate_ref, dtw_ref, dtb_ref, rate_ref, skip_ref, ow_ref,
    y_ref, ck_ref, br_ref, h_scr, delta_scr, u_scr, rate_scr, *, slots
):
    rows, width = inp_ref.shape
    steps = rows // slots
    states = rate_ref.shape[0]
    chunk = max(128, 2048 // slots)

    @pl.when(pl.program_id(0) == 0)
    def _():
        h_scr[...] = jnp.zeros_like(h_scr)
        for n in range(states):
            rate_scr[n] = jnp.broadcast_to(rate_ref[n : n + 1, :] * LOG2E, (slots, width))

    ck_ref[0] = h_scr[...]
    delta = softplus(dot(dtl_ref[...], dtw_ref[...], ((1,), (1,))) + dtb_ref[...])
    delta_scr[...] = delta
    u_scr[...] = delta * inp_ref[...].astype(F32)
    for first in range(0, width, chunk):
        lanes = slice(first, first + chunk)

        def step(t, held):
            at = pl.ds(pl.multiple_of(t * slots, slots), slots)
            d = delta_scr[at, lanes]
            u = u_scr[at, lanes]
            bc = bc_ref[at, :]
            y = jnp.zeros_like(d)
            after = []
            for n in range(states):
                h = jnp.exp2(d * rate_scr[n, :, lanes]) * held[n] + u * bc[:, n : n + 1]
                y = y + h * bc[:, states + n : states + n + 1]
                after.append(h)
            y_ref[at, lanes] = y
            return tuple(after)

        held = lax.fori_loop(0, steps, step, tuple(h_scr[n, :, lanes] for n in range(states)))
        for n in range(states):
            h_scr[n, :, lanes] = held[n]
    y = y_ref[...] + skip_ref[...] * inp_ref[...].astype(F32)
    y_ref[...] = y
    gate = gate_ref[...]
    gated = (y * (gate * sigmoid(gate))).astype(BF16)
    br_ref[...] = dot(gated, ow_ref[...]).astype(br_ref.dtype)


def lane_sums(parts):
    lane = lax.broadcasted_iota(jnp.int32, parts[0].shape, 1)
    bit = 1
    while len(parts) > 1:
        low = (lane & bit) == 0
        merged = []
        for j in range(0, len(parts), 2):
            kept = jnp.where(low, parts[j], parts[j + 1])
            moved = jnp.where(low, parts[j + 1], parts[j])
            merged.append(kept + pltpu.roll(moved, bit, 1))
        parts = merged
        bit *= 2
    total = parts[0]
    while bit < total.shape[1]:
        total = total + pltpu.roll(total, bit, 1)
        bit *= 2
    return total


def back_kernel(
    gb_ref, dtl_ref, bc_ref, inp_ref, gate_ref, y_ref, ck_ref, dtw_ref, dtb_ref, rate_ref, skip_ref, ow_ref,
    gis_ref, ggate_ref, gproj_ref, gout_ref, grank_ref, gdec_ref, gskip_ref, gbias_ref,
    lam_scr, dacc_scr, sacc_scr, bacc_scr, rate_scr, delta_scr, u_scr, gy_scr, gu_scr, gd_scr, h_scr, a_scr, gbc_scr, *, slots
):
    rows, width = inp_ref.shape
    steps = rows // slots
    states = rate_ref.shape[0]
    rank = dtl_ref.shape[1]
    chunk = 128
    step_id = pl.program_id(0)

    @pl.when(step_id == 0)
    def _():
        lam_scr[...] = jnp.zeros_like(lam_scr)
        dacc_scr[...] = jnp.zeros_like(dacc_scr)
        sacc_scr[...] = jnp.zeros_like(sacc_scr)
        bacc_scr[...] = jnp.zeros_like(bacc_scr)
        gout_ref[...] = jnp.zeros_like(gout_ref)
        grank_ref[...] = jnp.zeros_like(grank_ref)
        for n in range(states):
            rate_scr[n] = jnp.broadcast_to(rate_ref[n : n + 1, :] * LOG2E, (slots, width))

    gb = gb_ref[...]
    gate = gate_ref[...]
    sig = sigmoid(gate)
    silu = gate * sig
    y = y_ref[...]
    inp = inp_ref[...].astype(F32)
    g_gated = dot(gb, ow_ref[...], ((1,), (1,)))
    g_y = g_gated * silu
    gy_scr[...] = g_y
    ggate_ref[...] = (g_gated * y * (sig * (1.0 + gate * (1.0 - sig)))).astype(BF16)
    gout_ref[...] += dot((y * silu).astype(BF16), gb, ((0,), (0,)))
    sacc_scr[...] += jnp.sum((g_y * inp).reshape(steps, slots, width), axis=0)
    z = dot(dtl_ref[...], dtw_ref[...], ((1,), (1,))) + dtb_ref[...]
    delta = softplus(z)
    delta_scr[...] = delta
    u_scr[...] = delta * inp

    for first in range(0, width, chunk):
        lanes = slice(first, first + chunk)

        def replay(t, held):
            at = pl.ds(pl.multiple_of(t * slots, slots), slots)
            d = delta_scr[at, lanes]
            u = u_scr[at, lanes]
            gy = gy_scr[at, lanes]
            bc = bc_ref[at, :]
            after = []
            for n in range(states):
                h_scr[t, n] = held[n]
                a = jnp.exp2(d * rate_scr[n, :, lanes])
                a_scr[t, n] = a
                h = a * held[n] + u * bc[:, n : n + 1]
                part = h * gy
                if first:
                    part = part + gbc_scr[t, states + n]
                gbc_scr[t, states + n] = part
                after.append(h)
            return tuple(after)

        lax.fori_loop(0, steps, replay, tuple(ck_ref[0, n, :, lanes] for n in range(states)))

        def reverse(k, held):
            lams, sums = held
            t = steps - 1 - k
            at = pl.ds(pl.multiple_of(t * slots, slots), slots)
            d = delta_scr[at, lanes]
            u = u_scr[at, lanes]
            gy = gy_scr[at, lanes]
            bc = bc_ref[at, :]
            gu = jnp.zeros_like(d)
            gd = jnp.zeros_like(d)
            lams_after, sums_after = [], []
            for n in range(states):
                lam = lams[n] + gy * bc[:, states + n : states + n + 1]
                gu = gu + lam * bc[:, n : n + 1]
                part = lam * u
                if first:
                    part = part + gbc_scr[t, n]
                gbc_scr[t, n] = part
                carried = a_scr[t, n] * lam
                q = carried * h_scr[t, n]
                gd = gd + q * rate_scr[n, :, lanes]
                sums_after.append(sums[n] + q * d)
                lams_after.append(carried)
            gu_scr[at, lanes] = gu
            gd_scr[at, lanes] = gd
            return tuple(lams_after), tuple(sums_after)

        lams, sums = lax.fori_loop(
            0,
            steps,
            reverse,
            (
                tuple(lam_scr[n, :, lanes] for n in range(states)),
                tuple(dacc_scr[n, :, lanes] for n in range(states)),
            ),
        )
        for n in range(states):
            lam_scr[n, :, lanes] = lams[n]
            dacc_scr[n, :, lanes] = sums[n]

    def reduce_lanes(t, carry):
        at = pl.ds(pl.multiple_of(t * slots, slots), slots)
        total = lane_sums([gbc_scr[t, k] for k in range(2 * states)])
        gproj_ref[at, rank:] = total[:, : 2 * states]
        return carry

    lax.fori_loop(0, steps, reduce_lanes, 0)
    gu = gu_scr[...]
    gis_ref[...] = gu * delta_scr[...] + skip_ref[...] * gy_scr[...]
    g_pre = (gd_scr[...] * (1.0 / LOG2E) + gu * inp) * sigmoid(z)
    bacc_scr[...] += jnp.sum(g_pre.reshape(steps, slots, width), axis=0)
    g_low = g_pre.astype(BF16)
    grank_ref[...] += dot(g_low, dtl_ref[...], ((0,), (0,)))
    gproj_ref[:, :rank] = dot(g_low, dtw_ref[...])

    @pl.when(step_id == pl.num_programs(0) - 1)
    def _():
        for n in range(states):
            gdec_ref[n : n + 1, :] = jnp.sum(dacc_scr[n], axis=0, keepdims=True) * rate_ref[n : n + 1, :]
        gskip_ref[...] = jnp.sum(sacc_scr[...], axis=0, keepdims=True)
        gbias_ref[...] = jnp.sum(bacc_scr[...], axis=0, keepdims=True)


def tail_kernel(
    gproj_ref, inp_ref, gis_ref, ggate_ref, inner_ref, before_ref, x_ref, gain_ref, win_ref, xw_ref, cw_ref, cb_ref,
    gnorm_ref, gin_ref, gsel_ref, gcw_ref, gcb_ref, pad_scr, gpad_scr, wacc_scr, cacc_scr, *, slots
):
    rows, width = inp_ref.shape
    steps = rows // slots
    halo = 3 * slots
    step_id = pl.program_id(0)
    last = pl.num_programs(0) - 1

    @pl.when(step_id == 0)
    def _():
        gpad_scr[rows : rows + halo, :] = jnp.zeros((halo, width), F32)
        wacc_scr[...] = jnp.zeros_like(wacc_scr)
        cacc_scr[...] = jnp.zeros_like(cacc_scr)
        gin_ref[...] = jnp.zeros_like(gin_ref)
        gsel_ref[...] = jnp.zeros_like(gsel_ref)

    gproj = gproj_ref[...]
    gsel_ref[...] += dot(inp_ref[...], gproj, ((0,), (0,)))
    g_inputs = gis_ref[...] + dot(gproj, xw_ref[...], ((1,), (1,)))
    first = (step_id < last).astype(F32)
    pad_scr[0:halo, :] = before_ref[slots : slots + halo, :] * first
    pad_scr[halo : halo + rows, :] = inner_ref[...]
    total = jnp.broadcast_to(cb_ref[...], (rows, width))
    for tap in range(4):
        total = total + cw_ref[tap : tap + 1, :] * pad_scr[tap * slots : tap * slots + rows, :]
    sig = sigmoid(total)
    g_conv = g_inputs * (sig * (1.0 + total * (1.0 - sig)))
    gpad_scr[0:rows, :] = g_conv
    g_inner = jnp.zeros((rows, width), F32)
    for tap in range(4):
        back = (3 - tap) * slots
        g_inner = g_inner + cw_ref[tap : tap + 1, :] * gpad_scr[back : back + rows, :]
        wacc_scr[tap] += jnp.sum(
            (g_conv * pad_scr[tap * slots : tap * slots + rows, :]).reshape(steps, slots, width), axis=0
        )
    cacc_scr[...] += jnp.sum(g_conv.reshape(steps, slots, width), axis=0)
    gpad_scr[rows : rows + halo, :] = gpad_scr[0:halo, :]
    g_both = jnp.concatenate([g_inner.astype(BF16), ggate_ref[...]], axis=1)
    normed = rms_normed(x_ref[...].astype(F32), gain_ref[...])
    gin_ref[...] += dot(normed, g_both, ((0,), (0,)))
    gnorm_ref[...] = dot(g_both, win_ref[...], ((1,), (1,))).astype(gnorm_ref.dtype)

    @pl.when(step_id == last)
    def _():
        for tap in range(4):
            gcw_ref[tap : tap + 1, :] = jnp.sum(wacc_scr[tap], axis=0, keepdims=True)
        gcb_ref[...] = jnp.sum(cacc_scr[...], axis=0, keepdims=True)


def whole(shape):
    return pl.BlockSpec(shape, lambda i: (0,) * len(shape))


def params():
    return pltpu.CompilerParams(vmem_limit_bytes=VMEM_BYTES, dimension_semantics=("arbitrary",))


def body(
    tokens, cotangent, lengths, deal_order, norm_gain, in_weight, conv_weight, conv_bias,
    x_weight, dt_weight, dt_bias, decay_log, skip_gain, out_weight, *, n_dp, n_f
):
    seqs, own, model = tokens.shape
    slots = seqs // n_dp
    inner_rows, states = decay_log.shape
    rank = dt_weight.shape[1]
    proj_cols = x_weight.shape[1]
    width = inner_rows * n_dp
    length = own * n_dp * n_f
    d_rows = in_weight.shape[0]
    total_rows = length * slots
    group = lax.axis_index("dp")
    member = lax.axis_index("fsdp")

    low = lambda v: v.astype(BF16)
    slot_ids = jnp.arange(seqs, dtype=jnp.int32)
    seq_len = jnp.sum(jnp.where(deal_order[:, None] == slot_ids[None, :], lengths[:, None], 0), axis=0)
    own_pos = (group * n_f + member) * own + jnp.arange(own, dtype=jnp.int32)
    own_mask = own_pos[None, :] < seq_len[:, None]

    def spread(v):
        v = v.reshape(n_dp, slots, own, model).transpose(0, 2, 1, 3)
        v = lax.all_to_all(v, "dp", 0, 0, tiled=True)
        v = lax.all_gather(v, "fsdp", axis=0, tiled=False)
        return v.transpose(1, 0, 2, 3, 4).reshape(total_rows, model)

    def collect(v):
        v = v.reshape(n_dp, n_f, own, slots, model).transpose(1, 0, 2, 3, 4)
        v = lax.psum_scatter(v.reshape(total_rows, model), "fsdp", scatter_dimension=0, tiled=True)
        v = lax.all_to_all(v.reshape(n_dp, own, slots, model), "dp", 0, 0, tiled=True)
        return v.transpose(0, 2, 1, 3).reshape(seqs, own, model)

    x = spread(tokens)
    g_branch = spread(jnp.where(own_mask[:, :, None], cotangent, jnp.zeros_like(cotangent)))

    win = low(in_weight).reshape(d_rows, 2, n_dp, n_f, inner_rows).transpose(3, 0, 1, 2, 4)
    win = lax.all_to_all(win.reshape(n_f, d_rows, 2 * width), "fsdp", 0, 0, tiled=True)
    win = lax.all_gather(win.reshape(n_f * d_rows, 2 * width), "dp", axis=0, tiled=True)
    gain = lax.all_gather(low(norm_gain), BOTH, axis=0, tiled=True).astype(F32)[None, :]
    packed = jnp.concatenate(
        [
            low(v)
            for v in (
                out_weight, x_weight, dt_weight, decay_log, conv_weight,
                conv_bias[:, None], dt_bias[:, None], skip_gain[:, None],
            )
        ],
        axis=1,
    )
    packed = lax.all_gather(packed, "dp", axis=0, tiled=True)
    cuts = [model, proj_cols, rank, states, 4, 1, 1, 1]
    pieces, start = [], 0
    for cut in cuts:
        pieces.append(packed[:, start : start + cut])
        start += cut
    ow, xw, dtw, decay, cw, cb, dtb, skip = pieces
    rate = -jnp.exp(decay.astype(F32)).T
    cw, cb, dtb, skip = (v.astype(F32).T for v in (cw, cb, dtb, skip))

    rows = STEPS * slots
    blocks = length // STEPS
    grid = (blocks,)
    row_spec = lambda cols: pl.BlockSpec((rows, cols), lambda i: (i, 0))
    rev_spec = lambda cols: pl.BlockSpec((rows, cols), lambda i: (blocks - 1 - i, 0))
    like = jax.ShapeDtypeStruct

    inner, gate, inp, proj = pl.pallas_call(
        functools.partial(front_kernel, slots=slots),
        grid=grid,
        in_specs=[
            row_spec(model), whole((1, model)), whole((model, 2 * width)), whole((4, width)), whole((1, width)),
            whole((width, proj_cols)),
        ],
        out_specs=[row_spec(width), row_spec(width), row_spec(width), row_spec(proj_cols)],
        out_shape=[
            like((total_rows, width), F32), like((total_rows, width), F32), like((total_rows, width), BF16),
            like((total_rows, proj_cols), F32),
        ],
        scratch_shapes=[pltpu.VMEM((rows + 3 * slots, width), F32)],
        compiler_params=params(),
        name="front",
    )(x, gain, win, cw, cb, xw)

    proj = lax.psum(proj, "fsdp")
    dtl = low(proj[:, :rank])
    bc = proj[:, rank:]

    y, ck, branch = pl.pallas_call(
        functools.partial(mix_kernel, slots=slots),
        grid=grid,
        in_specs=[
            row_spec(rank), row_spec(2 * states), row_spec(width), row_spec(width), whole((width, rank)),
            whole((1, width)), whole((states, width)), whole((1, width)), whole((width, model)),
        ],
        out_specs=[
            row_spec(width), pl.BlockSpec((1, states, slots, width), lambda i: (i, 0, 0, 0)), row_spec(model),
        ],
        out_shape=[
            like((total_rows, width), F32), like((blocks, states, slots, width), F32), like((total_rows, model), BF16),
        ],
        scratch_shapes=[
            pltpu.VMEM((states, slots, width), F32), pltpu.VMEM((rows, width), F32), pltpu.VMEM((rows, width), F32),
            pltpu.VMEM((states, slots, width), F32),
        ],
        compiler_params=params(),
        name="mix",
    )(dtl, bc, inp, gate, dtw, dtb, rate, skip, ow)

    gis, ggate, gproj, gout, grank, gdec, gskip, gbias = pl.pallas_call(
        functools.partial(back_kernel, slots=slots),
        grid=grid,
        in_specs=[
            rev_spec(model), rev_spec(rank), rev_spec(2 * states), rev_spec(width), rev_spec(width), rev_spec(width),
            pl.BlockSpec((1, states, slots, width), lambda i: (blocks - 1 - i, 0, 0, 0)),
            whole((width, rank)), whole((1, width)), whole((states, width)), whole((1, width)), whole((width, model)),
        ],
        out_specs=[
            rev_spec(width), rev_spec(width), rev_spec(proj_cols), whole((width, model)), whole((width, rank)),
            whole((states, width)), whole((1, width)), whole((1, width)),
        ],
        out_shape=[
            like((total_rows, width), F32), like((total_rows, width), BF16), like((total_rows, proj_cols), F32),
            like((width, model), F32), like((width, rank), F32), like((states, width), F32), like((1, width), F32),
            like((1, width), F32),
        ],
        scratch_shapes=[
            pltpu.VMEM((states, slots, width), F32), pltpu.VMEM((states, slots, width), F32),
            pltpu.VMEM((slots, width), F32), pltpu.VMEM((slots, width), F32), pltpu.VMEM((states, slots, width), F32),
        ]
        + [pltpu.VMEM((rows, width), F32)] * 5
        + [
            pltpu.VMEM((STEPS, states, slots, 128), F32), pltpu.VMEM((STEPS, states, slots, 128), F32),
            pltpu.VMEM((STEPS, 2 * states, slots, 128), F32),
        ],
        compiler_params=params(),
        name="back",
    )(g_branch, dtl, bc, inp, gate, y, ck, dtw, dtb, rate, skip, ow)

    gproj = low(lax.psum(gproj, "fsdp"))

    gnorm, gin, gsel, gcw, gcb = pl.pallas_call(
        functools.partial(tail_kernel, slots=slots),
        grid=grid,
        in_specs=[
            rev_spec(proj_cols), rev_spec(width), rev_spec(width), rev_spec(width), rev_spec(width),
            pl.BlockSpec((4 * slots, width), lambda i: (jnp.maximum((blocks - 1 - i) * (STEPS // 4) - 1, 0), 0)),
            rev_spec(model), whole((1, model)), whole((model, 2 * width)), whole((width, proj_cols)), whole((4, width)),
            whole((1, width)),
        ],
        out_specs=[
            rev_spec(model), whole((model, 2 * width)), whole((width, proj_cols)), whole((4, width)), whole((1, width)),
        ],
        out_shape=[
            like((total_rows, model), BF16), like((model, 2 * width), F32), like((width, proj_cols), F32),
            like((4, width), F32), like((1, width), F32),
        ],
        scratch_shapes=[
            pltpu.VMEM((rows + 3 * slots, width), F32), pltpu.VMEM((rows + 3 * slots, width), F32),
            pltpu.VMEM((4, slots, width), F32), pltpu.VMEM((slots, width), F32),
        ],
        compiler_params=params(),
        name="tail",
    )(gproj, inp, gis, ggate, inner, inner, x, gain, win, xw, cw, cb)

    hidden = tokens.astype(F32)
    upstream = cotangent.astype(F32)
    output = (hidden + jnp.where(own_mask[:, :, None], collect(branch).astype(F32), 0.0)).astype(BF16)
    g_normed = collect(gnorm).astype(F32)
    factor = lax.rsqrt(jnp.mean(hidden * hidden, axis=-1, keepdims=True) + EPSILON)
    weighted = gain * g_normed
    input_grad = (
        upstream + factor * weighted - hidden * factor**3 * jnp.mean(hidden * weighted, axis=-1, keepdims=True)
    ).astype(BF16)
    gain_grad = lax.psum_scatter(
        jnp.sum(g_normed * hidden * factor, axis=(0, 1)), BOTH, scatter_dimension=0, tiled=True
    )

    gin = lax.psum_scatter(low(gin), "dp", scatter_dimension=0, tiled=True)
    gin = lax.all_to_all(gin.reshape(n_f, d_rows, 2 * width), "fsdp", 0, 0, tiled=True)
    gin = gin.reshape(n_f, d_rows, 2, n_dp, inner_rows).transpose(1, 2, 3, 0, 4).reshape(d_rows, -1).astype(F32)
    small = jnp.concatenate([gsel, grank, gdec.T, gcw.T, gcb.T, gbias.T, gskip.T], axis=1)
    small = lax.psum_scatter(jnp.concatenate([low(gout), low(small)], axis=1), "dp", scatter_dimension=0, tiled=True)
    small = small.astype(F32)
    cuts = [model, proj_cols, rank, states, 4, 1, 1, 1]
    pieces, start = [], 0
    for cut in cuts:
        pieces.append(small[:, start : start + cut])
        start += cut
    gout, gsel, grank, gdec, gcw, gcb, gbias, gskip = pieces
    return (
        output, input_grad, gain_grad, gin, gcw, gcb[:, 0], gsel, grank, gbias[:, 0], gdec, gskip[:, 0], gout,
    )


def solution(mesh):
    rows1, rows2, pos = P(BOTH), P(BOTH, None), P(None, BOTH, None)
    return jax.shard_map(
        functools.partial(body, n_dp=mesh.shape["dp"], n_f=mesh.shape["fsdp"]),
        mesh=mesh,
        in_specs=(pos, pos, P(), P(), rows1, rows2, rows2, rows1, rows2, rows2, rows1, rows2, rows1, rows2),
        out_specs=(pos, pos, rows1, rows2, rows2, rows1, rows2, rows2, rows1, rows2, rows1, rows2),
        check_vma=False,
    )
```

time: 2570 us -> 1290 us (0.50)
  waiting for transfers between devices: 1570 us -> 373 us
  Pallas kernels: 0 us -> 511 us
  other arithmetic: 314 us -> 27.7 us
  matrix products: 143 us -> 0 us
  local copies, waits for them, and re-layouts: 188 us -> 82.6 us
  blocking collectives: 308 us -> 267 us
    reduce_scatter x5 -> x4, waiting for transfers between devices: 1430 us -> 202 us  [the longest x2 139 us: collect(): lax.psum_scatter(v.reshape(total_rows, model), 'fsdp', scatter_dimension=...]
    pallas_call x0 -> x4, Pallas kernels: none -> 511 us  [the longest x1 379 us: body(): pl.pallas_call(functools.partial(back_kernel, slots=slots), grid=grid, in...]
    all_gather x5 -> x0, blocking collectives: 193 us -> none  [body(): lax.all_gather(for_sending(lowered), ('dp', 'fsdp'), axis=0, tiled=True)]
    reduce_sum x204 -> x3, other arithmetic: 168 us -> 0.97 us  [the longest x1 0.59 us: body(): jnp.sum(g_normed * hidden * factor, axis=(0, 1))]
    dot_general x12 -> x0, matrix products: 143 us -> none  [the longest x1 25.8 us: body(): jnp.einsum('td,tf->df', normed_low, grad_both, preferred_element_type=jnp...]
    all_to_all x0 -> x4, blocking collectives: none -> 119 us  [the longest x1 45.6 us: body(): lax.all_to_all(gin.reshape(n_f, d_rows, 2 * width), 'fsdp', 0, 0, tiled=T...]
    slice x51 -> x16, local copies, waits for them, and re-layouts: 81.5 us -> 15.9 us  [the longest x8 6.42 us: body(): pieces.append(packed[:, start:start + cut])]
    psum x0 -> x1, blocking collectives: none -> 62.9 us  [body(): gproj = low(lax.psum(gproj, 'fsdp'))]
  transfers between devices with their start and end apart: 14 -> 11, of which waited for: 10 -> 9; matrix products, arithmetic and copies ran while one was open for 7% -> 6% of each run, Pallas kernels for 0% -> 2%
where the time goes in v1:
time: 1290 us; the launch traced here: 1280 us
  Pallas kernels  511 us (40%)
  waiting for transfers between devices  373 us (29%)
  blocking collectives  267 us (21%)
  local copies, waits for them, and re-layouts  82.6 us (6%)
  other arithmetic  27.7 us (2%)
  between operations  14.2 us (1%)
    pallas_call x1, Pallas kernels, body(): pl.pallas_call(functools.partial(back_kernel, slots=slots), grid=grid, in...  379 us
    reduce_scatter x2, waiting for transfers between devices, collect(): lax.psum_scatter(v.reshape(total_rows, model), 'fsdp', scatter_dimension=...  139 us
    unnamed x2, blocking collectives  84.7 us
    pallas_call x1, Pallas kernels, body(): pl.pallas_call(functools.partial(mix_kernel, slots=slots), grid=grid, in_...  77.2 us
    psum x1, blocking collectives, body(): gproj = low(lax.psum(gproj, 'fsdp'))  62.9 us
    all_gather x2, waiting for transfers between devices, spread(): v = lax.all_gather(v, 'fsdp', axis=0, tiled=False)  60.4 us
    psum x1, waiting for transfers between devices, body(): proj = lax.psum(proj, 'fsdp')  57.4 us
    all_to_all x1, blocking collectives, body(): lax.all_to_all(gin.reshape(n_f, d_rows, 2 * width), 'fsdp', 0, 0, tiled=T...  45.6 us
  transfers between devices with their start and end apart: 11, of which 9 were waited for; matrix products, arithmetic and copies ran while one was open for 6% of the time, Pallas kernels for 2%

profile of v1, /device:TPU:0, one launch (start us, length us, event | category | flops | bytes accessed | tf_op | source)
XLA Modules:
  0.0 1284.2 jit_solution(4382800157537716703)
XLA Ops:
  13.4 3.9 concatenate.9
  17.3 25.3 %all_to_all.30 = bf16[4,8,8,2048]{3,1,2,0:T(8,128)(2,1)S(1)} all-to-all(bf16[4,8,8,2048]{3,1,2,0:T(8,128)(2,1)S(1)} %bitcast.91), channel_id=1, replica_groups=mesh['dp'=4,'fsdp'=8] {'dp'}, dimensions={0} | all-to-all | bytes 2097152 | tf_op jit(solution)/shard_map/all_to_all | solution.py:336
  45.9 31.9 %all_to_all.31 = bf16[8,64,1024]{2,1,0:T(8,128)(2,1)} all-to-all(bf16[8,64,1024]{2,1,0:T(8,128)(2,1)S(1)} %reshape.137), channel_id=1, replica_groups=mesh['dp'=4,'fsdp'=8] {'fsdp'}, dimensions={0} | all-to-all | bytes 2097152 | tf_op jit(solution)/shard_map/all_to_all | solution.py:350
  78.3 16.5 %all_to_all.32 = bf16[4,8,8,2048]{3,1,2,0:T(8,128)(2,1)S(1)} all-to-all(bf16[4,8,8,2048]{3,1,2,0:T(8,128)(2,1)S(1)} %bitcast.99), channel_id=1, replica_groups=mesh['dp'=4,'fsdp'=8] {'dp'}, dimensions={0} | all-to-all | bytes 2097152 | tf_op jit(solution)/shard_map/all_to_all | solution.py:336
  96.6 44.9 %all-reduce = bf16[2048]{0:T(1024)(128)(2,1)S(1)} all-reduce(bf16[2048]{0:T(1024)(128)(2,1)S(1)} %dynamic-update-slice), channel_id=1, replica_groups=mesh['dp'=4,'fsdp'=8] {'dp','fsdp'}, use_global_device_ids=true, to_apply=%add | all-reduce | flops 2048 | bytes 8192
  148.6 8.6 copy.116
  157.2 44.7 %all-gather.7.cloned.1.call-done.win_ref = bf16[2048,1024]{1,0:T(8,128)(2,1)} async-done(((bf16[512,1024]{1,0:T(8,128)(2,1)}), bf16[2048,1024]{1,0:T(8,128)(2,1)}) %all-gather.7.cloned.1.call-update) | async-done | bytes 4194320 | tf_op jit(solution)/shard_map/all_gather | solution.py:351
  201.8 19.5 %front.1 = (f32[2048,512]{1,0:T(8,128)}, f32[2048,512]{1,0:T(8,128)}, bf16[2048,512]{1,0:T(8,128)(2,1)}, f32[2048,160]{1,0:T(8,128)}) custom-call(bf16[2048,2048]{1,0:T(8,128)(2,1)} %bitcast.85, f32[1,2048]{1,0:T(1,128)} %bitcast.104, bf16[2048,1024]{1,0:T(8,128)(2,1)} %all-gather.7.cloned.1.call-done.win_ref, f32[4,512]{1,0:T(4,128)} %convert_bitcast_fusion.4.cw_ref, ...), custom_call_target="tpu_custom_call" | custom-call | tf_op jit(solution)/shard_map/front/pallas_call | solution.py:380
  222.9 2.5 copy.122.ow_ref
  227.5 58.4 %all-gather.13.cloned.1.call-done = bf16[32,8,8,2048]{3,2,1,0:T(8,128)(2,1)} async-done(((bf16[4,8,8,2048]{3,2,1,0:T(8,128)(2,1)}), bf16[32,8,8,2048]{3,2,1,0:T(8,128)(2,1)}) %all-gather.13.cloned.1.call-update) | async-done | bytes 8388624 | tf_op jit(solution)/shard_map/all_gather | solution.py:337
  285.9 8.3 copy.126
  294.2 57.4 %all-reduce.5.cloned.1.call-done = f32[2048,160]{1,0:T(8,128)} async-done(((f32[2048,160]{1,0:T(8,128)}), f32[2048,160]{1,0:T(8,128)}) %all-reduce.5.cloned.1.call-update) | async-done | bytes 1310736 | tf_op jit(solution)/shard_map/psum | solution.py:397
  356.0 77.2 %mix.1 = (f32[2048,512]{1,0:T(8,128)}, f32[8,16,8,512]{3,2,1,0:T(8,128)}, bf16[2048,2048]{1,0:T(8,128)(2,1)}) custom-call(bf16[2048,128]{1,0:T(8,128)(2,1)} %slice.106.dtl_ref, f32[2048,32]{1,0:T(8,128)} %slice.77.bc_ref, bf16[2048,512]{1,0:T(8,128)(2,1)} %get-tuple-element.33.inp_ref, f32[2048,512]{1,0:T(8,128)} %get-tuple-element.34.gate_ref, ...), custom_call_target="tpu_custom_call" | custom-call | tf_op jit(solution)/shard_map/mix/pallas_call | solution.py:401
  433.1 379.2 %back.1 = (f32[2048,512]{1,0:T(8,128)}, bf16[2048,512]{1,0:T(8,128)(2,1)}, f32[2048,160]{1,0:T(8,128)}, f32[512,2048]{1,0:T(8,128)}, f32[512,128]{1,0:T(8,128)},...) custom-call(bf16[2048,2048]{1,0:T(8,128)(2,1)} %bitcast.90, bf16[2048,128]{1,0:T(8,128)(2,1)} %slice.106.dtl_ref, ...), custom_call_target="tpu_custom_call" | custom-call | tf_op jit(solution)/shard_map/back/pallas_call | solution.py:422
  812.4 62.9 %all-reduce.6.gproj_ref = bf16[2048,160]{1,0:T(8,128)(2,1)} all-reduce(f32[2048,160]{1,0:T(8,128)} %get-tuple-element.38), channel_id=1, replica_groups=mesh['dp'=4,'fsdp'=8] {'fsdp'}, use_global_device_ids=true, to_apply=%region_4.5 | all-reduce | flops 327680 | bytes 1966080 | tf_op jit(solution)/shard_map/psum | solution.py:452
  875.2 35.0 %tail.1 = (bf16[2048,2048]{1,0:T(8,128)(2,1)}, f32[2048,1024]{1,0:T(8,128)}, f32[512,160]{1,0:T(8,128)}, f32[4,512]{1,0:T(4,128)}, f32[1,512]{1,0:T(1,128)}) custom-call(bf16[2048,160]{1,0:T(8,128)(2,1)} %all-reduce.6.gproj_ref, bf16[2048,512]{1,0:T(8,128)(2,1)} %get-tuple-element.33.inp_ref, f32[2048,512]{1,0:T(8,128)} %get-tuple-element.39.gis_ref, ...), custom_call_target="tpu_custom_call" | custom-call | tf_op jit(solution)/shard_map/tail/pallas_call | solution.py:454
  910.2 6.1 convert_element_type.131
  916.4 8.5 copy.130
  927.6 2.8 convert_element_type.136
  933.8 4.8 concatenate.10
  938.7 8.4 copy.123
  947.1 21.5 %reduce-scatter.9.cloned.1.call-done = bf16[512,1024]{1,0:T(8,128)(2,1)} async-done(((bf16[2048,1024]{1,0:T(8,128)(2,1)}), bf16[512,1024]{1,0:T(8,128)(2,1)}) %reduce-scatter.9.cloned.1.call-update) | async-done | bytes 1048592 | tf_op jit(solution)/shard_map/reduce_scatter | solution.py:491
  968.5 45.6 %all_to_all.33 = bf16[8,64,1024]{2,1,0:T(8,128)(2,1)} all-to-all(bf16[8,64,1024]{2,1,0:T(8,128)(2,1)} %bitcast.103), channel_id=1, replica_groups=mesh['dp'=4,'fsdp'=8] {'fsdp'}, dimensions={0} | all-to-all | bytes 2097152 | tf_op jit(solution)/shard_map/all_to_all | solution.py:492
  1014.2 60.9 %reduce-scatter.7.cloned.1.call-done = bf16[256,2048]{1,0:T(8,128)(2,1)} async-done(((bf16[2048,2048]{1,0:T(8,128)(2,1)}), bf16[256,2048]{1,0:T(8,128)(2,1)}) %reduce-scatter.7.cloned.1.call-update) | async-done | bytes 1048592 | tf_op jit(solution)/shard_map/reduce_scatter | solution.py:342
  1075.0 4.2 all-to-all-start.4
  1079.6 41.5 %reduce-scatter.11.cloned.1.call-done = bf16[128,2359]{1,0:T(8,128)(2,1)} async-done(((bf16[512,2359]{1,0:T(8,128)(2,1)}), bf16[128,2359]{1,0:T(8,128)(2,1)}) %reduce-scatter.11.cloned.1.call-update) | async-done | bytes 603920 | tf_op jit(solution)/shard_map/reduce_scatter | solution.py:495
  1135.2 77.9 %reduce-scatter.5.cloned.1.call-done = bf16[256,2048]{1,0:T(8,128)(2,1)} async-done(((bf16[2048,2048]{1,0:T(8,128)(2,1)}), bf16[256,2048]{1,0:T(8,128)(2,1)}) %reduce-scatter.5.cloned.1.call-update) | async-done | bytes 1048592 | tf_op jit(solution)/shard_map/reduce_scatter | solution.py:342
  1213.1 4.2 all-to-all-start.2
  1220.6 8.5 all-to-all-done.2
  1230.6 2.6 copy.124
  1233.2 39.8 %all-reduce.1 = f32[2048]{0:T(1024)S(1)} all-reduce(f32[2048]{0:T(1024)S(1)} %get-tuple-element.115), channel_id=6, replica_groups=mesh['dp'=4,'fsdp'=8] {'dp','fsdp'}, use_global_device_ids=true, to_apply=%region_8.9.clone | all-reduce | flops 2048 | bytes 16384
  1273.6 4.1 fusion.4
  (115 shorter events, 52.8 us)
Async XLA Ops:
  7.2 10.1 copy-start
  7.2 134.9 %all-gather.9.cloned.1.call-start = ((), (), s32[]{:S(2)}) async-start(), calls=%async_computation.11 | async-start | bytes 3020800 | tf_op jit(solution)/shard_map/all_gather | solution.py:363
  17.3 131.3 %all-gather.11.cloned.1.call-start = ((), (), s32[]{:S(2)}) async-start(), calls=%async_computation.17 | async-start | bytes 9437184 | tf_op jit(solution)/shard_map/all_gather | solution.py:337
  42.6 1.7 copy-start.3
  44.2 157.6 %all-gather.7.cloned.1.call-start = ((), (), s32[]{:S(2)}) async-start(), calls=%async_computation.10 | async-start | bytes 5242880 | tf_op jit(solution)/shard_map/all_gather | solution.py:351
  45.9 32.0 %copy-start.11 = (s32[32]{0:T(128)S(1)}, s32[32]{0:T(128)}, u32[]{:S(2)}) copy-start(s32[32]{0:T(128)} %param.16) | copy-start | bytes 388
  45.9 32.0 %copy-start.12 = (s32[32]{0:T(128)S(1)}, s32[32]{0:T(128)}, u32[]{:S(2)}) copy-start(s32[32]{0:T(128)} %param.17) | copy-start | bytes 388
  45.9 32.2 %copy-start.2 = (bf16[32,8,2048]{2,1,0:T(8,128)(2,1)S(1)}, bf16[32,8,2048]{2,1,0:T(8,128)(2,1)}, u32[]{:S(2)}) copy-start(bf16[32,8,2048]{2,1,0:T(8,128)(2,1)} %param.15) | copy-start | bytes 3145732
  77.8 208.1 %all-gather.13.cloned.1.call-start = ((), (), s32[]{:S(2)}) async-start(), calls=%async_computation.18 | async-start | bytes 9437184 | tf_op jit(solution)/shard_map/all_gather | solution.py:337
  94.7 1.6 copy-start.13
  96.3 255.3 %all-reduce.5.cloned.1.call-start = ((), (), s32[]{:S(2)}) async-start(), calls=%async_computation.12 | async-start | bytes 4194304 | tf_op jit(solution)/shard_map/psum | solution.py:397
  221.3 1.6 slice-start
  221.3 747.2 %reduce-scatter.9.cloned.1.call-start = ((), (), s32[]{:S(2)}) async-start(), calls=%async_computation.15 | async-start | bytes 5242880 | tf_op jit(solution)/shard_map/reduce_scatter | solution.py:491
  222.9 2.5 slice-start.1
  916.4 158.6 %reduce-scatter.7.cloned.1.call-start = ((), (), s32[]{:S(2)}) async-start(), calls=%async_computation.14 | async-start | bytes 9437184 | tf_op jit(solution)/shard_map/reduce_scatter | solution.py:342
  924.9 1.0 copy-start.4
  924.9 1.1 copy-start.7
  924.9 1.9 copy-start.10
  924.9 196.1 %reduce-scatter.11.cloned.1.call-start = ((), (), s32[]{:S(2)}) async-start(), calls=%async_computation.16 | async-start | bytes 3112960 | tf_op jit(solution)/shard_map/reduce_scatter | solution.py:495
  927.6 2.8 copy-start.6
  927.6 3.6 copy-start.9
  927.6 4.4 copy-start.8
  938.6 274.4 %reduce-scatter.5.cloned.1.call-start = ((), (), s32[]{:S(2)}) async-start(), calls=%async_computation.13 | async-start | bytes 9437184 | tf_op jit(solution)/shard_map/reduce_scatter | solution.py:342
  1075.0 138.0 %all-to-all-start.4 = ((bf16[4,8,8,2048]{3,2,1,0:T(8,128)(2,1)}), bf16[4,8,8,2048]{3,2,1,0:T(8,128)(2,1)}, u32[]{:S(2)}, u32[]{:S(2)}) async-start(bf16[4,8,8,2048]{3,2,1,0:T(8,128)(2,1)} %bitcast.101), calls=%async_computation.6 | async-start | bytes 2097152 | tf_op jit(solution)/shard_map/all_to_all | solution.py:343
  1121.0 5.8 copy-start.1
  1213.1 16.1 %all-to-all-start.2 = ((bf16[4,8,8,2048]{3,2,1,0:T(8,128)(2,1)}), bf16[4,8,8,2048]{3,2,1,0:T(8,128)(2,1)}, u32[]{:S(2)}, u32[]{:S(2)}) async-start(bf16[4,8,8,2048]{3,2,1,0:T(8,128)(2,1)} %bitcast.102), calls=%async_computation.3 | async-start | bytes 2097152 | tf_op jit(solution)/shard_map/all_to_all | solution.py:343
  1218.8 1.2 copy-start.5
Sparse Core Ops, SparseCore 0:
  17.4 45.9 all-gather.8
  65.6 82.9 all-gather.10
  150.4 51.3 all-gather.6
  203.8 82.0 all-gather.12
  288.1 63.4 all-reduce.4
  916.5 51.9 reduce-scatter.8
  970.9 104.0 reduce-scatter.6
  1078.4 42.5 reduce-scatter.10
  1123.4 89.5 reduce-scatter.4

commit v2 on v1

--- a/solution.py
+++ b/solution.py
@@ -8,6 +8,8 @@
 
 EPSILON = 1e-05
 STEPS = 32
+PAIR = 2
+TOGETHER = 8
 LOG2E = 1.4426950408889634
 BOTH = ("dp", "fsdp")
 F32 = jnp.float32
@@ -58,14 +60,39 @@
     pad_ref[0:halo, :] = pad_ref[rows : rows + halo, :]
 
 
+def spread_lanes(bc_ref, bcb_scr, slots):
+    steps, count = bcb_scr.shape[0], bcb_scr.shape[1]
+    together = TOGETHER
+
+    def some(k, carry):
+        for n in range(count):
+            for j in range(together):
+                t = k * together + j
+                at = pl.ds(pl.multiple_of(t * slots, slots), slots)
+                bcb_scr[t, n] = jnp.broadcast_to(bc_ref[at, n : n + 1], (slots, 128))
+        return carry
+
+    lax.fori_loop(0, steps // together, some, 0)
+
+
+def widen(piece, width):
+    return jnp.concatenate([piece] * (width // 128), axis=1)
+
+
+def narrow(value):
+    total = value[:, :128]
+    for first in range(128, value.shape[1], 128):
+        total = total + value[:, first : first + 128]
+    return total
+
+
 def mix_kernel(
     dtl_ref, bc_ref, inp_ref, gate_ref, dtw_ref, dtb_ref, rate_ref, skip_ref, ow_ref,
-    y_ref, ck_ref, br_ref, h_scr, delta_scr, u_scr, rate_scr, *, slots
+    y_ref, ck_ref, br_ref, h_scr, delta_scr, u_scr, rate_scr, bcb_scr, *, slots
 ):
     rows, width = inp_ref.shape
     steps = rows // slots
     states = rate_ref.shape[0]
-    chunk = max(128, 2048 // slots)
 
     @pl.when(pl.program_id(0) == 0)
     def _():
@@ -77,31 +104,35 @@
     delta = softplus(dot(dtl_ref[...], dtw_ref[...], ((1,), (1,))) + dtb_ref[...])
     delta_scr[...] = delta
     u_scr[...] = delta * inp_ref[...].astype(F32)
-    for first in range(0, width, chunk):
-        lanes = slice(first, first + chunk)
-
-        def step(t, held):
-            at = pl.ds(pl.multiple_of(t * slots, slots), slots)
-            d = delta_scr[at, lanes]
-            u = u_scr[at, lanes]
-            bc = bc_ref[at, :]
-            y = jnp.zeros_like(d)
-            after = []
-            for n in range(states):
-                h = jnp.exp2(d * rate_scr[n, :, lanes]) * held[n] + u * bc[:, n : n + 1]
-                y = y + h * bc[:, states + n : states + n + 1]
-                after.append(h)
-            y_ref[at, lanes] = y
-            return tuple(after)
-
-        held = lax.fori_loop(0, steps, step, tuple(h_scr[n, :, lanes] for n in range(states)))
+    spread_lanes(bc_ref, bcb_scr, slots)
+
+    def step(k, carry):
+        ats, ds, us, ys = [], [], [], []
+        for j in range(PAIR):
+            at = pl.ds(pl.multiple_of((k * PAIR + j) * slots, slots), slots)
+            ats.append(at)
+            ds.append(delta_scr[at, :])
+            us.append(u_scr[at, :])
+            ys.append(None)
         for n in range(states):
-            h_scr[n, :, lanes] = held[n]
+            rate = rate_scr[n]
+            h = h_scr[n]
+            for j in range(PAIR):
+                t = k * PAIR + j
+                h = jnp.exp2(ds[j] * rate) * h + us[j] * widen(bcb_scr[t, n], width)
+                term = h * widen(bcb_scr[t, states + n], width)
+                ys[j] = term if n == 0 else ys[j] + term
+            h_scr[n] = h
+        for j in range(PAIR):
+            y_ref[ats[j], :] = ys[j]
+        return carry
+
+    lax.fori_loop(0, steps // PAIR, step, 0)
     y = y_ref[...] + skip_ref[...] * inp_ref[...].astype(F32)
     y_ref[...] = y
     gate = gate_ref[...]
     gated = (y * (gate * sigmoid(gate))).astype(BF16)
-    br_ref[...] = dot(gated, ow_ref[...]).astype(br_ref.dtype)
+    br_ref[...] = dot(gated, ow_ref[...]).astype(br_ref.dtype).reshape(br_ref.shape)
 
 
 def lane_sums(parts):
@@ -126,13 +157,12 @@
 def back_kernel(
     gb_ref, dtl_ref, bc_ref, inp_ref, gate_ref, y_ref, ck_ref, dtw_ref, dtb_ref, rate_ref, skip_ref, ow_ref,
     gis_ref, ggate_ref, gproj_ref, gout_ref, grank_ref, gdec_ref, gskip_ref, gbias_ref,
-    lam_scr, dacc_scr, sacc_scr, bacc_scr, rate_scr, delta_scr, u_scr, gy_scr, gu_scr, gd_scr, h_scr, a_scr, gbc_scr, *, slots
+    lam_scr, dacc_scr, sacc_scr, bacc_scr, rate_scr, delta_scr, u_scr, gy_scr, gu_scr, gd_scr, h_scr, a_scr, gbc_scr, bcb_scr, h_now, *, slots
 ):
     rows, width = inp_ref.shape
     steps = rows // slots
     states = rate_ref.shape[0]
     rank = dtl_ref.shape[1]
-    chunk = 128
     step_id = pl.program_id(0)
 
     @pl.when(step_id == 0)
@@ -163,77 +193,76 @@
     delta_scr[...] = delta
     u_scr[...] = delta * inp
 
-    for first in range(0, width, chunk):
-        lanes = slice(first, first + chunk)
-
-        def replay(t, held):
+    spread_lanes(bc_ref, bcb_scr, slots)
+    h_now[...] = ck_ref[0]
+
+    def replay(k, carry):
+        ds, us, gys = [], [], []
+        for j in range(PAIR):
+            at = pl.ds(pl.multiple_of((k * PAIR + j) * slots, slots), slots)
+            ds.append(delta_scr[at, :])
+            us.append(u_scr[at, :])
+            gys.append(gy_scr[at, :])
+        for n in range(states):
+            rate = rate_scr[n]
+            h = h_now[n]
+            for j in range(PAIR):
+                t = k * PAIR + j
+                h_scr[t, n] = h
+                decay = jnp.exp2(ds[j] * rate)
+                a_scr[t, n] = decay
+                h = decay * h + us[j] * widen(bcb_scr[t, n], width)
+                gbc_scr[t, states + n] = narrow(h * gys[j])
+            h_now[n] = h
+        return carry
+
+    lax.fori_loop(0, steps // PAIR, replay, 0)
+
+    def reverse(k, carry):
+        ats, ds, us, gys, gus, gds, ts = [], [], [], [], [], [], []
+        for j in range(PAIR):
+            t = steps - 1 - (k * PAIR + j)
             at = pl.ds(pl.multiple_of(t * slots, slots), slots)
-            d = delta_scr[at, lanes]
-            u = u_scr[at, lanes]
-            gy = gy_scr[at, lanes]
-            bc = bc_ref[at, :]
-            after = []
-            for n in range(states):
-                h_scr[t, n] = held[n]
-                a = jnp.exp2(d * rate_scr[n, :, lanes])
-                a_scr[t, n] = a
-                h = a * held[n] + u * bc[:, n : n + 1]
-                part = h * gy
-                if first:
-                    part = part + gbc_scr[t, states + n]
-                gbc_scr[t, states + n] = part
-                after.append(h)
-            return tuple(after)
-
-        lax.fori_loop(0, steps, replay, tuple(ck_ref[0, n, :, lanes] for n in range(states)))
-
-        def reverse(k, held):
-            lams, sums = held
-            t = steps - 1 - k
-            at = pl.ds(pl.multiple_of(t * slots, slots), slots)
-            d = delta_scr[at, lanes]
-            u = u_scr[at, lanes]
-            gy = gy_scr[at, lanes]
-            bc = bc_ref[at, :]
-            gu = jnp.zeros_like(d)
-            gd = jnp.zeros_like(d)
-            lams_after, sums_after = [], []
-            for n in range(states):
-                lam = lams[n] + gy * bc[:, states + n : states + n + 1]
-                gu = gu + lam * bc[:, n : n + 1]
-                part = lam * u
-                if first:
-                    part = part + gbc_scr[t, n]
-                gbc_scr[t, n] = part
+            ts.append(t)
+            ats.append(at)
+            ds.append(delta_scr[at, :])
+            us.append(u_scr[at, :])
+            gys.append(gy_scr[at, :])
+            gus.append(None)
+            gds.append(None)
+        for n in range(states):
+            rate = rate_scr[n]
+            carried = lam_scr[n]
+            total = dacc_scr[n]
+            for j in range(PAIR):
+                t = ts[j]
+                lam = carried + gys[j] * widen(bcb_scr[t, states + n], width)
+                term = lam * widen(bcb_scr[t, n], width)
+                gus[j] = term if n == 0 else gus[j] + term
+                gbc_scr[t, n] = narrow(lam * us[j])
                 carried = a_scr[t, n] * lam
                 q = carried * h_scr[t, n]
-                gd = gd + q * rate_scr[n, :, lanes]
-                sums_after.append(sums[n] + q * d)
-                lams_after.append(carried)
-            gu_scr[at, lanes] = gu
-            gd_scr[at, lanes] = gd
-            return tuple(lams_after), tuple(sums_after)
-
-        lams, sums = lax.fori_loop(
-            0,
-            steps,
-            reverse,
-            (
-                tuple(lam_scr[n, :, lanes] for n in range(states)),
-                tuple(dacc_scr[n, :, lanes] for n in range(states)),
-            ),
-        )
-        for n in range(states):
-            lam_scr[n, :, lanes] = lams[n]
-            dacc_scr[n, :, lanes] = sums[n]
-
-    def reduce_lanes(t, carry):
-        at = pl.ds(pl.multiple_of(t * slots, slots), slots)
-        total = lane_sums([gbc_scr[t, k] for k in range(2 * states)])
-        gproj_ref[at, rank:] = total[:, : 2 * states]
+                term = q * rate
+                gds[j] = term if n == 0 else gds[j] + term
+                total = total + q * ds[j]
+            lam_scr[n] = carried
+            dacc_scr[n] = total
+        for j in range(PAIR):
+            gu_scr[ats[j], :] = gus[j]
+            gd_scr[ats[j], :] = gds[j]
         return carry
 
-    lax.fori_loop(0, steps, reduce_lanes, 0)
+    lax.fori_loop(0, steps // PAIR, reverse, 0)
+
+    def reduce_lanes(k, carry):
+        for j in range(TOGETHER):
+            t = k * TOGETHER + j
+            at = pl.ds(pl.multiple_of(t * slots, slots), slots)
+            total = lane_sums([gbc_scr[t, n] for n in range(2 * states)])
+            gproj_ref[at, rank:] = total[:, : 2 * states]
+        return carry
+
+    lax.fori_loop(0, steps // TOGETHER, reduce_lanes, 0)
     gu = gu_scr[...]
     gis_ref[...] = gu * delta_scr[...] + skip_ref[...] * gy_scr[...]
     g_pre = (gd_scr[...] * (1.0 / LOG2E) + gu * inp) * sigmoid(z)
@@ -292,13 +321,211 @@
     g_both = jnp.concatenate([g_inner.astype(BF16), ggate_ref[...]], axis=1)
     normed = rms_normed(x_ref[...].astype(F32), gain_ref[...])
     gin_ref[...] += dot(normed, g_both, ((0,), (0,)))
-    gnorm_ref[...] = dot(g_both, win_ref[...], ((1,), (1,))).astype(gnorm_ref.dtype)
+    gnorm_ref[...] = dot(g_both, win_ref[...], ((1,), (1,))).astype(gnorm_ref.dtype).reshape(gnorm_ref.shape)
 
     @pl.when(step_id == last)
     def _():
         for tap in range(4):
             gcw_ref[tap : tap + 1, :] = jnp.sum(wacc_scr[tap], axis=0, keepdims=True)
         gcb_ref[...] = jnp.sum(cacc_scr[...], axis=0, keepdims=True)
+
+
+def remote(src, dst, send, recv, where):
+    return pltpu.make_async_remote_copy(
+        src_ref=src, dst_ref=dst, send_sem=send, recv_sem=recv, device_id=where, device_id_type=pl.DeviceIdType.MESH
+    )
+
+
+def gather_kernel(
+    tok_ref, win_ref, gain_ref, pk_ref, x_ref, w_ref, g_ref, p_ref,
+    tok_buf, win_buf, gain_buf, pk_buf, local_sem,
+    tdp_send, tdp_recv, up_send, up_recv, down_send, down_recv, core_send, core_recv,
+    w1_send, w1_recv, w2_send, w2_recv, g1_send, g1_recv, g2_send, g2_recv, p_send, p_recv, *, n_dp, n_f
+):
+    d = lax.axis_index("dp")
+    f = lax.axis_index("fsdp")
+    n_z = n_f // 2
+    z = f // 2
+    core = f % 2
+    partner = z * 2 + (1 - core)
+
+    barrier = pltpu.get_barrier_semaphore()
+    for k in range(1, n_f):
+        pl.semaphore_signal(barrier, inc=1, device_id=(d, (f + k) % n_f), device_id_type=pl.DeviceIdType.MESH)
+    for k in range(1, n_dp):
+        pl.semaphore_signal(barrier, inc=1, device_id=((d + k) % n_dp, f), device_id_type=pl.DeviceIdType.MESH)
+    pl.semaphore_wait(barrier, n_f + n_dp - 2)
+
+    loads = (
+        pltpu.make_async_copy(tok_ref.at[d], tok_buf, local_sem.at[0]),
+        pltpu.make_async_copy(win_ref.at[f], win_buf, local_sem.at[1]),
+        pltpu.make_async_copy(gain_ref, gain_buf, local_sem.at[2]),
+        pltpu.make_async_copy(pk_ref, pk_buf, local_sem.at[3]),
+    )
+    stores = (
+        pltpu.make_async_copy(tok_buf, x_ref.at[d, f], local_sem.at[4]),
+        pltpu.make_async_copy(win_buf, w_ref.at[d, f], local_sem.at[5]),
+        pltpu.make_async_copy(gain_buf, g_ref.at[d, f], local_sem.at[6]),
+        pltpu.make_async_copy(pk_buf, p_ref.at[d], local_sem.at[7]),
+    )
+    for load in loads:
+        load.start()
+
+    def tok_dp(k):
+        to = (d + k) % n_dp
+        return remote(tok_ref.at[to], x_ref.at[d, f], tdp_send.at[k], tdp_recv.at[k], (to, f))
+
+    def tok_dp_arrival(k):
+        src = (d - k + n_dp) % n_dp
+        return remote(tok_ref.at[d], x_ref.at[src, f], tdp_send.at[k], tdp_recv.at[k], (src, f))
+
+    def w1(k):
+        to = (f + k) % n_f
+        return remote(win_ref.at[to], w_ref.at[d, f], w1_send.at[k], w1_recv.at[k], (d, to))
+
+    def w1_arrival(k):
+        src = (f - k + n_f) % n_f
+        return remote(win_ref.at[f], w_ref.at[d, src], w1_send.at[k], w1_recv.at[k], (d, src))
+
+    def g1(k):
+        to = (f + k) % n_f
+        return remote(gain_ref, g_ref.at[d, f], g1_send.at[k], g1_recv.at[k], (d, to))
+
+    def g1_arrival(k):
+        src = (f - k + n_f) % n_f
+        return remote(gain_ref, g_ref.at[d, src], g1_send.at[k], g1_recv.at[k], (d, src))
+
+    def w2(k):
+        to = (d + k) % n_dp
+        return remote(w_ref.at[d], w_ref.at[d], w2_send.at[k], w2_recv.at[k], (to, f))
+
+    def w2_arrival(k):
+        src = (d - k + n_dp) % n_dp
+        return remote(w_ref.at[src], w_ref.at[src], w2_send.at[k], w2_recv.at[k], (src, f))
+
+    def g2(k):
+        to = (d + k) % n_dp
+        return remote(g_ref.at[d], g_ref.at[d], g2_send.at[k], g2_recv.at[k], (to, f))
+
+    def g2_arrival(k):
+        src = (d - k + n_dp) % n_dp
+        return remote(g_ref.at[src], g_ref.at[src], g2_send.at[k], g2_recv.at[k], (src, f))
+
+    def pk(k):
+        to = (d + k) % n_dp
+        return remote(pk_ref, p_ref.at[d], p_send.at[k], p_recv.at[k], (to, f))
+
+    def pk_arrival(k):
+        src = (d - k + n_dp) % n_dp
+        return remote(pk_ref, p_ref.at[src], p_send.at[k], p_recv.at[k], (src, f))
+
+    def block(j, origin, side):
+        at = (d - j + n_dp) % n_dp
+        return x_ref.at[at, origin * 2 + side]
+
+    def up(j, origin, src=None):
+        ref = block(j, origin, core)
+        return remote(ref if src is None else src, ref, up_send.at[origin, j], up_recv.at[origin, j], (d, f + 2))
+
+    def down(j, origin, src=None):
+        ref = block(j, origin, core)
+        return remote(ref if src is None else src, ref, down_send.at[origin, j], down_recv.at[origin, j], (d, f - 2))
+
+    def across(j, origin, src=None):
+        ref = block(j, origin, core)
+        return remote(
+            ref if src is None else src, ref, core_send.at[origin, j], core_recv.at[origin, j], (d, partner)
+        )
+
+    def across_arrival(j, origin):
+        ref = block(j, origin, 1 - core)
+        return remote(ref, ref, core_send.at[origin, j], core_recv.at[origin, j], (d, partner))
+
+    def launch(j, src=None):
+        @pl.when(z < n_z - 1)
+        def _():
+            up(j, z, src).start()
+
+        @pl.when(z > 0)
+        def _():
+            down(j, z, src).start()
+
+        across(j, z, src).start()
+
+    for k in range(1, n_f):
+        w1(k).start()
+    for k in range(1, n_dp):
+        tok_dp(k).start()
+    launch(0, tok_ref.at[d])
+    for k in range(1, n_f):
+        g1(k).start()
+    for k in range(1, n_dp):
+        pk(k).start()
+    for load, store in zip(loads, stores):
+        load.wait()
+        store.start()
+    for k in range(1, n_dp):
+        tok_dp_arrival(k).wait_recv()
+        launch(k)
+    for store in stores:
+        store.wait()
+    for k in range(1, n_f):
+        w1_arrival(k).wait_recv()
+        g1_arrival(k).wait_recv()
+    for k in range(1, n_dp):
+        w2(k).start()
+        g2(k).start()
+    for far in range(1, n_z):
+        for j in range(n_dp):
+
+            @pl.when(z >= far)
+            def _():
+                origin = z - far
+                up(j, origin).wait_recv()
+
+                @pl.when(z < n_z - 1)
+                def _():
+                    up(j, origin).start()
+
+                across(j, origin).start()
+
+            @pl.when(z + far < n_z)
+            def _():
+                origin = z + far
+                down(j, origin).wait_recv()
+
+                @pl.when(z > 0)
+                def _():
+                    down(j, origin).start()
+
+                across(j, origin).start()
+
+    for origin in range(n_z):
+        for j in range(n_dp):
+            across_arrival(j, origin).wait_recv()
+            across(j, origin).wait_send()
+    for origin in range(n_z):
+        for j in range(n_dp):
+
+            @pl.when((origin <= z) & (z < n_z - 1))
+            def _():
+                up(j, origin).wait_send()
+
+            @pl.when((origin >= z) & (z > 0))
+            def _():
+                down(j, origin).wait_send()
+
+    for k in range(1, n_dp):
+        pk_arrival(k).wait_recv()
+        w2_arrival(k).wait_recv()
+        g2_arrival(k).wait_recv()
+        tok_dp(k).wait_send()
+        w2(k).wait_send()
+        g2(k).wait_send()
+        pk(k).wait_send()
+    for k in range(1, n_f):
+        w1(k).wait_send()
+        g1(k).wait_send()
 
 
 def whole(shape):
@@ -338,18 +565,16 @@
         return v.transpose(1, 0, 2, 3, 4).reshape(total_rows, model)
 
     def collect(v):
-        v = v.reshape(n_dp, n_f, own, slots, model).transpose(1, 0, 2, 3, 4)
         v = lax.psum_scatter(v.reshape(total_rows, model), "fsdp", scatter_dimension=0, tiled=True)
         v = lax.all_to_all(v.reshape(n_dp, own, slots, model), "dp", 0, 0, tiled=True)
         return v.transpose(0, 2, 1, 3).reshape(seqs, own, model)
 
-    x = spread(tokens)
     g_branch = spread(jnp.where(own_mask[:, :, None], cotangent, jnp.zeros_like(cotangent)))
 
+    tok = tokens.reshape(n_dp, slots, own, model).transpose(0, 2, 1, 3).reshape(n_dp, own * slots, model)
     win = low(in_weight).reshape(d_rows, 2, n_dp, n_f, inner_rows).transpose(3, 0, 1, 2, 4)
-    win = lax.all_to_all(win.reshape(n_f, d_rows, 2 * width), "fsdp", 0, 0, tiled=True)
-    win = lax.all_gather(win.reshape(n_f * d_rows, 2 * width), "dp", axis=0, tiled=True)
-    gain = lax.all_gather(low(norm_gain), BOTH, axis=0, tiled=True).astype(F32)[None, :]
+    win = win.reshape(n_f, d_rows, 2 * width)
+    gain_tile = jnp.zeros((8, 128), F32).at[0, :d_rows].set(low(norm_gain).astype(F32))
     packed = jnp.concatenate(
         [
             low(v)
@@ -360,7 +585,34 @@
         ],
         axis=1,
     )
-    packed = lax.all_gather(packed, "dp", axis=0, tiled=True)
+    packed = jnp.pad(packed, ((0, 0), (0, -packed.shape[1] % 128)))
+    n_z = n_f // 2
+    dma = pltpu.SemaphoreType.DMA
+    hbm = pl.BlockSpec(memory_space=pl.ANY)
+    x, win, gain, packed = pl.pallas_call(
+        functools.partial(gather_kernel, n_dp=n_dp, n_f=n_f),
+        in_specs=[hbm] * 4,
+        out_specs=[hbm] * 4,
+        out_shape=[
+            jax.ShapeDtypeStruct((n_dp, n_f) + tok.shape[1:], BF16),
+            jax.ShapeDtypeStruct((n_dp, n_f) + win.shape[1:], BF16),
+            jax.ShapeDtypeStruct((n_dp, n_f, 8, 128), F32),
+            jax.ShapeDtypeStruct((n_dp,) + packed.shape, BF16),
+        ],
+        scratch_shapes=[
+            pltpu.VMEM(tok.shape[1:], BF16), pltpu.VMEM(win.shape[1:], BF16), pltpu.VMEM((8, 128), F32),
+            pltpu.VMEM(packed.shape, BF16), dma((8,)), dma((n_dp,)), dma((n_dp,)),
+        ]
+        + [dma((n_z, n_dp))] * 6
+        + [dma((n_f,)), dma((n_f,)), dma((n_dp,)), dma((n_dp,)), dma((n_f,)), dma((n_f,))]
+        + [dma((n_dp,))] * 4,
+        compiler_params=pltpu.CompilerParams(collective_id=1, has_side_effects=True),
+        name="gather",
+    )(tok, win, gain_tile, packed)
+    x = x.reshape(total_rows, model)
+    win = win.reshape(model, 2 * width)
+    gain = gain[:, :, 0, :d_rows].reshape(1, model)
+    packed = packed.reshape(width, -1)
     cuts = [model, proj_cols, rank, states, 4, 1, 1, 1]
     pieces, start = [], 0
     for cut in cuts:
@@ -376,6 +628,12 @@
     row_spec = lambda cols: pl.BlockSpec((rows, cols), lambda i: (i, 0))
     rev_spec = lambda cols: pl.BlockSpec((rows, cols), lambda i: (blocks - 1 - i, 0))
     like = jax.ShapeDtypeStruct
+    held = STEPS // own
+    per = n_f // held
+    piece = (held, 1, own * slots, model)
+    piece_spec = pl.BlockSpec(piece, lambda i: (i % per, i // per, 0, 0))
+    rev_piece_spec = pl.BlockSpec(piece, lambda i: ((blocks - 1 - i) % per, (blocks - 1 - i) // per, 0, 0))
+    pieces_shape = like((n_f, n_dp, own * slots, model), BF16)
 
     inner, gate, inp, proj = pl.pallas_call(
         functools.partial(front_kernel, slots=slots),
@@ -406,14 +664,14 @@
             whole((1, width)), whole((states, width)), whole((1, width)), whole((width, model)),
         ],
         out_specs=[
-            row_spec(width), pl.BlockSpec((1, states, slots, width), lambda i: (i, 0, 0, 0)), row_spec(model),
+            row_spec(width), pl.BlockSpec((1, states, slots, width), lambda i: (i, 0, 0, 0)), piece_spec,
         ],
         out_shape=[
-            like((total_rows, width), F32), like((blocks, states, slots, width), F32), like((total_rows, model), BF16),
+            like((total_rows, width), F32), like((blocks, states, slots, width), F32), pieces_shape,
         ],
         scratch_shapes=[
             pltpu.VMEM((states, slots, width), F32), pltpu.VMEM((rows, width), F32), pltpu.VMEM((rows, width), F32),
-            pltpu.VMEM((states, slots, width), F32),
+            pltpu.VMEM((states, slots, width), F32), pltpu.VMEM((STEPS, 2 * states, slots, 128), F32),
         ],
         compiler_params=params(),
         name="mix",
@@ -442,8 +700,9 @@
         ]
         + [pltpu.VMEM((rows, width), F32)] * 5
         + [
-            pltpu.VMEM((STEPS, states, slots, 128), F32), pltpu.VMEM((STEPS, states, slots, 128), F32),
-            pltpu.VMEM((STEPS, 2 * states, slots, 128), F32),
+            pltpu.VMEM((STEPS, states, slots, width), F32), pltpu.VMEM((STEPS, states, slots, width), F32),
+            pltpu.VMEM((STEPS, 2 * states, slots, 128), F32), pltpu.VMEM((STEPS, 2 * states, slots, 128), F32),
+            pltpu.VMEM((states, slots, width), F32),
         ],
         compiler_params=params(),
         name="back",
@@ -461,10 +720,10 @@
             whole((1, width)),
         ],
         out_specs=[
-            rev_spec(model), whole((model, 2 * width)), whole((width, proj_cols)), whole((4, width)), whole((1, width)),
+            rev_piece_spec, whole((model, 2 * width)), whole((width, proj_cols)), whole((4, width)), whole((1, width)),
         ],
         out_shape=[
-            like((total_rows, model), BF16), like((model, 2 * width), F32), like((width, proj_cols), F32),
+            pieces_shape, like((model, 2 * width), F32), like((width, proj_cols), F32),
             like((4, width), F32), like((1, width), F32),
         ],
         scratch_shapes=[

time: 1290 us -> 882 us (0.68)
  Pallas kernels: 511 us -> 294 us
  blocking collectives: 267 us -> 103 us
  local copies, waits for them, and re-layouts: 82.6 us -> 63.2 us
    pallas_call x1, Pallas kernels: 379 us -> 104 us  [body(): pl.pallas_call(functools.partial(back_kernel, slots=slots), grid=grid, in...]
    all_to_all x4 -> x0, blocking collectives: 119 us -> none  [the longest x1 45.6 us: body(): lax.all_to_all(gin.reshape(n_f, d_rows, 2 * width), 'fsdp', 0, 0, tiled=T...]
    pallas_call x0 -> x1, Pallas kernels: none -> 93.3 us  [body(): pl.pallas_call(functools.partial(gather_kernel, n_dp=n_dp, n_f=n_f), in_s...]
    reduce_scatter x2, waiting for transfers between devices: 139 us -> 188 us  [collect(): lax.psum_scatter(v.reshape(total_rows, model), 'fsdp', scatter_dimension=...]
    unnamed x2 -> x1, blocking collectives: 84.7 us -> 39.5 us
    all_gather x2 -> x0, waiting for transfers between devices: 44.7 us -> none  [the longest x1 44.7 us: body(): lax.all_gather(win.reshape(n_f * d_rows, 2 * width), 'dp', axis=0, tiled=...]
    pallas_call x1, Pallas kernels: 77.2 us -> 42.7 us  [body(): pl.pallas_call(functools.partial(mix_kernel, slots=slots), grid=grid, in_...]
    all_gather x2 -> x1, waiting for transfers between devices: 60.4 us -> 36.9 us  [spread(): v = lax.all_gather(v, 'fsdp', axis=0, tiled=False)]
  transfers between devices with their start and end apart: 11 -> 10, of which waited for: 9 -> 6; matrix products, arithmetic and copies ran while one was open for 6% -> 8% of each run, Pallas kernels for 2% -> 18%
where the time goes in v2:
time: 882 us; the launch traced here: 880 us
  waiting for transfers between devices  361 us (41%)
  Pallas kernels  294 us (33%)
  blocking collectives  103 us (12%)
  local copies, waits for them, and re-layouts  63.2 us (7%)
  other arithmetic  25.9 us (3%)
  starting transfers between devices  18.1 us (2%)
  between operations  14.5 us (2%)
    reduce_scatter x2, waiting for transfers between devices, collect(): lax.psum_scatter(v.reshape(total_rows, model), 'fsdp', scatter_dimension=...  188 us
    pallas_call x1, Pallas kernels, body(): pl.pallas_call(functools.partial(back_kernel, slots=slots), grid=grid, in...  104 us
    pallas_call x1, Pallas kernels, body(): pl.pallas_call(functools.partial(gather_kernel, n_dp=n_dp, n_f=n_f), in_s...  93.3 us
    psum x1, blocking collectives, body(): gproj = low(lax.psum(gproj, 'fsdp'))  63.7 us
    psum x1, waiting for transfers between devices, body(): proj = lax.psum(proj, 'fsdp')  55.5 us
    pallas_call x1, Pallas kernels, body(): pl.pallas_call(functools.partial(mix_kernel, slots=slots), grid=grid, in_...  42.7 us
    reduce_scatter x1, waiting for transfers between devices, body(): lax.psum_scatter(jnp.concatenate([low(gout), low(small)], axis=1), 'dp',...  41.2 us
    unnamed x1, blocking collectives  39.5 us
  transfers between devices with their start and end apart: 10, of which 6 were waited for; matrix products, arithmetic and copies ran while one was open for 8% of the time, Pallas kernels for 18%

profile of v2, /device:TPU:0, one launch (start us, length us, event | category | flops | bytes accessed | tf_op | source)
XLA Modules:
  0.0 880.2 jit_solution(5202308787638576319)
XLA Ops:
  8.0 2.3 broadcast_select_fusion
  10.4 5.2 all-to-all-start.1
  15.5 1.8 convert_bitcast_fusion
  26.0 93.3 %gather.1 = (bf16[4,8,64,2048]{3,2,1,0:T(8,128)(2,1)}, bf16[4,8,64,1024]{3,2,1,0:T(8,128)(2,1)}, f32[4,8,8,128]{3,2,1,0:T(8,128)}, bf16[4,128,2432]{2,1,0:T(8,128)(2,1)}) custom-call(bf16[4,64,2048]{2,1,0:T(8,128)(2,1)} %bitcast.87, bf16[8,64,1024]{2,1,0:T(8,128)(2,1)} %reshape.168.win_ref, f32[8,128]{1,0:T(8,128)} %pad_convert_fusion.gain_ref, ...), custom_call_target="tpu_custom_call" | custom-call | tf_op jit(solution)/shard_map/gather/pallas_call | solution.py:592
  126.4 19.4 %front.1 = (f32[2048,512]{1,0:T(8,128)}, f32[2048,512]{1,0:T(8,128)}, bf16[2048,512]{1,0:T(8,128)(2,1)}, f32[2048,160]{1,0:T(8,128)}) custom-call(bf16[2048,2048]{1,0:T(8,128)(2,1)} %bitcast.76, f32[1,2048]{1,0:T(1,128)} %reshape_squeeze.3.gain_ref, bf16[2048,1024]{1,0:T(8,128)(2,1)} %bitcast.79, f32[4,512]{1,0:T(4,128)} %bitcast.100, ...), custom_call_target="tpu_custom_call" | custom-call | tf_op jit(solution)/shard_map/front/pallas_call | solution.py:638
  147.7 3.2 slice.102.ow_ref
  155.1 55.5 %all-reduce.6.cloned.1.call-done = f32[2048,160]{1,0:T(8,128)} async-done(((f32[2048,160]{1,0:T(8,128)}), f32[2048,160]{1,0:T(8,128)}) %all-reduce.6.cloned.1.call-update) | async-done | bytes 1310736 | tf_op jit(solution)/shard_map/psum | solution.py:655
  210.6 2.3 slice.97.bc_ref
  212.8 2.1 slice.117.dtl_ref
  214.9 42.7 %mix.1 = (f32[2048,512]{1,0:T(8,128)}, f32[8,16,8,512]{3,2,1,0:T(8,128)}, bf16[8,4,64,2048]{3,2,1,0:T(8,128)(2,1)}) custom-call(bf16[2048,128]{1,0:T(8,128)(2,1)} %slice.117.dtl_ref, f32[2048,32]{1,0:T(8,128)} %slice.97.bc_ref, bf16[2048,512]{1,0:T(8,128)(2,1)} %get-tuple-element.53.inp_ref, f32[2048,512]{1,0:T(8,128)} %get-tuple-element.54.gate_ref, ...), custom_call_target="tpu_custom_call" | custom-call | tf_op jit(solution)/shard_map/mix/pallas_call | solution.py:659
  257.6 36.9 %all-gather.3.cloned.1.call-done = bf16[32,8,8,2048]{3,2,1,0:T(8,128)(2,1)} async-done(((bf16[4,8,8,2048]{3,2,1,0:T(8,128)(2,1)}), bf16[32,8,8,2048]{3,2,1,0:T(8,128)(2,1)}) %all-gather.3.cloned.1.call-update) | async-done | bytes 8388624 | tf_op jit(solution)/shard_map/all_gather | solution.py:564
  294.5 8.3 copy.174
  302.7 103.8 %back.1 = (f32[2048,512]{1,0:T(8,128)}, bf16[2048,512]{1,0:T(8,128)(2,1)}, f32[2048,160]{1,0:T(8,128)}, f32[512,2048]{1,0:T(8,128)}, f32[512,128]{1,0:T(8,128)},...) custom-call(bf16[2048,2048]{1,0:T(8,128)(2,1)} %bitcast.78, bf16[2048,128]{1,0:T(8,128)(2,1)} %slice.117.dtl_ref, ...), custom_call_target="tpu_custom_call" | custom-call | tf_op jit(solution)/shard_map/back/pallas_call | solution.py:680
  406.5 63.7 %all-reduce.7.gproj_ref = bf16[2048,160]{1,0:T(8,128)(2,1)} all-reduce(f32[2048,160]{1,0:T(8,128)} %get-tuple-element.58), channel_id=1, replica_groups=mesh['dp'=4,'fsdp'=8] {'fsdp'}, use_global_device_ids=true, to_apply=%region_4.5 | all-reduce | flops 327680 | bytes 1966080 | tf_op jit(solution)/shard_map/psum | solution.py:711
  470.2 35.2 %tail.1 = (bf16[8,4,64,2048]{3,2,1,0:T(8,128)(2,1)}, f32[2048,1024]{1,0:T(8,128)}, f32[512,160]{1,0:T(8,128)}, f32[4,512]{1,0:T(4,128)}, f32[1,512]{1,0:T(1,128)}) custom-call(bf16[2048,160]{1,0:T(8,128)(2,1)} %all-reduce.7.gproj_ref, bf16[2048,512]{1,0:T(8,128)(2,1)} %get-tuple-element.53.inp_ref, f32[2048,512]{1,0:T(8,128)} %get-tuple-element.59.gis_ref, ...), custom_call_target="tpu_custom_call" | custom-call | tf_op jit(solution)/shard_map/tail/pallas_call | solution.py:713
  505.4 6.0 convert_element_type.130
  514.8 2.5 convert_element_type.135
  520.8 4.7 concatenate.12
  525.5 38.4 %reduce-scatter.9.cloned.1.call-done = bf16[512,1024]{1,0:T(8,128)(2,1)} async-done(((bf16[2048,1024]{1,0:T(8,128)(2,1)}), bf16[512,1024]{1,0:T(8,128)(2,1)}) %reduce-scatter.9.cloned.1.call-update) | async-done | bytes 1048592 | tf_op jit(solution)/shard_map/reduce_scatter | solution.py:750
  563.9 4.6 all-to-all-start.3
  568.5 101.9 %reduce-scatter.7.cloned.1.call-done = bf16[256,2048]{1,0:T(8,128)(2,1)} async-done(((bf16[2048,2048]{1,0:T(8,128)(2,1)}), bf16[256,2048]{1,0:T(8,128)(2,1)}) %reduce-scatter.7.cloned.1.call-update) | async-done | bytes 1048592 | tf_op jit(solution)/shard_map/reduce_scatter | solution.py:568
  670.4 2.8 copy.178
  674.2 3.5 all-to-all-start.2
  678.1 86.0 %reduce-scatter.5.cloned.1.call-done = bf16[256,2048]{1,0:T(8,128)(2,1)} async-done(((bf16[2048,2048]{1,0:T(8,128)(2,1)}), bf16[256,2048]{1,0:T(8,128)(2,1)}) %reduce-scatter.5.cloned.1.call-update) | async-done | bytes 1048592 | tf_op jit(solution)/shard_map/reduce_scatter | solution.py:568
  764.0 2.8 copy.172
  766.8 4.3 all-to-all-start
  771.1 41.2 %reduce-scatter.11.cloned.1.call-done = bf16[128,2359]{1,0:T(8,128)(2,1)} async-done(((bf16[512,2359]{1,0:T(8,128)(2,1)}), bf16[128,2359]{1,0:T(8,128)(2,1)}) %reduce-scatter.11.cloned.1.call-update) | async-done | bytes 603920 | tf_op jit(solution)/shard_map/reduce_scatter | solution.py:754
  820.6 2.9 reshape.186
  823.6 2.8 copy.179
  826.4 2.5 copy.203
  829.8 39.5 %all-reduce.2 = f32[2048]{0:T(1024)S(1)} all-reduce(f32[2048]{0:T(1024)S(1)} %get-tuple-element.147), channel_id=5, replica_groups=mesh['dp'=4,'fsdp'=8] {'dp','fsdp'}, use_global_device_ids=true, to_apply=%region_8.9.clone | all-reduce | flops 2048 | bytes 16384
  869.9 3.5 fusion.4
  (124 shorter events, 40.3 us)
Async XLA Ops:
  8.0 2.3 copy-start.6
  10.4 135.5 %all-to-all-start.1 = ((bf16[4,8,8,2048]{3,1,2,0:T(8,128)(2,1)}), bf16[4,8,8,2048]{3,1,2,0:T(8,128)(2,1)S(1)}, u32[]{:S(2)}, u32[]{:S(2)}) async-start(bf16[4,8,8,2048]{3,1,2,0:T(8,128)(2,1)} %bitcast.21), calls=%async_computation.2 | async-start | bytes 2097152 | tf_op jit(solution)/shard_map/all_to_all | solution.py:563
  15.5 195.0 %all-reduce.6.cloned.1.call-start = ((), (), s32[]{:S(2)}) async-start(), calls=%async_computation.8 | async-start | bytes 4194304 | tf_op jit(solution)/shard_map/psum | solution.py:655
  18.0 2.9 copy-start.5
  18.0 3.1 copy-start.9
  18.0 3.2 copy-start.11
  18.0 3.3 copy-start.15
  18.0 3.5 copy-start.16
  18.1 3.6 copy-start.17
  18.1 4.6 copy-start
  19.6 4.6 copy-start.18
  145.8 148.7 %all-gather.3.cloned.1.call-start = ((), (), s32[]{:S(2)}) async-start(), calls=%async_computation.13 | async-start | bytes 9437184 | tf_op jit(solution)/shard_map/all_gather | solution.py:564
  147.4 416.5 %reduce-scatter.9.cloned.1.call-start = ((), (), s32[]{:S(2)}) async-start(), calls=%async_computation.11 | async-start | bytes 5242880 | tf_op jit(solution)/shard_map/reduce_scatter | solution.py:750
  511.5 159.0 %reduce-scatter.7.cloned.1.call-start = ((), (), s32[]{:S(2)}) async-start(), calls=%async_computation.10 | async-start | bytes 9437184 | tf_op jit(solution)/shard_map/reduce_scatter | solution.py:568
  512.0 252.0 %reduce-scatter.5.cloned.1.call-start = ((), (), s32[]{:S(2)}) async-start(), calls=%async_computation.9 | async-start | bytes 9437184 | tf_op jit(solution)/shard_map/reduce_scatter | solution.py:568
  512.1 1.0 copy-start.4
  512.1 1.1 copy-start.10
  512.1 1.9 copy-start.14
  512.6 299.7 %reduce-scatter.11.cloned.1.call-start = ((), (), s32[]{:S(2)}) async-start(), calls=%async_computation.12 | async-start | bytes 3112960 | tf_op jit(solution)/shard_map/reduce_scatter | solution.py:754
  514.8 2.5 copy-start.8
  514.8 3.3 copy-start.13
  514.8 4.1 copy-start.12
  563.9 109.3 %all-to-all-start.3 = ((bf16[8,64,1024]{2,1,0:T(8,128)(2,1)}), bf16[8,64,1024]{2,1,0:T(8,128)(2,1)S(1)}, u32[]{:S(2)}, u32[]{:S(2)}) async-start(bf16[8,64,1024]{2,1,0:T(8,128)(2,1)} %bitcast.98), calls=%async_computation.6 | async-start | bytes 2097152 | tf_op jit(solution)/shard_map/all_to_all | solution.py:751
  673.2 1.0 copy-start.2
  674.2 92.6 %all-to-all-start.2 = ((bf16[4,8,8,2048]{3,1,2,0:T(8,128)(2,1)}), bf16[4,8,8,2048]{3,1,2,0:T(8,128)(2,1)S(1)}, u32[]{:S(2)}, u32[]{:S(2)}) async-start(bf16[4,8,8,2048]{3,1,2,0:T(8,128)(2,1)} %copy.178), calls=%async_computation.4 | async-start | bytes 2097152 | tf_op jit(solution)/shard_map/all_to_all | solution.py:569
  766.8 103.0 %all-to-all-start = ((bf16[4,8,8,2048]{3,1,2,0:T(8,128)(2,1)}), bf16[4,8,8,2048]{3,1,2,0:T(8,128)(2,1)}, u32[]{:S(2)}, u32[]{:S(2)}) async-start(bf16[4,8,8,2048]{3,1,2,0:T(8,128)(2,1)} %copy.172), calls=%async_computation.1 | async-start | bytes 2097152 | tf_op jit(solution)/shard_map/all_to_all | solution.py:569
  812.3 5.8 copy-start.1
  829.1 40.7 %copy-start.3 = (bf16[32,8,2048]{2,1,0:T(8,128)(2,1)S(1)}, bf16[32,8,2048]{2,1,0:T(8,128)(2,1)}, u32[]{:S(2)}) copy-start(bf16[32,8,2048]{2,1,0:T(8,128)(2,1)} %param.17) | copy-start | bytes 3145732
  829.2 40.7 %copy-start.7 = (pred[32,8]{1,0:T(8,128)(4,1)S(1)}, pred[32,8]{1,0:T(8,128)(4,1)}, u32[]{:S(2)}) copy-start(pred[32,8]{1,0:T(8,128)(4,1)} %copy-done.6) | copy-start | bytes 772
Sparse Core Ops, SparseCore 0:
  145.9 64.6 all-reduce.5
  212.7 81.6 all-gather.2
  511.6 52.2 reduce-scatter.8
  566.2 104.2 reduce-scatter.6
  672.7 91.3 reduce-scatter.4
  767.3 44.9 reduce-scatter.10

commit v3 on v2

--- a/solution.py
+++ b/solution.py
@@ -35,7 +35,7 @@
 
 
 def front_kernel(
-    x_ref, gain_ref, win_ref, cw_ref, cb_ref, xw_ref, inner_ref, gate_ref, inp_ref, proj_ref, pad_ref, *, slots
+    x_ref, gain_ref, win_ref, cw_ref, cb_ref, xw_ref, inner_ref, gate_ref, inp_ref, proj_ref, pad_ref, *, slots, length
 ):
     rows = x_ref.shape[0]
     width = inner_ref.shape[1]
@@ -56,7 +56,8 @@
         total = total + cw_ref[tap : tap + 1, :] * pad_ref[tap * slots : tap * slots + rows, :]
     inp = (total * sigmoid(total)).astype(BF16)
     inp_ref[...] = inp
-    proj_ref[...] = dot(inp, xw_ref[...])
+    proj = dot(inp, xw_ref[...])
+    pack_rows(proj_ref, proj[:, : proj.shape[1] - 32], proj[:, proj.shape[1] - 32 :], length)
     pad_ref[0:halo, :] = pad_ref[rows : rows + halo, :]
 
 
@@ -157,12 +158,11 @@
 def back_kernel(
     gb_ref, dtl_ref, bc_ref, inp_ref, gate_ref, y_ref, ck_ref, dtw_ref, dtb_ref, rate_ref, skip_ref, ow_ref,
     gis_ref, ggate_ref, gproj_ref, gout_ref, grank_ref, gdec_ref, gskip_ref, gbias_ref,
-    lam_scr, dacc_scr, sacc_scr, bacc_scr, rate_scr, delta_scr, u_scr, gy_scr, gu_scr, gd_scr, h_scr, a_scr, gbc_scr, bcb_scr, h_now, *, slots
+    lam_scr, dacc_scr, sacc_scr, bacc_scr, rate_scr, delta_scr, u_scr, gy_scr, gu_scr, gd_scr, h_scr, a_scr, gbc_scr, bcb_scr, h_now, gbc_ref, *, slots, length
 ):
     rows, width = inp_ref.shape
     steps = rows // slots
     states = rate_ref.shape[0]
-    rank = dtl_ref.shape[1]
     step_id = pl.program_id(0)
 
     @pl.when(step_id == 0)
@@ -176,7 +176,7 @@
         for n in range(states):
             rate_scr[n] = jnp.broadcast_to(rate_ref[n : n + 1, :] * LOG2E, (slots, width))
 
-    gb = gb_ref[...]
+    gb = gb_ref[...].reshape(rows, gb_ref.shape[-1])
     gate = gate_ref[...]
     sig = sigmoid(gate)
     silu = gate * sig
@@ -259,7 +259,7 @@
             t = k * TOGETHER + j
             at = pl.ds(pl.multiple_of(t * slots, slots), slots)
             total = lane_sums([gbc_scr[t, n] for n in range(2 * states)])
-            gproj_ref[at, rank:] = total[:, : 2 * states]
+            gbc_ref[at, :] = total[:, : 2 * states]
         return carry
 
     lax.fori_loop(0, steps // TOGETHER, reduce_lanes, 0)
@@ -269,7 +269,7 @@
     bacc_scr[...] += jnp.sum(g_pre.reshape(steps, slots, width), axis=0)
     g_low = g_pre.astype(BF16)
     grank_ref[...] += dot(g_low, dtl_ref[...], ((0,), (0,)))
-    gproj_ref[:, :rank] = dot(g_low, dtw_ref[...])
+    pack_rows(gproj_ref, dot(g_low, dtw_ref[...]), gbc_ref[...], length)
 
     @pl.when(step_id == pl.num_programs(0) - 1)
     def _():
@@ -280,8 +280,9 @@
 
 
 def tail_kernel(
-    gproj_ref, inp_ref, gis_ref, ggate_ref, inner_ref, before_ref, x_ref, gain_ref, win_ref, xw_ref, cw_ref, cb_ref,
-    gnorm_ref, gin_ref, gsel_ref, gcw_ref, gcb_ref, pad_scr, gpad_scr, wacc_scr, cacc_scr, *, slots
+    gdtl_ref, gbc_ref, inp_ref, gis_ref, ggate_ref, inner_ref, before_ref, x_ref, gain_ref, win_ref, xw_ref, cw_ref,
+    cb_ref, gnorm_ref, gin_ref, gsel_ref, gcw_ref, gcb_ref, ggain_ref,
+    gin_scr, pad_scr, gpad_scr, wacc_scr, cacc_scr, *, slots
 ):
     rows, width = inp_ref.shape
     steps = rows // slots
@@ -294,10 +295,11 @@
         gpad_scr[rows : rows + halo, :] = jnp.zeros((halo, width), F32)
         wacc_scr[...] = jnp.zeros_like(wacc_scr)
         cacc_scr[...] = jnp.zeros_like(cacc_scr)
-        gin_ref[...] = jnp.zeros_like(gin_ref)
+        gin_scr[...] = jnp.zeros_like(gin_scr)
+        ggain_ref[...] = jnp.zeros_like(ggain_ref)
         gsel_ref[...] = jnp.zeros_like(gsel_ref)
 
-    gproj = gproj_ref[...]
+    gproj = jnp.concatenate([gdtl_ref[...], gbc_ref[...]], axis=1)
     gsel_ref[...] += dot(inp_ref[...], gproj, ((0,), (0,)))
     g_inputs = gis_ref[...] + dot(gproj, xw_ref[...], ((1,), (1,)))
     first = (step_id < last).astype(F32)
@@ -319,15 +321,19 @@
     cacc_scr[...] += jnp.sum(g_conv.reshape(steps, slots, width), axis=0)
     gpad_scr[rows : rows + halo, :] = gpad_scr[0:halo, :]
     g_both = jnp.concatenate([g_inner.astype(BF16), ggate_ref[...]], axis=1)
-    normed = rms_normed(x_ref[...].astype(F32), gain_ref[...])
-    gin_ref[...] += dot(normed, g_both, ((0,), (0,)))
-    gnorm_ref[...] = dot(g_both, win_ref[...], ((1,), (1,))).astype(gnorm_ref.dtype).reshape(gnorm_ref.shape)
+    x = x_ref[...].astype(F32)
+    scaled = x * lax.rsqrt(jnp.mean(x * x, axis=-1, keepdims=True) + EPSILON)
+    gin_scr[...] += dot((scaled * gain_ref[...]).astype(BF16), g_both, ((0,), (0,)))
+    g_normed = dot(g_both, win_ref[...], ((1,), (1,)))
+    ggain_ref[...] += jnp.sum(g_normed * scaled, axis=0, keepdims=True)
+    gnorm_ref[...] = g_normed.astype(gnorm_ref.dtype).reshape(gnorm_ref.shape)
 
     @pl.when(step_id == last)
     def _():
         for tap in range(4):
             gcw_ref[tap : tap + 1, :] = jnp.sum(wacc_scr[tap], axis=0, keepdims=True)
         gcb_ref[...] = jnp.sum(cacc_scr[...], axis=0, keepdims=True)
+        gin_ref[...] = gin_scr[...].astype(gin_ref.dtype)
 
 
 def remote(src, dst, send, recv, where):
@@ -337,9 +343,9 @@
 
 
 def gather_kernel(
-    tok_ref, win_ref, gain_ref, pk_ref, x_ref, w_ref, g_ref, p_ref,
-    tok_buf, win_buf, gain_buf, pk_buf, local_sem,
-    tdp_send, tdp_recv, up_send, up_recv, down_send, down_recv, core_send, core_recv,
+    tok_ref, cot_ref, win_ref, gain_ref, pk_ref, x_ref, c_ref, w_ref, g_ref, p_ref,
+    tok_buf, cot_buf, win_buf, gain_buf, pk_buf, local_sem,
+    tdp_send, tdp_recv, cdp_send, cdp_recv, up_send, up_recv, down_send, down_recv, core_send, core_recv,
     w1_send, w1_recv, w2_send, w2_recv, g1_send, g1_recv, g2_send, g2_recv, p_send, p_recv, *, n_dp, n_f
 ):
     d = lax.axis_index("dp")
@@ -361,12 +367,14 @@
         pltpu.make_async_copy(win_ref.at[f], win_buf, local_sem.at[1]),
         pltpu.make_async_copy(gain_ref, gain_buf, local_sem.at[2]),
         pltpu.make_async_copy(pk_ref, pk_buf, local_sem.at[3]),
+        pltpu.make_async_copy(cot_ref.at[d], cot_buf, local_sem.at[8]),
     )
     stores = (
         pltpu.make_async_copy(tok_buf, x_ref.at[d, f], local_sem.at[4]),
         pltpu.make_async_copy(win_buf, w_ref.at[d, f], local_sem.at[5]),
         pltpu.make_async_copy(gain_buf, g_ref.at[d, f], local_sem.at[6]),
         pltpu.make_async_copy(pk_buf, p_ref.at[d], local_sem.at[7]),
+        pltpu.make_async_copy(cot_buf, c_ref.at[d], local_sem.at[9]),
     )
     for load in loads:
         load.start()
@@ -378,6 +386,14 @@
     def tok_dp_arrival(k):
         src = (d - k + n_dp) % n_dp
         return remote(tok_ref.at[d], x_ref.at[src, f], tdp_send.at[k], tdp_recv.at[k], (src, f))
+
+    def cot_dp(k):
+        to = (d + k) % n_dp
+        return remote(cot_ref.at[to], c_ref.at[d], cdp_send.at[k], cdp_recv.at[k], (to, f))
+
+    def cot_dp_arrival(k):
+        src = (d - k + n_dp) % n_dp
+        return remote(cot_ref.at[d], c_ref.at[src], cdp_send.at[k], cdp_recv.at[k], (src, f))
 
     def w1(k):
         to = (f + k) % n_f
@@ -461,6 +477,8 @@
         g1(k).start()
     for k in range(1, n_dp):
         pk(k).start()
+    for k in range(1, n_dp):
+        cot_dp(k).start()
     for load, store in zip(loads, stores):
         load.wait()
         store.start()
@@ -517,6 +535,8 @@
 
     for k in range(1, n_dp):
         pk_arrival(k).wait_recv()
+        cot_dp_arrival(k).wait_recv()
+        cot_dp(k).wait_send()
         w2_arrival(k).wait_recv()
         g2_arrival(k).wait_recv()
         tok_dp(k).wait_send()
@@ -528,8 +548,319 @@
         g1(k).wait_send()
 
 
+def pack_rows(out_ref, main, rest, chunk):
+    part = chunk // 4
+    for q in range(main.shape[0] // chunk):
+        out_ref[q, 0:chunk, :] = main[q * chunk : (q + 1) * chunk, :]
+        for j in range(4):
+            first = q * chunk + j * part
+            out_ref[q, chunk : chunk + part, j * 32 : (j + 1) * 32] = rest[first : first + part, :]
+
+
+def combine_kernel(
+    part_ref, main_ref, rest_ref, one, sums, two, tops, rests,
+    one_send, one_recv, two_send, two_recv, top_send, top_recv, rest_send, rest_recv,
+    ctop_send, ctop_recv, crest_send, crest_recv, *, n_dp, n_f
+):
+    d = lax.axis_index("dp")
+    f = lax.axis_index("fsdp")
+    n_z = n_f // 2
+    z = f // 2
+    core = f % 2
+    other = 1 - core
+    partner = z * 2 + other
+    chunk = tops.shape[2]
+
+    barrier = pltpu.get_barrier_semaphore()
+    pl.semaphore_signal(barrier, inc=1, device_id=(d, partner), device_id_type=pl.DeviceIdType.MESH)
+    for k in range(1, n_z):
+        pl.semaphore_signal(
+            barrier, inc=1, device_id=(d, (z + k) % n_z * 2 + core), device_id_type=pl.DeviceIdType.MESH
+        )
+    pl.semaphore_wait(barrier, n_z)
+
+    def first(k):
+        to = (z + k) % n_z
+        return remote(part_ref.at[to, other], one.at[to], one_send.at[k], one_recv.at[k], (d, partner))
+
+    def second(k):
+        to = (z + k) % n_z
+        return remote(sums.at[to], two.at[k], two_send.at[k], two_recv.at[k], (d, to * 2 + core))
+
+    def third(k):
+        to = ((z + k) % n_z * 2 + core,)
+        return (
+            remote(tops.at[z, core], tops.at[z, core], top_send.at[k], top_recv.at[k], (d,) + to),
+            remote(rests.at[z, core], rests.at[z, core], rest_send.at[k], rest_recv.at[k], (d,) + to),
+        )
+
+    def third_arrival(k):
+        src = (z - k + n_z) % n_z
+        to = (src * 2 + core,)
+        return (
+            remote(tops.at[src, core], tops.at[src, core], top_send.at[k], top_recv.at[k], (d,) + to),
+            remote(rests.at[src, core], rests.at[src, core], rest_send.at[k], rest_recv.at[k], (d,) + to),
+        )
+
+    def fourth(k, side):
+        src = (z - k + n_z) % n_z
+        return (
+            remote(tops.at[src, side], tops.at[src, side], ctop_send.at[k], ctop_recv.at[k], (d, partner)),
+            remote(rests.at[src, side], rests.at[src, side], crest_send.at[k], crest_recv.at[k], (d, partner)),
+        )
+
+    order = list(range(1, n_z)) + [0]
+    for k in order:
+        first(k).start()
+    for k in order:
+        to = (z + k) % n_z
+        first(k).wait_recv()
+        sums[to] = (part_ref[to, core] + one[to]).astype(sums.dtype)
+        if k:
+            second(k).start()
+    total = part_ref[z, core] + one[z]
+    for k in range(1, n_z):
+        second(k).wait_recv()
+        total = total + two[k].astype(F32)
+    tops[z, core] = total[0:chunk, :].astype(tops.dtype)
+    rests[z, core] = total[chunk:, :].astype(rests.dtype)
+    for k in range(1, n_z):
+        for copy in third(k):
+            copy.start()
+    for copy in fourth(0, core):
+        copy.start()
+    for k in range(1, n_z):
+        for copy in third_arrival(k):
+            copy.wait_recv()
+        for copy in fourth(k, core):
+            copy.start()
+    for k in range(n_z):
+        for copy in fourth(k, other):
+            copy.wait_recv()
+    part = chunk // 4
+    for a in range(n_z):
+        for b in range(2):
+            at = (a * 2 + b) * chunk
+            main_ref[at : at + chunk, :] = tops[a, b]
+            rest = rests[a, b]
+            for j in range(4):
+                rest_ref[at + j * part : at + (j + 1) * part, :] = rest[:, j * 32 : (j + 1) * 32]
+    for k in range(n_z):
+        first(k).wait_send()
+        for copy in fourth(k, core):
+            copy.wait_send()
+        if k:
+            second(k).wait_send()
+            for copy in third(k):
+                copy.wait_send()
+
+
+def scatter_kernel(
+    gn_ref, gin_ref, gg_ref, out_ref, gout_ref, ggout_ref,
+    mine, theirs, rup, rdown, blocks, got, gsum, ggot, ggsum, local_sem,
+    one_send, one_recv, up_send, up_recv, down_send, down_recv, dp_send, dp_recv,
+    w1_send, w1_recv, w2_send, w2_recv, g1_send, g1_recv, g2_send, g2_recv, *, n_dp, n_f
+):
+    d = lax.axis_index("dp")
+    f = lax.axis_index("fsdp")
+    n_z = n_f // 2
+    z = f // 2
+    core = f % 2
+    other = 1 - core
+    partner = z * 2 + other
+
+    barrier = pltpu.get_barrier_semaphore()
+    for k in range(1, n_f):
+        pl.semaphore_signal(barrier, inc=1, device_id=(d, (f + k) % n_f), device_id_type=pl.DeviceIdType.MESH)
+    for k in range(1, n_dp):
+        pl.semaphore_signal(barrier, inc=1, device_id=((d + k) % n_dp, f), device_id_type=pl.DeviceIdType.MESH)
+    pl.semaphore_wait(barrier, n_f + n_dp - 2)
+
+    def one(to, j):
+        return remote(
+            gn_ref.at[to * 2 + other, j], theirs.at[to, j], one_send.at[to, j], one_recv.at[to, j], (d, partner)
+        )
+
+    def up(to, j):
+        return remote(mine.at[to, j], rup.at[to, j], up_send.at[to, j], up_recv.at[to, j], (d, f + 2))
+
+    def down(to, j):
+        return remote(mine.at[to, j], rdown.at[to, j], down_send.at[to, j], down_recv.at[to, j], (d, f - 2))
+
+    def dp(k):
+        to = (d + k) % n_dp
+        return remote(blocks.at[to], out_ref.at[d], dp_send.at[k], dp_recv.at[k], (to, f))
+
+    def dp_arrival(k):
+        src = (d - k + n_dp) % n_dp
+        return remote(blocks.at[src], out_ref.at[src], dp_send.at[k], dp_recv.at[k], (src, f))
+
+    def w1(k):
+        to = (d + k) % n_dp
+        return remote(gin_ref.at[to], got.at[k], w1_send.at[k], w1_recv.at[k], (to, f))
+
+    def g1(k):
+        to = (d + k) % n_dp
+        return remote(gg_ref.at[to], ggot.at[k], g1_send.at[k], g1_recv.at[k], (to, f))
+
+    def w2(k):
+        to = (f + k) % n_f
+        return remote(gsum.at[to], gout_ref.at[f], w2_send.at[k], w2_recv.at[k], (d, to))
+
+    def w2_arrival(k):
+        src = (f - k + n_f) % n_f
+        return remote(gsum.at[src], gout_ref.at[src], w2_send.at[k], w2_recv.at[k], (d, src))
+
+    def g2(k):
+        to = (f + k) % n_f
+        return remote(ggsum.at[to], ggout_ref.at[f], g2_send.at[k], g2_recv.at[k], (d, to))
+
+    def g2_arrival(k):
+        src = (f - k + n_f) % n_f
+        return remote(ggsum.at[src], ggout_ref.at[src], g2_send.at[k], g2_recv.at[k], (d, src))
+
+    def load(to, j):
+        return pltpu.make_async_copy(gn_ref.at[to * 2 + core, j], mine.at[to, j], local_sem.at[to, j])
+
+    own_gin = pltpu.make_async_copy(gin_ref.at[d], got.at[0], local_sem.at[n_z, 0])
+    own_gg = pltpu.make_async_copy(gg_ref.at[d], ggot.at[0], local_sem.at[n_z, 1])
+    put_block = pltpu.make_async_copy(blocks.at[d], out_ref.at[d], local_sem.at[n_z, 2])
+    put_gin = pltpu.make_async_copy(gsum.at[f], gout_ref.at[f], local_sem.at[n_z, 3])
+    put_gg = pltpu.make_async_copy(ggsum.at[f], ggout_ref.at[f], local_sem.at[n_z + 1, 0])
+
+    for far in range(n_z - 1, -1, -1):
+        for j in range(n_dp):
+
+            @pl.when(z + far < n_z)
+            def _():
+                one(z + far, j).start()
+                load(z + far, j).start()
+
+            if far:
+
+                @pl.when(z >= far)
+                def _():
+                    one(z - far, j).start()
+                    load(z - far, j).start()
+
+    for k in range(1, n_dp):
+        w1(k).start()
+        g1(k).start()
+    own_gin.start()
+    own_gg.start()
+
+    def pair(to, j):
+        one(to, j).wait_recv()
+        load(to, j).wait()
+        return mine[to, j].astype(F32) + theirs[to, j].astype(F32)
+
+    def weights():
+        own_gin.wait()
+        own_gg.wait()
+        for k in range(1, n_dp):
+            w1(k).wait_recv()
+            g1(k).wait_recv()
+
+        def add(q, carry):
+            total = got[0, q].astype(F32)
+            for k in range(1, n_dp):
+                total = total + got[k, q].astype(F32)
+            gsum[q] = total.astype(gsum.dtype)
+            total = ggot[0, q]
+            for k in range(1, n_dp):
+                total = total + ggot[k, q]
+            ggsum[q] = total
+            return carry
+
+        lax.fori_loop(0, n_f, add, 0)
+        for k in range(1, n_f):
+            w2(k).start()
+            g2(k).start()
+        put_gin.start()
+        put_gg.start()
+
+    for far in range(n_z - 1, 0, -1):
+        for j in range(n_dp):
+
+            @pl.when(z + far < n_z)
+            def _():
+                to = z + far
+                total = pair(to, j)
+                mine[to, j] = total.astype(mine.dtype)
+
+                @pl.when(z > 0)
+                def _():
+                    up(to, j).wait_recv()
+                    mine[to, j] = (mine[to, j].astype(F32) + rup[to, j].astype(F32)).astype(mine.dtype)
+
+                up(to, j).start()
+
+            @pl.when(z >= far)
+            def _():
+                to = z - far
+                total = pair(to, j)
+                mine[to, j] = total.astype(mine.dtype)
+
+                @pl.when(z < n_z - 1)
+                def _():
+                    down(to, j).wait_recv()
+                    mine[to, j] = (mine[to, j].astype(F32) + rdown[to, j].astype(F32)).astype(mine.dtype)
+
+                down(to, j).start()
+
+    weights()
+    for j in range(n_dp):
+        mine[z, j] = pair(z, j).astype(mine.dtype)
+
+        @pl.when(z > 0)
+        def _():
+            up(z, j).wait_recv()
+            mine[z, j] = (mine[z, j].astype(F32) + rup[z, j].astype(F32)).astype(mine.dtype)
+
+        @pl.when(z < n_z - 1)
+        def _():
+            down(z, j).wait_recv()
+            mine[z, j] = (mine[z, j].astype(F32) + rdown[z, j].astype(F32)).astype(mine.dtype)
+
+        blocks[j] = mine[z, j]
+    for k in range(1, n_dp):
+        dp(k).start()
+    put_block.start()
+
+    for k in range(1, n_f):
+        w2_arrival(k).wait_recv()
+        g2_arrival(k).wait_recv()
+    for k in range(1, n_dp):
+        dp_arrival(k).wait_recv()
+    put_block.wait()
+    put_gin.wait()
+    put_gg.wait()
+    for k in range(1, n_f):
+        w2(k).wait_send()
+        g2(k).wait_send()
+    for k in range(1, n_dp):
+        w1(k).wait_send()
+        g1(k).wait_send()
+        dp(k).wait_send()
+    for to in range(n_z):
+        for j in range(n_dp):
+            one(to, j).wait_send()
+
+            @pl.when(z < to)
+            def _():
+                up(to, j).wait_send()
+
+            @pl.when(z > to)
+            def _():
+                down(to, j).wait_send()
+
+
 def whole(shape):
     return pl.BlockSpec(shape, lambda i: (0,) * len(shape))
+
+
+def cost(micros):
+    return pl.CostEstimate(flops=int(micros * 1.15e9), bytes_accessed=1 << 20, transcendentals=0)
 
 
 def params():
@@ -558,20 +889,17 @@
     own_pos = (group * n_f + member) * own + jnp.arange(own, dtype=jnp.int32)
     own_mask = own_pos[None, :] < seq_len[:, None]
 
-    def spread(v):
-        v = v.reshape(n_dp, slots, own, model).transpose(0, 2, 1, 3)
-        v = lax.all_to_all(v, "dp", 0, 0, tiled=True)
-        v = lax.all_gather(v, "fsdp", axis=0, tiled=False)
-        return v.transpose(1, 0, 2, 3, 4).reshape(total_rows, model)
+    def by_group(v):
+        return v.reshape(n_dp, slots, own, model).transpose(0, 2, 1, 3).reshape(n_dp, own * slots, model)
 
     def collect(v):
         v = lax.psum_scatter(v.reshape(total_rows, model), "fsdp", scatter_dimension=0, tiled=True)
         v = lax.all_to_all(v.reshape(n_dp, own, slots, model), "dp", 0, 0, tiled=True)
         return v.transpose(0, 2, 1, 3).reshape(seqs, own, model)
 
-    g_branch = spread(jnp.where(own_mask[:, :, None], cotangent, jnp.zeros_like(cotangent)))
-
-    tok = tokens.reshape(n_dp, slots, own, model).transpose(0, 2, 1, 3).reshape(n_dp, own * slots, model)
+    masked = by_group(jnp.where(own_mask[:, :, None], cotangent, jnp.zeros_like(cotangent)))
+
+    tok = by_group(tokens)
     win = low(in_weight).reshape(d_rows, 2, n_dp, n_f, inner_rows).transpose(3, 0, 1, 2, 4)
     win = win.reshape(n_f, d_rows, 2 * width)
     gain_tile = jnp.zeros((8, 128), F32).at[0, :d_rows].set(low(norm_gain).astype(F32))
@@ -589,26 +917,30 @@
     n_z = n_f // 2
     dma = pltpu.SemaphoreType.DMA
     hbm = pl.BlockSpec(memory_space=pl.ANY)
-    x, win, gain, packed = pl.pallas_call(
+    x, g_branch, win, gain, packed = pl.pallas_call(
         functools.partial(gather_kernel, n_dp=n_dp, n_f=n_f),
-        in_specs=[hbm] * 4,
-        out_specs=[hbm] * 4,
+        in_specs=[hbm] * 5,
+        out_specs=[hbm] * 5,
         out_shape=[
             jax.ShapeDtypeStruct((n_dp, n_f) + tok.shape[1:], BF16),
+            jax.ShapeDtypeStruct(tok.shape, BF16),
             jax.ShapeDtypeStruct((n_dp, n_f) + win.shape[1:], BF16),
             jax.ShapeDtypeStruct((n_dp, n_f, 8, 128), F32),
             jax.ShapeDtypeStruct((n_dp,) + packed.shape, BF16),
         ],
         scratch_shapes=[
-            pltpu.VMEM(tok.shape[1:], BF16), pltpu.VMEM(win.shape[1:], BF16), pltpu.VMEM((8, 128), F32),
-            pltpu.VMEM(packed.shape, BF16), dma((8,)), dma((n_dp,)), dma((n_dp,)),
+            pltpu.VMEM(tok.shape[1:], BF16), pltpu.VMEM(tok.shape[1:], BF16), pltpu.VMEM(win.shape[1:], BF16),
+            pltpu.VMEM((8, 128), F32), pltpu.VMEM(packed.shape, BF16), dma((10,)),
+            dma((n_dp,)), dma((n_dp,)), dma((n_dp,)), dma((n_dp,)),
         ]
         + [dma((n_z, n_dp))] * 6
         + [dma((n_f,)), dma((n_f,)), dma((n_dp,)), dma((n_dp,)), dma((n_f,)), dma((n_f,))]
         + [dma((n_dp,))] * 4,
         compiler_params=pltpu.CompilerParams(collective_id=1, has_side_effects=True),
+        cost_estimate=cost(90),
         name="gather",
-    )(tok, win, gain_tile, packed)
+    )(tok, masked, win, gain_tile, packed)
+    g_branch = lax.all_gather(g_branch, "fsdp", axis=0, tiled=False)
     x = x.reshape(total_rows, model)
     win = win.reshape(model, 2 * width)
     gain = gain[:, :, 0, :d_rows].reshape(1, model)
@@ -634,27 +966,51 @@
     piece_spec = pl.BlockSpec(piece, lambda i: (i % per, i // per, 0, 0))
     rev_piece_spec = pl.BlockSpec(piece, lambda i: ((blocks - 1 - i) % per, (blocks - 1 - i) // per, 0, 0))
     pieces_shape = like((n_f, n_dp, own * slots, model), BF16)
+    packed_rows = length + length // 4
+    parts = rows // length
+    part_spec = pl.BlockSpec((parts, packed_rows, 128), lambda i: (i, 0, 0))
+    rev_part_spec = pl.BlockSpec((parts, packed_rows, 128), lambda i: (blocks - 1 - i, 0, 0))
+    parts_shape = like((n_f, packed_rows, 128), F32)
+
+    def combine(v, rest_type, number):
+        vmem = pl.BlockSpec(memory_space=pltpu.VMEM)
+        return pl.pallas_call(
+            functools.partial(combine_kernel, n_dp=n_dp, n_f=n_f),
+            in_specs=[vmem],
+            out_specs=[vmem, vmem],
+            out_shape=[like((total_rows, rank), BF16), like((total_rows, 2 * states), rest_type)],
+            scratch_shapes=[
+                pltpu.VMEM((n_z, packed_rows, 128), F32), pltpu.VMEM((n_z, packed_rows, 128), F32),
+                pltpu.VMEM((n_z, packed_rows, 128), F32), pltpu.VMEM((n_z, 2, length, 128), BF16),
+                pltpu.VMEM((n_z, 2, length // 4, 128), rest_type),
+            ]
+            + [dma((n_z,))] * 12,
+            compiler_params=pltpu.CompilerParams(
+                collective_id=number, has_side_effects=True, vmem_limit_bytes=VMEM_BYTES
+            ),
+            cost_estimate=cost(28),
+        name="combine",
+        )(v.reshape(n_z, 2, packed_rows, 128))
 
     inner, gate, inp, proj = pl.pallas_call(
-        functools.partial(front_kernel, slots=slots),
+        functools.partial(front_kernel, slots=slots, length=length),
         grid=grid,
         in_specs=[
             row_spec(model), whole((1, model)), whole((model, 2 * width)), whole((4, width)), whole((1, width)),
             whole((width, proj_cols)),
         ],
-        out_specs=[row_spec(width), row_spec(width), row_spec(width), row_spec(proj_cols)],
+        out_specs=[row_spec(width), row_spec(width), row_spec(width), part_spec],
         out_shape=[
             like((total_rows, width), F32), like((total_rows, width), F32), like((total_rows, width), BF16),
-            like((total_rows, proj_cols), F32),
+            parts_shape,
         ],
         scratch_shapes=[pltpu.VMEM((rows + 3 * slots, width), F32)],
         compiler_params=params(),
+        cost_estimate=cost(20),
         name="front",
     )(x, gain, win, cw, cb, xw)
 
-    proj = lax.psum(proj, "fsdp")
-    dtl = low(proj[:, :rank])
-    bc = proj[:, rank:]
+    dtl, bc = combine(proj, F32, 2)
 
     y, ck, branch = pl.pallas_call(
         functools.partial(mix_kernel, slots=slots),
@@ -674,23 +1030,24 @@
             pltpu.VMEM((states, slots, width), F32), pltpu.VMEM((STEPS, 2 * states, slots, 128), F32),
         ],
         compiler_params=params(),
+        cost_estimate=cost(42),
         name="mix",
     )(dtl, bc, inp, gate, dtw, dtb, rate, skip, ow)
 
     gis, ggate, gproj, gout, grank, gdec, gskip, gbias = pl.pallas_call(
-        functools.partial(back_kernel, slots=slots),
+        functools.partial(back_kernel, slots=slots, length=length),
         grid=grid,
         in_specs=[
-            rev_spec(model), rev_spec(rank), rev_spec(2 * states), rev_spec(width), rev_spec(width), rev_spec(width),
+            rev_piece_spec, rev_spec(rank), rev_spec(2 * states), rev_spec(width), rev_spec(width), rev_spec(width),
             pl.BlockSpec((1, states, slots, width), lambda i: (blocks - 1 - i, 0, 0, 0)),
             whole((width, rank)), whole((1, width)), whole((states, width)), whole((1, width)), whole((width, model)),
         ],
         out_specs=[
-            rev_spec(width), rev_spec(width), rev_spec(proj_cols), whole((width, model)), whole((width, rank)),
+            rev_spec(width), rev_spec(width), rev_part_spec, whole((width, model)), whole((width, rank)),
             whole((states, width)), whole((1, width)), whole((1, width)),
         ],
         out_shape=[
-            like((total_rows, width), F32), like((total_rows, width), BF16), like((total_rows, proj_cols), F32),
+            like((total_rows, width), F32), like((total_rows, width), BF16), parts_shape,
             like((width, model), F32), like((width, rank), F32), like((states, width), F32), like((1, width), F32),
             like((1, width), F32),
         ],
@@ -702,57 +1059,84 @@
         + [
             pltpu.VMEM((STEPS, states, slots, width), F32), pltpu.VMEM((STEPS, states, slots, width), F32),
             pltpu.VMEM((STEPS, 2 * states, slots, 128), F32), pltpu.VMEM((STEPS, 2 * states, slots, 128), F32),
-            pltpu.VMEM((states, slots, width), F32),
+            pltpu.VMEM((states, slots, width), F32), pltpu.VMEM((rows, 2 * states), F32),
         ],
         compiler_params=params(),
+        cost_estimate=cost(104),
         name="back",
     )(g_branch, dtl, bc, inp, gate, y, ck, dtw, dtb, rate, skip, ow)
 
-    gproj = low(lax.psum(gproj, "fsdp"))
-
-    gnorm, gin, gsel, gcw, gcb = pl.pallas_call(
+    gdtl, gbc = combine(gproj, BF16, 3)
+
+    branch = collect(branch)
+    branch, gdtl = lax.optimization_barrier((branch, gdtl))
+    gnorm, gin, gsel, gcw, gcb, ggain = pl.pallas_call(
         functools.partial(tail_kernel, slots=slots),
         grid=grid,
         in_specs=[
-            rev_spec(proj_cols), rev_spec(width), rev_spec(width), rev_spec(width), rev_spec(width),
+            rev_spec(rank), rev_spec(2 * states), rev_spec(width), rev_spec(width), rev_spec(width), rev_spec(width),
             pl.BlockSpec((4 * slots, width), lambda i: (jnp.maximum((blocks - 1 - i) * (STEPS // 4) - 1, 0), 0)),
             rev_spec(model), whole((1, model)), whole((model, 2 * width)), whole((width, proj_cols)), whole((4, width)),
             whole((1, width)),
         ],
         out_specs=[
             rev_piece_spec, whole((model, 2 * width)), whole((width, proj_cols)), whole((4, width)), whole((1, width)),
+            whole((1, model)),
         ],
         out_shape=[
-            pieces_shape, like((model, 2 * width), F32), like((width, proj_cols), F32),
-            like((4, width), F32), like((1, width), F32),
+            pieces_shape, like((model, 2 * width), BF16), like((width, proj_cols), F32),
+            like((4, width), F32), like((1, width), F32), like((1, model), F32),
         ],
         scratch_shapes=[
-            pltpu.VMEM((rows + 3 * slots, width), F32), pltpu.VMEM((rows + 3 * slots, width), F32),
-            pltpu.VMEM((4, slots, width), F32), pltpu.VMEM((slots, width), F32),
+            pltpu.VMEM((model, 2 * width), F32), pltpu.VMEM((rows + 3 * slots, width), F32),
+            pltpu.VMEM((rows + 3 * slots, width), F32), pltpu.VMEM((4, slots, width), F32),
+            pltpu.VMEM((slots, width), F32),
         ],
         compiler_params=params(),
+        cost_estimate=cost(35),
         name="tail",
-    )(gproj, inp, gis, ggate, inner, inner, x, gain, win, xw, cw, cb)
+    )(gdtl, gbc, inp, gis, ggate, inner, inner, x, gain, win, xw, cw, cb)
+
+    small = jnp.concatenate([gsel, grank, gdec.T, gcw.T, gcb.T, gbias.T, gskip.T], axis=1)
+    small = lax.psum_scatter(jnp.concatenate([low(gout), low(small)], axis=1), "dp", scatter_dimension=0, tiled=True)
+    small = small.astype(F32)
+
+    gain_tiles = jnp.pad(ggain.reshape(n_dp, n_f, 1, d_rows), ((0, 0), (0, 0), (0, 7), (0, 128 - d_rows)))
+    tile = own * slots
+    g_normed, gin, gain_tiles = pl.pallas_call(
+        functools.partial(scatter_kernel, n_dp=n_dp, n_f=n_f),
+        in_specs=[hbm] * 3,
+        out_specs=[hbm] * 3,
+        out_shape=[
+            like((n_dp, tile, model), BF16), like((n_f, d_rows, 2 * width), BF16), like((n_f, 8, 128), F32),
+        ],
+        scratch_shapes=[pltpu.VMEM((n_z, n_dp, tile, model), BF16)] * 4
+        + [
+            pltpu.VMEM((n_dp, tile, model), BF16), pltpu.VMEM((n_dp, n_f, d_rows, 2 * width), BF16),
+            pltpu.VMEM((n_f, d_rows, 2 * width), BF16), pltpu.VMEM((n_dp, n_f, 8, 128), F32),
+            pltpu.VMEM((n_f, 8, 128), F32), dma((n_z + 2, n_dp)),
+        ]
+        + [dma((n_z, n_dp))] * 6
+        + [dma((n_dp,))] * 4
+        + [dma((n_f,))] * 2
+        + [dma((n_dp,))] * 2
+        + [dma((n_f,))] * 2,
+        compiler_params=pltpu.CompilerParams(collective_id=4, has_side_effects=True, vmem_limit_bytes=VMEM_BYTES),
+        cost_estimate=cost(92),
+        name="scatter",
+    )(gnorm, gin.reshape(n_dp, n_f, d_rows, 2 * width), gain_tiles)
 
     hidden = tokens.astype(F32)
     upstream = cotangent.astype(F32)
-    output = (hidden + jnp.where(own_mask[:, :, None], collect(branch).astype(F32), 0.0)).astype(BF16)
-    g_normed = collect(gnorm).astype(F32)
+    output = (hidden + jnp.where(own_mask[:, :, None], branch.astype(F32), 0.0)).astype(BF16)
+    g_normed = g_normed.reshape(n_dp, own, slots, model).transpose(0, 2, 1, 3).reshape(seqs, own, model).astype(F32)
     factor = lax.rsqrt(jnp.mean(hidden * hidden, axis=-1, keepdims=True) + EPSILON)
     weighted = gain * g_normed
     input_grad = (
         upstream + factor * weighted - hidden * factor**3 * jnp.mean(hidden * weighted, axis=-1, keepdims=True)
     ).astype(BF16)
-    gain_grad = lax.psum_scatter(
-        jnp.sum(g_normed * hidden * factor, axis=(0, 1)), BOTH, scatter_dimension=0, tiled=True
-    )
-
-    gin = lax.psum_scatter(low(gin), "dp", scatter_dimension=0, tiled=True)
-    gin = lax.all_to_all(gin.reshape(n_f, d_rows, 2 * width), "fsdp", 0, 0, tiled=True)
+    gain_grad = jnp.sum(gain_tiles[:, 0, :d_rows], axis=0)
     gin = gin.reshape(n_f, d_rows, 2, n_dp, inner_rows).transpose(1, 2, 3, 0, 4).reshape(d_rows, -1).astype(F32)
-    small = jnp.concatenate([gsel, grank, gdec.T, gcw.T, gcb.T, gbias.T, gskip.T], axis=1)
-    small = lax.psum_scatter(jnp.concatenate([low(gout), low(small)], axis=1), "dp", scatter_dimension=0, tiled=True)
-    small = small.astype(F32)
     cuts = [model, proj_cols, rank, states, 4, 1, 1, 1]
     pieces, start = [], 0
     for cut in cuts:

time: 882 us -> 573 us (0.65)
  waiting for transfers between devices: 361 us -> 0.08 us
  Pallas kernels: 294 us -> 488 us
  blocking collectives: 103 us -> 0 us
  local copies, waits for them, and re-layouts: 63.2 us -> 44.3 us
  starting transfers between devices: 18.1 us -> 4.05 us
    reduce_scatter x2 -> x1, waiting for transfers between devices: 188 us -> 0.02 us  [collect(): lax.psum_scatter(v.reshape(total_rows, model), 'fsdp', scatter_dimension=...]
    pallas_call x2 -> x5, Pallas kernels: 123 us -> 305 us  [the longest x1 104 us: body(): pl.pallas_call(functools.partial(back_kernel, slots=slots, length=length)...]
    psum x1 -> x0, blocking collectives: 63.7 us -> none  [body(): gproj = low(lax.psum(gproj, 'fsdp'))]
    psum x1 -> x0, waiting for transfers between devices: 55.5 us -> none  [body(): proj = lax.psum(proj, 'fsdp')]
    reduce_scatter x1, waiting for transfers between devices: 41.2 us -> 0.01 us  [body(): lax.psum_scatter(jnp.concatenate([low(gout), low(small)], axis=1), 'dp',...]
    unnamed x1 -> x0, blocking collectives: 39.5 us -> none
    reduce_scatter x1 -> x0, waiting for transfers between devices: 38.4 us -> none  [body(): gin = lax.psum_scatter(low(gin), 'dp', scatter_dimension=0, tiled=True)]
    all_gather x1, waiting for transfers between devices: 36.9 us -> 0.01 us  [body(): g_branch = lax.all_gather(g_branch, 'fsdp', axis=0, tiled=False)]
  transfers between devices with their start and end apart: 10 -> 4, of which waited for: 6 -> 0; matrix products, arithmetic and copies ran while one was open for 8% -> 6% of each run, Pallas kernels for 18% -> 61%
where the time goes in v3:
time: 573 us; the launch traced here: 571 us
  Pallas kernels  488 us (85%)
  local copies, waits for them, and re-layouts  44.3 us (8%)
  other arithmetic  20.7 us (4%)
  between operations  14.3 us (2%)
    pallas_call x1, Pallas kernels, body(): pl.pallas_call(functools.partial(gather_kernel, n_dp=n_dp, n_f=n_f), in_s...  105 us
    pallas_call x1, Pallas kernels, body(): pl.pallas_call(functools.partial(back_kernel, slots=slots, length=length)...  104 us
    pallas_call x1, Pallas kernels, body(): pl.pallas_call(functools.partial(scatter_kernel, n_dp=n_dp, n_f=n_f), in_...  92.6 us
    pallas_call x2, Pallas kernels, combine(): pl.pallas_call(functools.partial(combine_kernel, n_dp=n_dp, n_f=n_f), in_...  88.2 us
    pallas_call x1, Pallas kernels, body(): pl.pallas_call(functools.partial(mix_kernel, slots=slots), grid=grid, in_...  42.8 us
    pallas_call x1, Pallas kernels, body(): pl.pallas_call(functools.partial(tail_kernel, slots=slots), grid=grid, in...  35.3 us
    pallas_call x1, Pallas kernels, body(): pl.pallas_call(functools.partial(front_kernel, slots=slots, length=length...  20.2 us
  transfers between devices with their start and end apart: 4, of which 0 were waited for; matrix products, arithmetic and copies ran while one was open for 6% of the time, Pallas kernels for 61%

profile of v3, /device:TPU:0, one launch (start us, length us, event | category | flops | bytes accessed | tf_op | source)
XLA Modules:
  0.0 571.3 jit_solution(1859777417858828274)
XLA Ops:
  7.2 1.8 convert_bitcast_fusion.1
  9.8 1.5 reshape.176.win_ref
  12.0 1.4 convert_element_type.100
  15.0 2.5 copy_bitcast_fusion.2
  18.7 105.2 %gather.1 = (bf16[4,8,64,2048]{3,2,1,0:T(8,128)(2,1)}, bf16[4,64,2048]{2,1,0:T(8,128)(2,1)}, bf16[4,8,64,1024]{3,2,1,0:T(8,128)(2,1)}, f32[4,8,8,128]{3,2,1,0:T(8,128)}, bf16[4,128,2432]{2,1,0:T(8,128)(2,1)}) custom-call(bf16[4,64,2048]{2,1,0:T(8,128)(2,1)} %get-tuple-element.169.tok_ref, bf16[4,64,2048]{2,1,0:T(8,128)(2,1)} %get-tuple-element.168.cot_ref, ...), custom_call_target="tpu_custom_call" | custom-call | flops 103499997184 | bytes 1048576 | tf_op jit(solution)/shard_map/gather/pallas_call | solution.py:920
  124.2 1.7 slice.90.xw_ref
  125.8 1.7 slice.91.dtw_ref
  127.5 1.0 slice.93
  128.5 3.4 slice.95.ow_ref
  135.4 1.3 fusion.6
  139.5 20.2 %front.1 = (f32[2048,512]{1,0:T(8,128)}, f32[2048,512]{1,0:T(8,128)}, bf16[2048,512]{1,0:T(8,128)(2,1)}, f32[8,320,128]{2,1,0:T(8,128)}) custom-call(bf16[2048,2048]{1,0:T(8,128)(2,1)} %bitcast.94, f32[1,2048]{1,0:T(1,128)} %reshape_squeeze.3.gain_ref, bf16[2048,1024]{1,0:T(8,128)(2,1)} %bitcast.96, f32[4,512]{1,0:T(4,128)} %bitcast.91, ...), custom_call_target="tpu_custom_call" | custom-call | flops 23000000512 | bytes 1048576 | tf_op jit(solution)/shard_map/front/pallas_call | solution.py:995
  159.7 53.5 %combine.2 = (bf16[2048,128]{1,0:T(8,128)(2,1)}, f32[2048,32]{1,0:T(8,128)}) custom-call(f32[4,2,320,128]{3,2,1,0:T(8,128)} %bitcast.100), custom_call_target="tpu_custom_call" | custom-call | flops 32199999488 | bytes 1048576 | tf_op jit(solution)/shard_map/combine/pallas_call | solution.py:977
  213.2 42.8 %mix.1 = (f32[2048,512]{1,0:T(8,128)}, f32[8,16,8,512]{3,2,1,0:T(8,128)}, bf16[8,4,64,2048]{3,2,1,0:T(8,128)(2,1)}) custom-call(bf16[2048,128]{1,0:T(8,128)(2,1)} %get-tuple-element.64.dtl_ref, f32[2048,32]{1,0:T(8,128)} %get-tuple-element.65.bc_ref, bf16[2048,512]{1,0:T(8,128)(2,1)} %get-tuple-element.66.inp_ref, f32[2048,512]{1,0:T(8,128)} %get-tuple-element.67.gate_ref, ...), custom_call_target="tpu_custom_call" | custom-call | flops 48299999232 | bytes 1048576 | tf_op jit(solution)/shard_map/mix/pallas_call | solution.py:1015
  256.6 103.8 %back.1 = (f32[2048,512]{1,0:T(8,128)}, bf16[2048,512]{1,0:T(8,128)(2,1)}, f32[8,320,128]{2,1,0:T(8,128)}, f32[512,2048]{1,0:T(8,128)}, f32[512,128]{1,0:T(8,128...) custom-call(bf16[8,4,64,2048]{3,2,1,0:T(8,128)(2,1)} %bitcast.93, ...), custom_call_target="tpu_custom_call" | custom-call | flops 119599996928 | bytes 1048576 | tf_op jit(solution)/shard_map/back/pallas_call | solution.py:1037
  360.4 2.8 copy.144
  363.2 3.7 all-to-all-start
  367.0 34.6 %combine.3 = (bf16[2048,128]{1,0:T(8,128)(2,1)}, bf16[2048,32]{1,0:T(8,128)(2,1)}) custom-call(f32[4,2,320,128]{3,2,1,0:T(8,128)} %bitcast.99), custom_call_target="tpu_custom_call" | custom-call | flops 32199999488 | bytes 1048576 | tf_op jit(solution)/shard_map/combine/pallas_call | solution.py:977
  401.7 2.5 convert_element_type.124
  405.5 35.3 %tail.1 = (bf16[8,4,64,2048]{3,2,1,0:T(8,128)(2,1)}, bf16[2048,1024]{1,0:T(8,128)(2,1)}, f32[512,160]{1,0:T(8,128)}, f32[4,512]{1,0:T(4,128)}, f32[1,512]{1,0:T(1,128)}, /*index=5*/f32[1,2048]{1,0:T(1,128)}) custom-call(bf16[2048,128]{1,0:T(8,128)(2,1)} %get-tuple-element.75.gdtl_ref, bf16[2048,32]{1,0:T(8,128)(2,1)} %get-tuple-element.76.gbc_ref, ...), custom_call_target="tpu_custom_call" | custom-call | flops 40249999360 | bytes 1048576 | tf_op jit(solution)/shard_map/tail/pallas_call | solution.py:1073
  441.4 1.4 reduce.18
  442.8 1.1 convert.39
  445.6 4.9 concatenate.12
  451.2 92.6 %scatter.12 = (bf16[4,64,2048]{2,1,0:T(8,128)(2,1)}, bf16[8,64,1024]{2,1,0:T(8,128)(2,1)}, f32[8,8,128]{2,1,0:T(8,128)}) custom-call(bf16[8,4,64,2048]{3,2,1,0:T(8,128)(2,1)} %get-tuple-element.80.gn_ref, bf16[4,8,64,1024]{3,2,1,0:T(8,128)(2,1)} %bitcast.98, f32[4,8,8,128]{3,2,1,0:T(8,128)} %pad.15.gg_ref), custom_call_target="tpu_custom_call" | custom-call | flops 105799999488 | bytes 1048576 | tf_op jit(solution)/shard_map/scatter/pallas_call | solution.py:1106
  543.8 1.5 convert_bitcast_fusion
  545.3 1.2 copy.148
  546.5 1.9 reshape.194
  548.5 2.8 copy.149
  551.3 2.5 copy.174
  553.8 1.4 slice_reduce_fusion.3
  555.8 2.2 fusion.4
  559.6 1.2 convert_element_type.125
  563.7 1.1 slice.103
  (121 shorter events, 20.6 us)
Async XLA Ops:
  7.2 249.5 %all-gather.3.cloned.1.call-start = ((), (), s32[]{:S(2)}) async-start(), calls=%async_computation.5 | async-start | bytes 9437184 | tf_op jit(solution)/shard_map/all_gather | solution.py:943
  9.3 2.1 copy-start.19
  9.7 3.7 copy-start.9
  9.7 3.8 copy-start.11
  9.7 3.8 copy-start.15
  9.7 3.9 copy-start.16
  9.8 4.1 copy-start.20
  9.8 4.2 copy-start.21
  9.8 4.3 copy-start.22
  9.8 4.5 copy-start.23
  9.8 4.5 copy-start.24
  9.8 4.6 copy-start.3
  12.0 3.1 copy-start
  14.4 0.6 copy-start.12
  123.9 236.5 %reduce-scatter.3.cloned.1.call-start = ((), (), s32[]{:S(2)}) async-start(), calls=%async_computation.3 | async-start | bytes 9437184 | tf_op jit(solution)/shard_map/reduce_scatter | solution.py:896
  363.2 42.3 %all-to-all-start = ((bf16[4,8,8,2048]{3,1,2,0:T(8,128)(2,1)}), bf16[4,8,8,2048]{3,1,2,0:T(8,128)(2,1)S(1)}, u32[]{:S(2)}, u32[]{:S(2)}) async-start(bf16[4,8,8,2048]{3,1,2,0:T(8,128)(2,1)} %copy.144), calls=%async_computation.1 | async-start | bytes 2097152 | tf_op jit(solution)/shard_map/all_to_all | solution.py:897
  367.0 191.1 %reduce-scatter.5.cloned.1.call-start = ((), (), s32[]{:S(2)}) async-start(), calls=%async_computation.4 | async-start | bytes 3112960 | tf_op jit(solution)/shard_map/reduce_scatter | solution.py:1101
  401.7 2.6 copy-start.8
  401.7 2.6 copy-start.14
  401.7 2.7 copy-start.18
  401.7 2.9 copy-start.17
  405.5 35.3 %copy-start.5 = (bf16[4,8,8,2048]{3,1,2,0:T(8,128)(2,1)}, bf16[4,8,8,2048]{3,1,2,0:T(8,128)(2,1)S(1)}, u32[]{:S(2)}) copy-start(bf16[4,8,8,2048]{3,1,2,0:T(8,128)(2,1)S(1)} %all-to-all-done) | copy-start | bytes 3145732
  545.3 1.2 copy-start.7
  551.3 4.0 copy-start.1
  551.3 4.0 copy-start.10
  553.8 2.0 copy-start.4
  553.8 2.0 copy-start.6
  553.8 2.0 copy-start.13
  558.0 3.5 copy-start.2
Sparse Core Ops, SparseCore 0:
  124.0 102.7 all-gather.2
  256.1 94.3 reduce-scatter.2
  450.7 75.8 reduce-scatter.4

commit v4 on v3

v4 whole, which is shorter than its diff:
```python
import functools
import jax
import jax.numpy as jnp
from jax import lax
from jax.experimental import pallas as pl
from jax.experimental.pallas import tpu as pltpu
from jax.sharding import PartitionSpec as P

EPSILON = 1e-05
STEPS = 32
PAIR = 2
LAG = 4
LANES = 8
TOGETHER = 8
LOG2E = 1.4426950408889634
BOTH = ("dp", "fsdp")
F32 = jnp.float32
BF16 = jnp.bfloat16
VMEM_BYTES = 60 * 1024 * 1024
FULL_VMEM = 63 * 1024 * 1024
DECAY, TAPS, CONV_BIAS, DT_BIAS, SKIP = 32, 48, 52, 53, 54


def dot(a, b, dims=((1,), (0,))):
    return lax.dot_general(a, b, (dims, ((), ())), preferred_element_type=F32)


def sigmoid(v):
    return 1.0 / (1.0 + jnp.exp(-v))


def softplus(v):
    return jnp.maximum(v, 0.0) + jnp.log1p(jnp.exp(-jnp.abs(v)))


def rms_normed(x, gain):
    factor = lax.rsqrt(jnp.mean(x * x, axis=-1, keepdims=True) + EPSILON)
    return (x * factor * gain).astype(BF16)


def front_kernel(
    x_ref, gain_ref, win_ref, xw_ref, misc_ref, inner_ref, gate_ref, inp_ref, proj_ref, pad_ref, misc_scr, *, slots, length
):
    rows = x_ref.shape[0]
    width = inner_ref.shape[1]
    halo = 3 * slots
    normed = rms_normed(x_ref[...].astype(F32), gain_ref[...])
    both = dot(normed, win_ref[...])
    gate_ref[...] = both[:, width:]
    inner = both[:, :width]
    inner_ref[...] = inner

    @pl.when(pl.program_id(0) == 0)
    def _():
        pad_ref[0:halo, :] = jnp.zeros((halo, width), F32)
        misc_scr[...] = jnp.transpose(misc_ref[...].astype(F32))

    pad_ref[halo : halo + rows, :] = inner
    total = jnp.broadcast_to(misc_scr[CONV_BIAS : CONV_BIAS + 1, :], (rows, width))
    for tap in range(4):
        total = total + misc_scr[TAPS + tap : TAPS + tap + 1, :] * pad_ref[tap * slots : tap * slots + rows, :]
    inp = (total * sigmoid(total)).astype(BF16)
    inp_ref[...] = inp
    pack_rows(proj_ref, dot(inp, xw_ref[...]), dot(inp, misc_ref[...])[:, :DECAY], length)
    pad_ref[0:halo, :] = pad_ref[rows : rows + halo, :]


def spread_lanes(bc_ref, out_ref, k, slots, steps):
    for j in range(PAIR):
        t = jnp.minimum(k * PAIR + j, steps - 1)
        at = pl.ds(pl.multiple_of(t * slots, slots), slots)
        for n in range(out_ref.shape[1]):
            out_ref[j, n] = jnp.broadcast_to(bc_ref[at, n : n + 1], (slots, 128))


def widen(piece, width):
    return jnp.concatenate([piece] * (width // 128), axis=1)


def narrow(value):
    total = value[:, :128]
    for first in range(128, value.shape[1], 128):
        total = total + value[:, first : first + 128]
    return total


def mix_kernel(
    dtl_ref, bc_ref, inp_ref, gate_ref, dtw_ref, misc_ref, ow_ref,
    y_ref, ck_ref, br_ref, h_scr, delta_scr, u_scr, rate_scr, even_scr, odd_scr, misc_scr, *, slots
):
    rows, width = inp_ref.shape
    steps = rows // slots
    states = h_scr.shape[0]

    @pl.when(pl.program_id(0) == 0)
    def _():
        h_scr[...] = jnp.zeros_like(h_scr)
        misc_scr[...] = jnp.transpose(misc_ref[...].astype(F32))
        for n in range(states):
            rate_scr[n] = jnp.broadcast_to(-jnp.exp(misc_scr[DECAY + n : DECAY + n + 1, :]) * LOG2E, (slots, width))

    ck_ref[0] = h_scr[...]
    delta = softplus(dot(dtl_ref[...], dtw_ref[...], ((1,), (1,))) + misc_scr[DT_BIAS : DT_BIAS + 1, :])
    delta_scr[...] = delta
    u_scr[...] = delta * inp_ref[...].astype(F32)
    spread_lanes(bc_ref, even_scr, 0, slots, steps)

    def step(k, bcb_scr, next_scr):
        spread_lanes(bc_ref, next_scr, k + 1, slots, steps)
        ats, ds, us, ys = [], [], [], []
        for j in range(PAIR):
            at = pl.ds(pl.multiple_of((k * PAIR + j) * slots, slots), slots)
            ats.append(at)
            ds.append(delta_scr[at, :])
            us.append(u_scr[at, :])
            ys.append(None)
        for n in range(states):
            rate = rate_scr[n]
            h = h_scr[n]
            for j in range(PAIR):
                h = jnp.exp2(ds[j] * rate) * h + us[j] * widen(bcb_scr[j, n], width)
                term = h * widen(bcb_scr[j, states + n], width)
                ys[j] = term if n == 0 else ys[j] + term
            h_scr[n] = h
        for j in range(PAIR):
            y_ref[ats[j], :] = ys[j]

    def steps_twice(k, carry):
        step(2 * k, even_scr, odd_scr)
        step(2 * k + 1, odd_scr, even_scr)
        return carry

    lax.fori_loop(0, steps // PAIR // 2, steps_twice, 0)
    y = y_ref[...] + misc_scr[SKIP : SKIP + 1, :] * inp_ref[...].astype(F32)
    y_ref[...] = y
    gate = gate_ref[...]
    gated = (y * (gate * sigmoid(gate))).astype(BF16)
    br_ref[...] = dot(gated, ow_ref[...]).astype(br_ref.dtype).reshape(br_ref.shape)


def lane_sums(parts):
    lane = lax.broadcasted_iota(jnp.int32, parts[0].shape, 1)
    bit = 1
    while len(parts) > 1:
        low = (lane & bit) == 0
        merged = []
        for j in range(0, len(parts), 2):
            kept = jnp.where(low, parts[j], parts[j + 1])
            moved = jnp.where(low, parts[j + 1], parts[j])
            merged.append(kept + pltpu.roll(moved, bit, 1))
        parts = merged
        bit *= 2
    total = parts[0]
    while bit < total.shape[1]:
        total = total + pltpu.roll(total, bit, 1)
        bit *= 2
    return total


def back_kernel(
    gb_ref, dtl_ref, bc_ref, inp_ref, gate_ref, y_ref, ck_ref, dtw_ref, misc_ref, ow_ref,
    gis_ref, ggate_ref, gproj_ref, gout_ref, gmisc_ref,
    lam_scr, dacc_scr, sacc_scr, bacc_scr, rate_scr, delta_scr, u_scr, gy_scr, gu_scr, gd_scr, h_scr, a_scr, gbt_scr,
    even_scr, odd_scr, sums_scr, h_now, gbc_ref, misc_scr, back_scr, gout_scr, *, slots, length
):
    rows, width = inp_ref.shape
    steps = rows // slots
    states = lam_scr.shape[0]
    rank = dtl_ref.shape[1]
    step_id = pl.program_id(0)

    @pl.when(step_id == 0)
    def _():
        lam_scr[...] = jnp.zeros_like(lam_scr)
        dacc_scr[...] = jnp.zeros_like(dacc_scr)
        sacc_scr[...] = jnp.zeros_like(sacc_scr)
        bacc_scr[...] = jnp.zeros_like(bacc_scr)
        gout_scr[...] = jnp.zeros_like(gout_scr)
        gmisc_ref[...] = jnp.zeros_like(gmisc_ref)
        misc_scr[...] = jnp.transpose(misc_ref[...].astype(F32))
        for n in range(states):
            rate_scr[n] = jnp.broadcast_to(-jnp.exp(misc_scr[DECAY + n : DECAY + n + 1, :]) * LOG2E, (slots, width))

    gb = gb_ref[...].reshape(rows, gb_ref.shape[-1])
    gate = gate_ref[...]
    sig = sigmoid(gate)
    silu = gate * sig
    y = y_ref[...]
    inp = inp_ref[...].astype(F32)
    g_gated = dot(gb, ow_ref[...], ((1,), (1,)))
    g_y = g_gated * silu
    gy_scr[...] = g_y
    ggate_ref[...] = (g_gated * y * (sig * (1.0 + gate * (1.0 - sig)))).astype(BF16)
    gout_scr[...] += dot((y * silu).astype(BF16), gb, ((0,), (0,)))
    sacc_scr[...] += jnp.sum((g_y * inp).reshape(steps, slots, width), axis=0)
    z = dot(dtl_ref[...], dtw_ref[...], ((1,), (1,))) + misc_scr[DT_BIAS : DT_BIAS + 1, :]
    delta = softplus(z)
    delta_scr[...] = delta
    u_scr[...] = delta * inp

    last = steps // PAIR - 1
    spread_lanes(bc_ref, even_scr, 0, slots, steps)
    h_now[...] = ck_ref[0]

    def replay(k, bcb_scr, next_scr):
        spread_lanes(bc_ref, next_scr, k + 1, slots, steps)
        ds, us, gys = [], [], []
        for j in range(PAIR):
            at = pl.ds(pl.multiple_of((k * PAIR + j) * slots, slots), slots)
            ds.append(delta_scr[at, :])
            us.append(u_scr[at, :])
            gys.append(gy_scr[at, :])
        for n in range(states):
            rate = rate_scr[n]
            h = h_now[n]
            for j in range(PAIR):
                t = k * PAIR + j
                h_scr[t, n] = h
                decay = jnp.exp2(ds[j] * rate)
                a_scr[t, n] = decay
                h = decay * h + us[j] * widen(bcb_scr[j, n], width)
                gbt_scr[states + n, pl.ds(pl.multiple_of(t * slots, slots), slots), :] = narrow(h * gys[j])
            h_now[n] = h

    def replay_twice(k, carry):
        replay(2 * k, even_scr, odd_scr)
        replay(2 * k + 1, odd_scr, even_scr)
        return carry

    lax.fori_loop(0, steps // PAIR // 2, replay_twice, 0)
    spread_lanes(bc_ref, even_scr, last, slots, steps)

    def reverse(k, bcb_scr, next_scr):
        spread_lanes(bc_ref, next_scr, jnp.maximum(k - 1, 0), slots, steps)
        ats, ds, us, gys, gus, gds, ts = [], [], [], [], [], [], []
        for j in range(PAIR):
            t = k * PAIR + j
            at = pl.ds(pl.multiple_of(t * slots, slots), slots)
            ts.append(t)
            ats.append(at)
            ds.append(delta_scr[at, :])
            us.append(u_scr[at, :])
            gys.append(gy_scr[at, :])
            gus.append(None)
            gds.append(None)
        for n in range(states):
            rate = rate_scr[n]
            carried = lam_scr[n]
            total = dacc_scr[n]
            for j in reversed(range(PAIR)):
                t = ts[j]
                lam = carried + gys[j] * widen(bcb_scr[j, states + n], width)
                term = lam * widen(bcb_scr[j, n], width)
                gus[j] = term if n == 0 else gus[j] + term
                gbt_scr[n, ats[j], :] = narrow(lam * us[j])
                carried = a_scr[t, n] * lam
                q = carried * h_scr[t, n]
                term = q * rate
                gds[j] = term if n == 0 else gds[j] + term
                total = total + q * ds[j]
            lam_scr[n] = carried
            dacc_scr[n] = total
        for j in range(PAIR):
            gu_scr[ats[j], :] = gus[j]
            gd_scr[ats[j], :] = gds[j]

    def reverse_twice(i, carry):
        k = last - 2 * i
        reverse(k, even_scr, odd_scr)
        reverse(k - 1, odd_scr, even_scr)
        return carry

    lax.fori_loop(0, steps // PAIR // 2, reverse_twice, 0)

    def reduce_lanes(k, carry):
        for j in range(LANES):
            n = k * LANES + j
            sums_scr[pl.ds(n, 1), :] = jnp.sum(jnp.transpose(gbt_scr[n]), axis=0, keepdims=True)
        return carry

    lax.fori_loop(0, 2 * states // LANES, reduce_lanes, 0)
    gbc_ref[...] = jnp.transpose(sums_scr[...])
    gu = gu_scr[...]
    gis_ref[...] = gu * delta_scr[...] + misc_scr[SKIP : SKIP + 1, :] * gy_scr[...]
    g_pre = (gd_scr[...] * (1.0 / LOG2E) + gu * inp) * sigmoid(z)
    bacc_scr[...] += jnp.sum(g_pre.reshape(steps, slots, width), axis=0)
    g_low = g_pre.astype(BF16)
    gmisc_ref[:, :rank] += dot(g_low, dtl_ref[...], ((0,), (0,)))
    pack_rows(gproj_ref, dot(g_low, dtw_ref[...]), gbc_ref[...], length)

    @pl.when(step_id == pl.num_programs(0) - 1)
    def _():
        back_scr[...] = jnp.zeros_like(back_scr)
        for n in range(states):
            rate = -jnp.exp(misc_scr[DECAY + n : DECAY + n + 1, :])
            back_scr[DECAY + n : DECAY + n + 1, :] = jnp.sum(dacc_scr[n], axis=0, keepdims=True) * rate
        back_scr[SKIP : SKIP + 1, :] = jnp.sum(sacc_scr[...], axis=0, keepdims=True)
        back_scr[DT_BIAS : DT_BIAS + 1, :] = jnp.sum(bacc_scr[...], axis=0, keepdims=True)
        gmisc_ref[:, rank:] = jnp.transpose(back_scr[...])
        gout_ref[...] = gout_scr[...].astype(gout_ref.dtype)


def remote(src, dst, send, recv, where):
    return pltpu.make_async_remote_copy(
        src_ref=src, dst_ref=dst, send_sem=send, recv_sem=recv, device_id=where, device_id_type=pl.DeviceIdType.MESH
    )


def gather_kernel(
    tok_ref, cot_ref, win_ref, gain_ref, pk_ref, x_ref, c_ref, w_ref, g_ref, p_ref,
    tok_buf, cot_buf, win_buf, gain_buf, pk_buf, local_sem,
    tdp_send, tdp_recv, cdp_send, cdp_recv, up_send, up_recv, down_send, down_recv, core_send, core_recv,
    w1_send, w1_recv, w2_send, w2_recv, g1_send, g1_recv, g2_send, g2_recv, p_send, p_recv, *, n_dp, n_f
):
    d = lax.axis_index("dp")
    f = lax.axis_index("fsdp")
    n_z = n_f // 2
    z = f // 2
    core = f % 2
    partner = z * 2 + (1 - core)

    barrier = pltpu.get_barrier_semaphore()
    for k in range(1, n_f):
        pl.semaphore_signal(barrier, inc=1, device_id=(d, (f + k) % n_f), device_id_type=pl.DeviceIdType.MESH)
    for k in range(1, n_dp):
        pl.semaphore_signal(barrier, inc=1, device_id=((d + k) % n_dp, f), device_id_type=pl.DeviceIdType.MESH)
    pl.semaphore_wait(barrier, n_f + n_dp - 2)

    loads = (
        pltpu.make_async_copy(tok_ref.at[d], tok_buf, local_sem.at[0]),
        pltpu.make_async_copy(win_ref.at[f], win_buf, local_sem.at[1]),
        pltpu.make_async_copy(gain_ref, gain_buf, local_sem.at[2]),
        pltpu.make_async_copy(pk_ref, pk_buf, local_sem.at[3]),
        pltpu.make_async_copy(cot_ref.at[d], cot_buf, local_sem.at[8]),
    )
    stores = (
        pltpu.make_async_copy(tok_buf, x_ref.at[d, f], local_sem.at[4]),
        pltpu.make_async_copy(win_buf, w_ref.at[d, f], local_sem.at[5]),
        pltpu.make_async_copy(gain_buf, g_ref.at[d, f], local_sem.at[6]),
        pltpu.make_async_copy(pk_buf, p_ref.at[d], local_sem.at[7]),
        pltpu.make_async_copy(cot_buf, c_ref.at[d], local_sem.at[9]),
    )
    for load in loads:
        load.start()

    def tok_dp(k):
        to = (d + k) % n_dp
        return remote(tok_ref.at[to], x_ref.at[d, f], tdp_send.at[k], tdp_recv.at[k], (to, f))

    def tok_dp_arrival(k):
        src = (d - k + n_dp) % n_dp
        return remote(tok_ref.at[d], x_ref.at[src, f], tdp_send.at[k], tdp_recv.at[k], (src, f))

    def cot_dp(k):
        to = (d + k) % n_dp
        return remote(cot_ref.at[to], c_ref.at[d], cdp_send.at[k], cdp_recv.at[k], (to, f))

    def cot_dp_arrival(k):
        src = (d - k + n_dp) % n_dp
        return remote(cot_ref.at[d], c_ref.at[src], cdp_send.at[k], cdp_recv.at[k], (src, f))

    def w1(k):
        to = (f + k) % n_f
        return remote(win_ref.at[to], w_ref.at[d, f], w1_send.at[k], w1_recv.at[k], (d, to))

    def w1_arrival(k):
        src = (f - k + n_f) % n_f
        return remote(win_ref.at[f], w_ref.at[d, src], w1_send.at[k], w1_recv.at[k], (d, src))

    def g1(k):
        to = (f + k) % n_f
        return remote(gain_ref, g_ref.at[d, f], g1_send.at[k], g1_recv.at[k], (d, to))

    def g1_arrival(k):
        src = (f - k + n_f) % n_f
        return remote(gain_ref, g_ref.at[d, src], g1_send.at[k], g1_recv.at[k], (d, src))

    def w2(k):
        to = (d + k) % n_dp
        return remote(w_ref.at[d], w_ref.at[d], w2_send.at[k], w2_recv.at[k], (to, f))

    def w2_arrival(k):
        src = (d - k + n_dp) % n_dp
        return remote(w_ref.at[src], w_ref.at[src], w2_send.at[k], w2_recv.at[k], (src, f))

    def g2(k):
        to = (d + k) % n_dp
        return remote(g_ref.at[d], g_ref.at[d], g2_send.at[k], g2_recv.at[k], (to, f))

    def g2_arrival(k):
        src = (d - k + n_dp) % n_dp
        return remote(g_ref.at[src], g_ref.at[src], g2_send.at[k], g2_recv.at[k], (src, f))

    def pk(k):
        to = (d + k) % n_dp
        return remote(pk_ref, p_ref.at[d], p_send.at[k], p_recv.at[k], (to, f))

    def pk_arrival(k):
        src = (d - k + n_dp) % n_dp
        return remote(pk_ref, p_ref.at[src], p_send.at[k], p_recv.at[k], (src, f))

    def block(j, origin, side):
        at = (d - j + n_dp) % n_dp
        return x_ref.at[at, origin * 2 + side]

    def up(j, origin, src=None):
        ref = block(j, origin, core)
        return remote(ref if src is None else src, ref, up_send.at[origin, j], up_recv.at[origin, j], (d, f + 2))

    def down(j, origin, src=None):
        ref = block(j, origin, core)
        return remote(ref if src is None else src, ref, down_send.at[origin, j], down_recv.at[origin, j], (d, f - 2))

    def across(j, origin, src=None):
        ref = block(j, origin, core)
        return remote(
            ref if src is None else src, ref, core_send.at[origin, j], core_recv.at[origin, j], (d, partner)
        )

    def across_arrival(j, origin):
        ref = block(j, origin, 1 - core)
        return remote(ref, ref, core_send.at[origin, j], core_recv.at[origin, j], (d, partner))

    def launch(j, src=None):
        @pl.when(z < n_z - 1)
        def _():
            up(j, z, src).start()

        @pl.when(z > 0)
        def _():
            down(j, z, src).start()

        across(j, z, src).start()

    for k in range(1, n_f):
        w1(k).start()
    for k in range(1, n_dp):
        tok_dp(k).start()
    launch(0, tok_ref.at[d])
    for k in range(1, n_f):
        g1(k).start()
    for k in range(1, n_dp):
        pk(k).start()
    for k in range(1, n_dp):
        cot_dp(k).start()
    for load, store in zip(loads, stores):
        load.wait()
        store.start()
    for k in range(1, n_dp):
        tok_dp_arrival(k).wait_recv()
        launch(k)
    for store in stores:
        store.wait()
    for k in range(1, n_f):
        w1_arrival(k).wait_recv()
        g1_arrival(k).wait_recv()
    for k in range(1, n_dp):
        w2(k).start()
        g2(k).start()
    for far in range(1, n_z):
        for j in range(n_dp):

            @pl.when(z >= far)
            def _():
                origin = z - far
                up(j, origin).wait_recv()

                @pl.when(z < n_z - 1)
                def _():
                    up(j, origin).start()

                across(j, origin).start()

            @pl.when(z + far < n_z)
            def _():
                origin = z + far
                down(j, origin).wait_recv()

                @pl.when(z > 0)
                def _():
                    down(j, origin).start()

                across(j, origin).start()

    for origin in range(n_z):
        for j in range(n_dp):
            across_arrival(j, origin).wait_recv()
            across(j, origin).wait_send()
    for origin in range(n_z):
        for j in range(n_dp):

            @pl.when((origin <= z) & (z < n_z - 1))
            def _():
                up(j, origin).wait_send()

            @pl.when((origin >= z) & (z > 0))
            def _():
                down(j, origin).wait_send()

    for k in range(1, n_dp):
        pk_arrival(k).wait_recv()
        cot_dp_arrival(k).wait_recv()
        cot_dp(k).wait_send()
        w2_arrival(k).wait_recv()
        g2_arrival(k).wait_recv()
        tok_dp(k).wait_send()
        w2(k).wait_send()
        g2(k).wait_send()
        pk(k).wait_send()
    for k in range(1, n_f):
        w1(k).wait_send()
        g1(k).wait_send()


def pack_rows(out_ref, main, rest, chunk):
    part = chunk // 4
    for q in range(main.shape[0] // chunk):
        out_ref[q, 0:chunk, :] = main[q * chunk : (q + 1) * chunk, :]
        for j in range(4):
            first = q * chunk + j * part
            out_ref[q, chunk : chunk + part, j * 32 : (j + 1) * 32] = rest[first : first + part, :]


def combine_kernel(
    part_ref, main_ref, rest_ref, one, sums, two, tops, rests,
    one_send, one_recv, two_send, two_recv, top_send, top_recv, rest_send, rest_recv,
    ctop_send, ctop_recv, crest_send, crest_recv, *, n_dp, n_f
):
    d = lax.axis_index("dp")
    f = lax.axis_index("fsdp")
    n_z = n_f // 2
    z = f // 2
    core = f % 2
    other = 1 - core
    partner = z * 2 + other
    chunk = tops.shape[2]

    barrier = pltpu.get_barrier_semaphore()
    pl.semaphore_signal(barrier, inc=1, device_id=(d, partner), device_id_type=pl.DeviceIdType.MESH)
    for k in range(1, n_z):
        pl.semaphore_signal(
            barrier, inc=1, device_id=(d, (z + k) % n_z * 2 + core), device_id_type=pl.DeviceIdType.MESH
        )
    pl.semaphore_wait(barrier, n_z)

    def first(k):
        to = (z + k) % n_z
        return remote(part_ref.at[to, other], one.at[to], one_send.at[k], one_recv.at[k], (d, partner))

    def second(k):
        to = (z + k) % n_z
        return remote(sums.at[to], two.at[k], two_send.at[k], two_recv.at[k], (d, to * 2 + core))

    def third(k):
        to = ((z + k) % n_z * 2 + core,)
        return (
            remote(tops.at[z, core], tops.at[z, core], top_send.at[k], top_recv.at[k], (d,) + to),
            remote(rests.at[z, core], rests.at[z, core], rest_send.at[k], rest_recv.at[k], (d,) + to),
        )

    def third_arrival(k):
        src = (z - k + n_z) % n_z
        to = (src * 2 + core,)
        return (
            remote(tops.at[src, core], tops.at[src, core], top_send.at[k], top_recv.at[k], (d,) + to),
            remote(rests.at[src, core], rests.at[src, core], rest_send.at[k], rest_recv.at[k], (d,) + to),
        )

    def fourth(k, side):
        src = (z - k + n_z) % n_z
        return (
            remote(tops.at[src, side], tops.at[src, side], ctop_send.at[k], ctop_recv.at[k], (d, partner)),
            remote(rests.at[src, side], rests.at[src, side], crest_send.at[k], crest_recv.at[k], (d, partner)),
        )

    order = list(range(1, n_z)) + [0]
    for k in order:
        first(k).start()
    for k in order:
        to = (z + k) % n_z
        first(k).wait_recv()
        sums[to] = (part_ref[to, core] + one[to]).astype(sums.dtype)
        if k:
            second(k).start()
    total = part_ref[z, core] + one[z]
    for k in range(1, n_z):
        second(k).wait_recv()
        total = total + two[k].astype(F32)
    tops[z, core] = total[0:chunk, :].astype(tops.dtype)
    rests[z, core] = total[chunk:, :].astype(rests.dtype)
    for k in range(1, n_z):
        for copy in third(k):
            copy.start()
    for copy in fourth(0, core):
        copy.start()
    for k in range(1, n_z):
        for copy in third_arrival(k):
            copy.wait_recv()
        for copy in fourth(k, core):
            copy.start()
    for k in range(n_z):
        for copy in fourth(k, other):
            copy.wait_recv()
    part = chunk // 4
    for a in range(n_z):
        for b in range(2):
            at = (a * 2 + b) * chunk
            main_ref[at : at + chunk, :] = tops[a, b]
            rest = rests[a, b]
            for j in range(4):
                rest_ref[at + j * part : at + (j + 1) * part, :] = rest[:, j * 32 : (j + 1) * 32]
    for k in range(n_z):
        first(k).wait_send()
        for copy in fourth(k, core):
            copy.wait_send()
        if k:
            second(k).wait_send()
            for copy in third(k):
                copy.wait_send()


def finish_kernel(
    gdtl_ref, gbc_ref, inp_ref, gis_ref, ggate_ref, inner_ref, before_ref, x_ref, gain_ref, win_ref, xw_ref, misc_ref,
    gout_ref, gback_ref, out_ref, gin_out, gout_out, gback_out, gtail_out, gg_out,
    misc_scr, tail_scr, gin_scr, gsel_scr, grest_scr, ggain_scr, pad_scr, gpad_scr, wacc_scr, cacc_scr,
    mine, theirs, passed, gin_low, gin_got, gin_sum, gin_all, gout_got, gback_got, gtail_low, gtail_got,
    gg_low, gg_got, gg_sum, gg_all, local_sem,
    one_send, one_recv, up_send, up_recv, down_send, down_recv, dp_send, dp_recv,
    w_send, w_recv, o_send, o_recv, b_send, b_recv, t_send, t_recv, g_send, g_recv,
    w2_send, w2_recv, g2_send, g2_recv, *, slots, n_dp, n_f
):
    d = lax.axis_index("dp")
    f = lax.axis_index("fsdp")
    n_z = n_f // 2
    z = f // 2
    core = f % 2
    other = 1 - core
    partner = z * 2 + other
    rows, width = inp_ref.shape
    steps = rows // slots
    halo = 3 * slots
    i = pl.program_id(0)
    blocks = mine.shape[0] * mine.shape[1] * mine.shape[2] // rows
    last = blocks - 1
    tile = mine.shape[2]
    held = rows // tile
    per = n_f // held
    pairs = held // 2
    rank = gdtl_ref.shape[1]
    d_rows, inner_rows = gin_out.shape[0], gout_out.shape[0]

    def place(q):
        return (last - q) // per, (last - q) % per * pairs

    def one(to, j):
        return remote(
            mine.at[to * 2 + other, j], theirs.at[to, j], one_send.at[to, j], one_recv.at[to, j], (d, partner)
        )

    def up(to, j):
        return remote(
            mine.at[to * 2 + core, j], passed.at[to + 1, j], up_send.at[to, j], up_recv.at[to, j], (d, f + 2)
        )

    def down(to, j):
        return remote(
            mine.at[to * 2 + core, j], passed.at[to, j], down_send.at[to, j], down_recv.at[to, j], (d, f - 2)
        )

    def dp(k):
        to = (d + k) % n_dp
        return remote(mine.at[f, to], out_ref.at[d], dp_send.at[k], dp_recv.at[k], (to, f))

    def dp_arrival(k):
        src = (d - k + n_dp) % n_dp
        return remote(mine.at[f, src], out_ref.at[src], dp_send.at[k], dp_recv.at[k], (src, f))

    def over_dp(src, dst, send, recv):
        return [
            remote(src.at[(d + k) % n_dp], dst.at[k], send.at[k], recv.at[k], ((d + k) % n_dp, f))
            for k in range(1, n_dp)
        ]

    def over_f(src, dst, send, recv, k):
        to = (f + k) % n_f
        return remote(src.at[to], dst.at[f], send.at[k], recv.at[k], (d, to))

    def over_f_arrival(src, dst, send, recv, k):
        to = (f - k + n_f) % n_f
        return remote(src.at[to], dst.at[to], send.at[k], recv.at[k], (d, to))

    outs = lambda: over_dp(gout_ref, gout_got, o_send, o_recv)
    backs = lambda: over_dp(gback_ref, gback_got, b_send, b_recv)
    ins = lambda: over_dp(gin_low, gin_got, w_send, w_recv)
    tails = lambda: over_dp(gtail_low, gtail_got, t_send, t_recv)
    gains = lambda: over_dp(gg_low, gg_got, g_send, g_recv)
    own_out = pltpu.make_async_copy(gout_ref.at[d], gout_got.at[0], local_sem.at[0])
    own_back = pltpu.make_async_copy(gback_ref.at[d], gback_got.at[0], local_sem.at[1])
    put = pltpu.make_async_copy(mine.at[f, d], out_ref.at[d], local_sem.at[2])

    def send_halves(q):
        j, first = place(q)
        for a in range(pairs):
            one(first + a, j).start()

    def pair(to, j):
        one(to, j).wait_recv()
        return mine[to * 2 + core, j].astype(F32) + theirs[to, j].astype(F32)

    def hops(step):
        q_up = step - 1 - LAG * z
        q_down = step - 1 - LAG * (n_z - 1 - z)
        q_end = step - 1 - LAG * jnp.maximum(z, n_z - 1 - z)

        @pl.when((q_up >= 0) & (q_up < blocks))
        def _():
            j, first = place(q_up)
            for a in range(pairs):
                to = first + a

                @pl.when(to > z)
                def _():
                    mine[to * 2 + core, j] = pair(to, j).astype(mine.dtype)

                    @pl.when(z > 0)
                    def _():
                        up(to, j).wait_recv()
                        mine[to * 2 + core, j] = (
                            mine[to * 2 + core, j].astype(F32) + passed[to + 1, j].astype(F32)
                        ).astype(mine.dtype)

            for a in range(pairs):

                @pl.when(first + a > z)
                def _():
                    up(first + a, j).start()

        @pl.when((q_down >= 0) & (q_down < blocks))
        def _():
            j, first = place(q_down)
            for a in range(pairs):
                to = first + a

                @pl.when(to < z)
                def _():
                    mine[to * 2 + core, j] = pair(to, j).astype(mine.dtype)

                    @pl.when(z < n_z - 1)
                    def _():
                        down(to, j).wait_recv()
                        mine[to * 2 + core, j] = (
                            mine[to * 2 + core, j].astype(F32) + passed[to, j].astype(F32)
                        ).astype(mine.dtype)

            for a in range(pairs):

                @pl.when(first + a < z)
                def _():
                    down(first + a, j).start()

        @pl.when((q_end >= 0) & (q_end < blocks))
        def _():
            j, first = place(q_end)

            @pl.when((z >= first) & (z < first + pairs))
            def _():
                mine[f, j] = pair(z, j).astype(mine.dtype)

                @pl.when(z > 0)
                def _():
                    up(z, j).wait_recv()
                    mine[f, j] = (mine[f, j].astype(F32) + passed[z + 1, j].astype(F32)).astype(mine.dtype)

                @pl.when(z < n_z - 1)
                def _():
                    down(z, j).wait_recv()
                    mine[f, j] = (mine[f, j].astype(F32) + passed[z, j].astype(F32)).astype(mine.dtype)

                for k in range(n_dp):

                    @pl.when(j == (d + k) % n_dp)
                    def _():
                        if k:
                            dp(k).start()
                        else:
                            put.start()

    @pl.when(i == 0)
    def _():
        barrier = pltpu.get_barrier_semaphore()
        for k in range(1, n_f):
            pl.semaphore_signal(barrier, inc=1, device_id=(d, (f + k) % n_f), device_id_type=pl.DeviceIdType.MESH)
        for k in range(1, n_dp):
            pl.semaphore_signal(barrier, inc=1, device_id=((d + k) % n_dp, f), device_id_type=pl.DeviceIdType.MESH)
        pl.semaphore_wait(barrier, n_f + n_dp - 2)
        for copy in outs() + backs():
            copy.start()
        own_out.start()
        own_back.start()
        gpad_scr[rows : rows + halo, :] = jnp.zeros((halo, width), F32)
        wacc_scr[...] = jnp.zeros_like(wacc_scr)
        cacc_scr[...] = jnp.zeros_like(cacc_scr)
        gin_scr[...] = jnp.zeros_like(gin_scr)
        gsel_scr[...] = jnp.zeros_like(gsel_scr)
        grest_scr[...] = jnp.zeros_like(grest_scr)
        ggain_scr[...] = jnp.zeros_like(ggain_scr)
        misc_scr[...] = jnp.transpose(misc_ref[...].astype(F32))

    @pl.when(i > 0)
    def _():
        send_halves(i - 1)

    gdtl = gdtl_ref[...]
    gbc = gbc_ref[...]
    inp = inp_ref[...]
    gsel_scr[...] += dot(inp, gdtl, ((0,), (0,)))
    grest_scr[:, :DECAY] += dot(inp, gbc, ((0,), (0,)))
    g_inputs = (
        gis_ref[...]
        + dot(gdtl, xw_ref[...], ((1,), (1,)))
        + dot(gbc, misc_ref[:, :DECAY], ((1,), (1,)))
    )
    pad_scr[0:halo, :] = before_ref[slots : slots + halo, :] * (i < last).astype(F32)
    pad_scr[halo : halo + rows, :] = inner_ref[...]
    total = jnp.broadcast_to(misc_scr[CONV_BIAS : CONV_BIAS + 1, :], (rows, width))
    for tap in range(4):
        total = total + misc_scr[TAPS + tap : TAPS + tap + 1, :] * pad_scr[tap * slots : tap * slots + rows, :]
    sig = sigmoid(total)
    g_conv = g_inputs * (sig * (1.0 + total * (1.0 - sig)))
    gpad_scr[0:rows, :] = g_conv
    g_inner = jnp.zeros((rows, width), F32)
    for tap in range(4):
        back = (3 - tap) * slots
        g_inner = g_inner + misc_scr[TAPS + tap : TAPS + tap + 1, :] * gpad_scr[back : back + rows, :]
        wacc_scr[tap] += jnp.sum(
            (g_conv * pad_scr[tap * slots : tap * slots + rows, :]).reshape(steps, slots, width), axis=0
        )
    cacc_scr[...] += jnp.sum(g_conv.reshape(steps, slots, width), axis=0)
    gpad_scr[rows : rows + halo, :] = gpad_scr[0:halo, :]
    g_both = jnp.concatenate([g_inner.astype(BF16), ggate_ref[...]], axis=1)
    x = x_ref[...].astype(F32)
    scaled = x * lax.rsqrt(jnp.mean(x * x, axis=-1, keepdims=True) + EPSILON)
    gin_scr[...] += dot((scaled * gain_ref[...]).astype(BF16), g_both, ((0,), (0,)))
    g_normed = dot(g_both, win_ref[...], ((1,), (1,)))
    ggain_scr[...] += jnp.sum(g_normed * scaled, axis=0, keepdims=True)
    block, first = place(i)
    for a in range(held):
        mine[first * 2 + a, block] = g_normed[a * tile : (a + 1) * tile, :].astype(mine.dtype)
    hops(i)

    @pl.when(i == last)
    def _():
        for a in range(n_dp):
            for b in range(n_f):
                at = (a * n_f + b) * d_rows
                gin_low[a, b] = gin_scr[at : at + d_rows, :].astype(gin_low.dtype)
                gg_low[a, b] = jnp.zeros((8, 128), F32)
                gg_low[a, b, 0:1, 0:d_rows] = ggain_scr[:, at : at + d_rows]
        tail_scr[...] = jnp.zeros_like(tail_scr)
        for tap in range(4):
            tail_scr[TAPS + tap : TAPS + tap + 1, :] = jnp.sum(wacc_scr[tap], axis=0, keepdims=True)
        tail_scr[CONV_BIAS : CONV_BIAS + 1, :] = jnp.sum(cacc_scr[...], axis=0, keepdims=True)
        grest_scr[:, DECAY:] = jnp.transpose(tail_scr[...])[:, DECAY:]
        for a in range(n_dp):
            at = a * inner_rows
            gtail_low[a, :, :rank] = gsel_scr[at : at + inner_rows, :]
            gtail_low[a, :, rank:] = grest_scr[at : at + inner_rows, :]
        send_halves(last)
        hops(blocks)
        for copy in ins() + tails() + gains():
            copy.start()
        own_out.wait()
        own_back.wait()
        for copy in outs() + backs():
            copy.wait_recv()
        total = gout_got[0].astype(F32)
        for k in range(1, n_dp):
            total = total + gout_got[k].astype(F32)
        gout_out[...] = total
        total = gback_got[0]
        for k in range(1, n_dp):
            total = total + gback_got[k]
        gback_out[...] = total

        def drain(step, carry):
            hops(step)
            return carry

        lax.fori_loop(blocks + 1, blocks + 1 + LAG * (n_z - 1), drain, 0)

        for copy in ins() + tails() + gains():
            copy.wait_recv()

        def add(q, carry):
            total = gin_low[d, q].astype(F32)
            for k in range(1, n_dp):
                total = total + gin_got[k, q].astype(F32)
            gin_sum[q] = total.astype(gin_sum.dtype)
            total = gg_low[d, q]
            for k in range(1, n_dp):
                total = total + gg_got[k, q]
            gg_sum[q] = total
            return carry

        lax.fori_loop(0, n_f, add, 0)
        for k in range(1, n_f):
            over_f(gin_sum, gin_all, w2_send, w2_recv, k).start()
            over_f(gg_sum, gg_all, g2_send, g2_recv, k).start()
        gin_all[f] = gin_sum[f]
        gg_all[f] = gg_sum[f]
        total = gtail_low[d]
        for k in range(1, n_dp):
            total = total + gtail_got[k]
        gtail_out[...] = total
        for k in range(1, n_f):
            over_f_arrival(gin_sum, gin_all, w2_send, w2_recv, k).wait_recv()
            over_f_arrival(gg_sum, gg_all, g2_send, g2_recv, k).wait_recv()
        total = gg_all[0]
        for b in range(1, n_f):
            total = total + gg_all[b]
        gg_out[...] = total
        for b in range(n_f):
            for h in range(2):
                for a in range(n_dp):
                    to = (h * n_dp + a) * n_f * inner_rows + b * inner_rows
                    at = (h * n_dp + a) * inner_rows
                    gin_out[:, to : to + inner_rows] = gin_all[b, :, at : at + inner_rows].astype(F32)
        for k in range(1, n_dp):
            dp_arrival(k).wait_recv()
            dp(k).wait_send()
        put.wait()
        for copy in outs() + backs() + ins() + tails() + gains():
            copy.wait_send()
        for k in range(1, n_f):
            over_f(gin_sum, gin_all, w2_send, w2_recv, k).wait_send()
            over_f(gg_sum, gg_all, g2_send, g2_recv, k).wait_send()
        for to in range(n_z):
            for j in range(n_dp):
                one(to, j).wait_send()

                @pl.when(z < to)
                def _():
                    up(to, j).wait_send()

                @pl.when(z > to)
                def _():
                    down(to, j).wait_send()


def whole(shape):
    return pl.BlockSpec(shape, lambda i: (0,) * len(shape))


def cost(micros):
    return pl.CostEstimate(flops=int(micros * 1.15e9), bytes_accessed=1 << 20, transcendentals=0)


def params():
    return pltpu.CompilerParams(vmem_limit_bytes=VMEM_BYTES, dimension_semantics=("arbitrary",))


def body(
    tokens, cotangent, lengths, deal_order, norm_gain, in_weight, conv_weight, conv_bias,
    x_weight, dt_weight, dt_bias, decay_log, skip_gain, out_weight, *, n_dp, n_f
):
    seqs, own, model = tokens.shape
    slots = seqs // n_dp
    inner_rows, states = decay_log.shape
    rank = dt_weight.shape[1]
    width = inner_rows * n_dp
    length = own * n_dp * n_f
    d_rows = in_weight.shape[0]
    total_rows = length * slots
    group = lax.axis_index("dp")
    member = lax.axis_index("fsdp")

    low = lambda v: v.astype(BF16)
    slot_ids = jnp.arange(seqs, dtype=jnp.int32)
    seq_len = jnp.sum(jnp.where(deal_order[:, None] == slot_ids[None, :], lengths[:, None], 0), axis=0)
    own_pos = (group * n_f + member) * own + jnp.arange(own, dtype=jnp.int32)
    own_mask = own_pos[None, :] < seq_len[:, None]

    def by_group(v):
        return v.reshape(n_dp, slots, own, model).transpose(0, 2, 1, 3).reshape(n_dp, own * slots, model)

    def collect(v):
        v = lax.psum_scatter(v.reshape(total_rows, model), "fsdp", scatter_dimension=0, tiled=True)
        v = lax.all_to_all(v.reshape(n_dp, own, slots, model), "dp", 0, 0, tiled=True)
        return v.transpose(0, 2, 1, 3).reshape(seqs, own, model)

    masked = by_group(jnp.where(own_mask[:, :, None], cotangent, jnp.zeros_like(cotangent)))

    tok = by_group(tokens)
    win = low(in_weight).reshape(d_rows, 2, n_dp, n_f, inner_rows).transpose(3, 0, 1, 2, 4)
    win = win.reshape(n_f, d_rows, 2 * width)
    gain_tile = jnp.zeros((8, 128), F32).at[0, :d_rows].set(low(norm_gain).astype(F32))
    misc = jnp.concatenate(
        [x_weight[:, rank:], decay_log, conv_weight, conv_bias[:, None], dt_bias[:, None], skip_gain[:, None]], axis=1
    )
    misc = jnp.pad(misc, ((0, 0), (0, 128 - misc.shape[1])))
    packed = low(jnp.concatenate([out_weight, x_weight[:, :rank], misc, dt_weight], axis=1))
    n_z = n_f // 2
    dma = pltpu.SemaphoreType.DMA
    hbm = pl.BlockSpec(memory_space=pl.ANY)
    x, g_branch, win, gain, packed = pl.pallas_call(
        functools.partial(gather_kernel, n_dp=n_dp, n_f=n_f),
        in_specs=[hbm] * 5,
        out_specs=[hbm] * 5,
        out_shape=[
            jax.ShapeDtypeStruct((n_dp, n_f) + tok.shape[1:], BF16),
            jax.ShapeDtypeStruct(tok.shape, BF16),
            jax.ShapeDtypeStruct((n_dp, n_f) + win.shape[1:], BF16),
            jax.ShapeDtypeStruct((n_dp, n_f, 8, 128), F32),
            jax.ShapeDtypeStruct((n_dp,) + packed.shape, BF16),
        ],
        scratch_shapes=[
            pltpu.VMEM(tok.shape[1:], BF16), pltpu.VMEM(tok.shape[1:], BF16), pltpu.VMEM(win.shape[1:], BF16),
            pltpu.VMEM((8, 128), F32), pltpu.VMEM(packed.shape, BF16), dma((10,)),
            dma((n_dp,)), dma((n_dp,)), dma((n_dp,)), dma((n_dp,)),
        ]
        + [dma((n_z, n_dp))] * 6
        + [dma((n_f,)), dma((n_f,)), dma((n_dp,)), dma((n_dp,)), dma((n_f,)), dma((n_f,))]
        + [dma((n_dp,))] * 4,
        compiler_params=pltpu.CompilerParams(collective_id=1, has_side_effects=True),
        cost_estimate=cost(90),
        name="gather",
    )(tok, masked, win, gain_tile, packed)
    g_branch = lax.all_gather(g_branch, "fsdp", axis=0, tiled=False)
    x = x.reshape(total_rows, model)
    win = win.reshape(model, 2 * width)
    gain = gain[:, :, 0, :d_rows].reshape(1, model)
    packed = packed.reshape(width, -1)
    rows = STEPS * slots
    blocks = length // STEPS
    grid = (blocks,)
    row_spec = lambda cols: pl.BlockSpec((rows, cols), lambda i: (i, 0))
    rev_spec = lambda cols: pl.BlockSpec((rows, cols), lambda i: (blocks - 1 - i, 0))
    once = dict(pipeline_mode=pl.Buffered(1))
    ow_spec = pl.BlockSpec((width, model), lambda i: (0, 0), **once)
    xw_spec = pl.BlockSpec((width, 128), lambda i: (0, model // 128), **once)
    misc_spec = pl.BlockSpec((width, 128), lambda i: (0, model // 128 + 1), **once)
    dtw_spec = pl.BlockSpec((width, 128), lambda i: (0, model // 128 + 2), **once)
    win_spec = pl.BlockSpec((model, 2 * width), lambda i: (0, 0), **once)
    misc_shape = pltpu.VMEM((128, width), F32)
    like = jax.ShapeDtypeStruct
    held = STEPS // own
    per = n_f // held
    piece = (held, 1, own * slots, model)
    piece_spec = pl.BlockSpec(piece, lambda i: (i % per, i // per, 0, 0))
    rev_piece_spec = pl.BlockSpec(piece, lambda i: ((blocks - 1 - i) % per, (blocks - 1 - i) // per, 0, 0))
    pieces_shape = like((n_f, n_dp, own * slots, model), BF16)
    packed_rows = length + length // 4
    parts = rows // length
    part_spec = pl.BlockSpec((parts, packed_rows, 128), lambda i: (i, 0, 0))
    rev_part_spec = pl.BlockSpec((parts, packed_rows, 128), lambda i: (blocks - 1 - i, 0, 0))
    parts_shape = like((n_f, packed_rows, 128), F32)

    def combine(v, rest_type, number):
        vmem = pl.BlockSpec(memory_space=pltpu.VMEM)
        return pl.pallas_call(
            functools.partial(combine_kernel, n_dp=n_dp, n_f=n_f),
            in_specs=[vmem],
            out_specs=[vmem, vmem],
            out_shape=[like((total_rows, rank), BF16), like((total_rows, 2 * states), rest_type)],
            scratch_shapes=[
                pltpu.VMEM((n_z, packed_rows, 128), F32), pltpu.VMEM((n_z, packed_rows, 128), BF16),
                pltpu.VMEM((n_z, packed_rows, 128), BF16), pltpu.VMEM((n_z, 2, length, 128), BF16),
                pltpu.VMEM((n_z, 2, length // 4, 128), rest_type),
            ]
            + [dma((n_z,))] * 12,
            compiler_params=pltpu.CompilerParams(
                collective_id=number, has_side_effects=True, vmem_limit_bytes=VMEM_BYTES
            ),
            cost_estimate=cost(28),
        name="combine",
        )(v.reshape(n_z, 2, packed_rows, 128))

    inner, gate, inp, proj = pl.pallas_call(
        functools.partial(front_kernel, slots=slots, length=length),
        grid=grid,
        in_specs=[
            row_spec(model), whole((1, model)), win_spec, xw_spec, misc_spec,
        ],
        out_specs=[row_spec(width), row_spec(width), row_spec(width), part_spec],
        out_shape=[
            like((total_rows, width), F32), like((total_rows, width), F32), like((total_rows, width), BF16),
            parts_shape,
        ],
        scratch_shapes=[pltpu.VMEM((rows + 3 * slots, width), F32), misc_shape],
        compiler_params=params(),
        cost_estimate=cost(20),
        name="front",
    )(x, gain, win, packed, packed)

    dtl, bc = combine(proj, F32, 2)

    y, ck, branch = pl.pallas_call(
        functools.partial(mix_kernel, slots=slots),
        grid=grid,
        in_specs=[
            row_spec(rank), row_spec(2 * states), row_spec(width), row_spec(width), dtw_spec, misc_spec, ow_spec,
        ],
        out_specs=[
            row_spec(width), pl.BlockSpec((1, states, slots, width), lambda i: (i, 0, 0, 0)), piece_spec,
        ],
        out_shape=[
            like((total_rows, width), F32), like((blocks, states, slots, width), F32), pieces_shape,
        ],
        scratch_shapes=[
            pltpu.VMEM((states, slots, width), F32), pltpu.VMEM((rows, width), F32), pltpu.VMEM((rows, width), F32),
            pltpu.VMEM((states, slots, width), F32), pltpu.VMEM((PAIR, 2 * states, slots, 128), F32),
            pltpu.VMEM((PAIR, 2 * states, slots, 128), F32), misc_shape,
        ],
        compiler_params=params(),
        cost_estimate=cost(36),
        name="mix",
    )(dtl, bc, inp, gate, packed, packed, packed)

    gis, ggate, gproj, gout, gmisc = pl.pallas_call(
        functools.partial(back_kernel, slots=slots, length=length),
        grid=grid,
        in_specs=[
            rev_piece_spec, rev_spec(rank), rev_spec(2 * states), rev_spec(width), rev_spec(width), rev_spec(width),
            pl.BlockSpec((1, states, slots, width), lambda i: (blocks - 1 - i, 0, 0, 0)), dtw_spec, misc_spec, ow_spec,
        ],
        out_specs=[
            rev_spec(width), rev_spec(width), rev_part_spec, whole((width, model)), whole((width, 256)),
        ],
        out_shape=[
            like((total_rows, width), F32), like((total_rows, width), BF16), parts_shape,
            like((width, model), BF16), like((width, 256), F32),
        ],
        scratch_shapes=[
            pltpu.VMEM((states, slots, width), F32), pltpu.VMEM((states, slots, width), F32),
            pltpu.VMEM((slots, width), F32), pltpu.VMEM((slots, width), F32), pltpu.VMEM((states, slots, width), F32),
        ]
        + [pltpu.VMEM((rows, width), F32)] * 5
        + [
            pltpu.VMEM((STEPS, states, slots, width), F32), pltpu.VMEM((STEPS, states, slots, width), F32),
            pltpu.VMEM((2 * states, rows, 128), F32), pltpu.VMEM((PAIR, 2 * states, slots, 128), F32),
            pltpu.VMEM((PAIR, 2 * states, slots, 128), F32), pltpu.VMEM((2 * states, rows), F32),
            pltpu.VMEM((states, slots, width), F32), pltpu.VMEM((rows, 2 * states), F32), misc_shape, misc_shape,
            pltpu.VMEM((width, model), F32),
        ],
        compiler_params=params(),
        cost_estimate=cost(95),
        name="back",
    )(g_branch, dtl, bc, inp, gate, y, ck, packed, packed, packed)

    gdtl, gbc = combine(gproj, BF16, 3)

    branch = collect(branch)
    branch, gdtl = lax.optimization_barrier((branch, gdtl))
    tile = own * slots
    vmem = pltpu.VMEM
    g_normed, gin, gout, gback, gtail, ggain = pl.pallas_call(
        functools.partial(finish_kernel, slots=slots, n_dp=n_dp, n_f=n_f),
        grid=grid,
        in_specs=[
            rev_spec(rank), rev_spec(2 * states), rev_spec(width), rev_spec(width), rev_spec(width), rev_spec(width),
            pl.BlockSpec((4 * slots, width), lambda i: (jnp.maximum((blocks - 1 - i) * (STEPS // 4) - 1, 0), 0)),
            rev_spec(model), whole((1, model)), win_spec, xw_spec, misc_spec, hbm, hbm,
        ],
        out_specs=[
            hbm, whole((d_rows, 2 * width * n_f)), whole((inner_rows, model)), whole((inner_rows, 256)),
            whole((inner_rows, 256)), whole((8, 128)),
        ],
        out_shape=[
            like((n_dp, tile, model), BF16), like((d_rows, 2 * width * n_f), F32), like((inner_rows, model), F32),
            like((inner_rows, 256), F32), like((inner_rows, 256), F32), like((8, 128), F32),
        ],
        scratch_shapes=[
            misc_shape, misc_shape, vmem((model, 2 * width), F32), vmem((width, 128), F32), vmem((width, 128), F32),
            vmem((1, model), F32), vmem((rows + 3 * slots, width), F32), vmem((rows + 3 * slots, width), F32),
            vmem((4, slots, width), F32), vmem((slots, width), F32),
            vmem((n_f, n_dp, tile, model), BF16), vmem((n_z, n_dp, tile, model), BF16),
            vmem((n_z + 1, n_dp, tile, model), BF16),
            vmem((n_dp, n_f, d_rows, 2 * width), BF16), vmem((n_dp, n_f, d_rows, 2 * width), BF16),
            vmem((n_f, d_rows, 2 * width), BF16), vmem((n_f, d_rows, 2 * width), BF16),
            vmem((n_dp, inner_rows, model), BF16), vmem((n_dp, inner_rows, 256), F32),
            vmem((n_dp, inner_rows, 256), F32), vmem((n_dp, inner_rows, 256), F32),
            vmem((n_dp, n_f, 8, 128), F32), vmem((n_dp, n_f, 8, 128), F32), vmem((n_f, 8, 128), F32),
            vmem((n_f, 8, 128), F32), dma((3,)),
        ]
        + [dma((n_z, n_dp))] * 6
        + [dma((n_dp,))] * 12
        + [dma((n_f,))] * 4,
        compiler_params=pltpu.CompilerParams(
            collective_id=4, has_side_effects=True, vmem_limit_bytes=FULL_VMEM, dimension_semantics=("arbitrary",)
        ),
        cost_estimate=cost(105),
        name="finish",
    )(
        gdtl, gbc, inp, gis, ggate, inner, inner, x, gain, win, packed, packed,
        gout.reshape(n_dp, inner_rows, model), gmisc.reshape(n_dp, inner_rows, 256),
    )

    hidden = tokens.astype(F32)
    upstream = cotangent.astype(F32)
    output = (hidden + jnp.where(own_mask[:, :, None], branch.astype(F32), 0.0)).astype(BF16)
    g_normed = g_normed.reshape(n_dp, own, slots, model).transpose(0, 2, 1, 3).reshape(seqs, own, model).astype(F32)
    factor = lax.rsqrt(jnp.mean(hidden * hidden, axis=-1, keepdims=True) + EPSILON)
    weighted = gain * g_normed
    input_grad = (
        upstream + factor * weighted - hidden * factor**3 * jnp.mean(hidden * weighted, axis=-1, keepdims=True)
    ).astype(BF16)
    conv_bias_grad = gtail[:, rank + CONV_BIAS]
    x_grad = gtail[:, : rank + 2 * states]
    return (
        output, input_grad, ggain[0, :d_rows], gin, gtail[:, rank + TAPS : rank + TAPS + 4], conv_bias_grad, x_grad,
        gback[:, :rank], gback[:, rank + DT_BIAS], gback[:, rank + DECAY : rank + DECAY + states],
        gback[:, rank + SKIP], gout,
    )


def solution(mesh):
    rows1, rows2, pos = P(BOTH), P(BOTH, None), P(None, BOTH, None)
    return jax.shard_map(
        functools.partial(body, n_dp=mesh.shape["dp"], n_f=mesh.shape["fsdp"]),
        mesh=mesh,
        in_specs=(pos, pos, P(), P(), rows1, rows2, rows2, rows1, rows2, rows2, rows1, rows2, rows1, rows2),
        out_specs=(pos, pos, rows1, rows2, rows2, rows1, rows2, rows2, rows1, rows2, rows1, rows2),
        check_vma=False,
    )
```

time: 573 us -> 507 us (0.88); the launches traced: 571 us -> 499 us
  Pallas kernels: 488 us -> 436 us
  local copies, waits for them, and re-layouts: 44.3 us -> 26.8 us
  other arithmetic: 20.7 us -> 10.8 us
  waiting for transfers between devices: 0.08 us -> 6.66 us
    pallas_call x2, Pallas kernels: 88.2 us -> 62.1 us  [combine(): pl.pallas_call(functools.partial(combine_kernel, n_dp=n_dp, n_f=n_f), in_...]
    pallas_call x1, Pallas kernels: 104 us -> 92 us  [body(): pl.pallas_call(functools.partial(back_kernel, slots=slots, length=length)...]
    pallas_call x1, Pallas kernels: 42.8 us -> 35.2 us  [body(): pl.pallas_call(functools.partial(mix_kernel, slots=slots), grid=grid, in_...]
    pallas_call x2 -> x1, Pallas kernels: 128 us -> 121 us  [body(): pl.pallas_call(functools.partial(finish_kernel, slots=slots, n_dp=n_dp, n...]
    reduce_scatter x1, waiting for transfers between devices: 0.02 us -> 6.43 us  [collect(): lax.psum_scatter(v.reshape(total_rows, model), 'fsdp', scatter_dimension=...]
    slice x11 -> x7, local copies, waits for them, and re-layouts: 12.6 us -> 8.02 us  [the longest x1 1.61 us: body(): gback[:, rank + SKIP]]
  transfers between devices with their start and end apart: 4 -> 3, of which waited for: 0 -> 2; matrix products, arithmetic and copies ran while one was open for 6% -> 0% of each run, Pallas kernels for 61% -> 42%
where the time goes in v4:
time: 507 us; the launch traced here: 499 us
  Pallas kernels  436 us (86%)
  local copies, waits for them, and re-layouts  26.8 us (5%)
  between operations  14.4 us (3%)
  other arithmetic  10.8 us (2%)
  waiting for transfers between devices  6.66 us (1%)
    pallas_call x1, Pallas kernels, body(): pl.pallas_call(functools.partial(finish_kernel, slots=slots, n_dp=n_dp, n...  121 us
    pallas_call x1, Pallas kernels, body(): pl.pallas_call(functools.partial(gather_kernel, n_dp=n_dp, n_f=n_f), in_s...  105 us
    pallas_call x1, Pallas kernels, body(): pl.pallas_call(functools.partial(back_kernel, slots=slots, length=length)...  92 us
    pallas_call x2, Pallas kernels, combine(): pl.pallas_call(functools.partial(combine_kernel, n_dp=n_dp, n_f=n_f), in_...  62.1 us
    pallas_call x1, Pallas kernels, body(): pl.pallas_call(functools.partial(mix_kernel, slots=slots), grid=grid, in_...  35.2 us
    pallas_call x1, Pallas kernels, body(): pl.pallas_call(functools.partial(front_kernel, slots=slots, length=length...  20.5 us
  transfers between devices with their start and end apart: 3, of which 2 were waited for; matrix products, arithmetic and copies ran while one was open for 0% of the time, Pallas kernels for 42%

profile of v4, /device:TPU:0, one launch (start us, length us, event | category | flops | bytes accessed | tf_op | source)
XLA Modules:
  0.0 498.9 jit_solution(2757902405951506448)
XLA Ops:
  7.2 0.7 slice.63
  8.0 0.8 slice.62
  8.8 1.8 convert_bitcast_fusion.1
  11.4 1.5 reshape.167.win_ref
  14.5 1.3 convert.39
  16.6 2.5 copy_bitcast_fusion.1
  19.2 0.9 fusion.9.pk_ref
  20.1 105.2 %gather.1 = (bf16[4,8,64,2048]{3,2,1,0:T(8,128)(2,1)}, bf16[4,64,2048]{2,1,0:T(8,128)(2,1)}, bf16[4,8,64,1024]{3,2,1,0:T(8,128)(2,1)}, f32[4,8,8,128]{3,2,1,0:T(8,128)}, bf16[4,128,2432]{2,1,0:T(8,128)(2,1)}) custom-call(bf16[4,64,2048]{2,1,0:T(8,128)(2,1)} %get-tuple-element.141.tok_ref, bf16[4,64,2048]{2,1,0:T(8,128)(2,1)} %get-tuple-element.140.cot_ref, ...), custom_call_target="tpu_custom_call" | custom-call | flops 103499997184 | bytes 1048576 | tf_op jit(solution)/shard_map/gather/pallas_call | solution.py:1005
  125.5 1.0 fusion.10
  126.5 0.7 reshape_squeeze.3.gain_ref
  127.2 20.5 %front.1 = (f32[2048,512]{1,0:T(8,128)}, f32[2048,512]{1,0:T(8,128)}, bf16[2048,512]{1,0:T(8,128)(2,1)}, f32[8,320,128]{2,1,0:T(8,128)}) custom-call(bf16[2048,2048]{1,0:T(8,128)(2,1)} %bitcast.59, f32[1,2048]{1,0:T(1,128)} %reshape_squeeze.3.gain_ref, bf16[2048,1024]{1,0:T(8,128)(2,1)} %bitcast.61, bf16[512,2432]{1,0:T(8,128)(2,1)} %bitcast.63, ...), custom_call_target="tpu_custom_call" | custom-call | flops 23000000512 | bytes 1048576 | tf_op jit(solution)/shard_map/front/pallas_call | solution.py:1078
  147.7 37.4 %combine.2 = (bf16[2048,128]{1,0:T(8,128)(2,1)}, f32[2048,32]{1,0:T(8,128)}) custom-call(f32[4,2,320,128]{3,2,1,0:T(8,128)} %bitcast.75), custom_call_target="tpu_custom_call" | custom-call | flops 32199999488 | bytes 1048576 | tf_op jit(solution)/shard_map/combine/pallas_call | solution.py:1060
  185.1 35.2 %mix.1 = (f32[2048,512]{1,0:T(8,128)}, f32[8,16,8,512]{3,2,1,0:T(8,128)}, bf16[8,4,64,2048]{3,2,1,0:T(8,128)(2,1)}) custom-call(bf16[2048,128]{1,0:T(8,128)(2,1)} %get-tuple-element.58.dtl_ref, f32[2048,32]{1,0:T(8,128)} %get-tuple-element.59.bc_ref, bf16[2048,512]{1,0:T(8,128)(2,1)} %get-tuple-element.60.inp_ref, f32[2048,512]{1,0:T(8,128)} %get-tuple-element.61.gate_ref, ...), custom_call_target="tpu_custom_call" | custom-call | flops 41400000512 | bytes 1048576 | tf_op jit(solution)/shard_map/mix/pallas_call | solution.py:1097
  220.3 0.7 mul.50
  221.2 92.0 %back.1 = (f32[2048,512]{1,0:T(8,128)}, bf16[2048,512]{1,0:T(8,128)(2,1)}, f32[8,320,128]{2,1,0:T(8,128)}, bf16[512,2048]{1,0:T(8,128)(2,1)}, f32[512,256]{1,0:T(8,128)}) custom-call(bf16[8,4,64,2048]{3,2,1,0:T(8,128)(2,1)} %bitcast.58, bf16[2048,128]{1,0:T(8,128)(2,1)} %get-tuple-element.58.dtl_ref, f32[2048,32]{1,0:T(8,128)} %get-tuple-element.59.bc_ref, ...), custom_call_target="tpu_custom_call" | custom-call | flops 109250002944 | bytes 1048576 | tf_op jit(solution)/shard_map/back/pallas_call | solution.py:1119
  313.2 6.4 %reduce-scatter.2.cloned.1.call-done = bf16[256,2048]{1,0:T(8,128)(2,1)} async-done(((bf16[2048,2048]{1,0:T(8,128)(2,1)}), bf16[256,2048]{1,0:T(8,128)(2,1)}) %reduce-scatter.2.cloned.1.call-update) | async-done | bytes 1048592 | tf_op jit(solution)/shard_map/reduce_scatter | solution.py:987
  319.6 2.8 copy.74
  322.4 4.5 all-to-all-start
  326.9 24.7 %combine.3 = (bf16[2048,128]{1,0:T(8,128)(2,1)}, bf16[2048,32]{1,0:T(8,128)(2,1)}) custom-call(f32[4,2,320,128]{3,2,1,0:T(8,128)} %bitcast.74), custom_call_target="tpu_custom_call" | custom-call | flops 32199999488 | bytes 1048576 | tf_op jit(solution)/shard_map/combine/pallas_call | solution.py:1060
  351.6 120.6 %finish.1 = (bf16[4,64,2048]{2,1,0:T(8,128)(2,1)}, f32[64,8192]{1,0:T(8,128)}, f32[128,2048]{1,0:T(8,128)}, f32[128,256]{1,0:T(8,128)}, f32[128,256]{1,0:T(8,128)}, /*index=5*/f32[8,128]{1,0:T(8,128)}) custom-call(bf16[2048,128]{1,0:T(8,128)(2,1)} %get-tuple-element.69.gdtl_ref, bf16[2048,32]{1,0:T(8,128)(2,1)} %get-tuple-element.70.gbc_ref, ...), custom_call_target="tpu_custom_call" | custom-call | flops 120749998080 | bytes 1048576 | tf_op jit(solution)/shard_map/finish/pallas_call | solution.py:1156
  472.2 0.9 slice.55
  473.2 1.5 slice_reduce_fusion.2
  474.7 1.5 slice.58
  476.2 1.6 slice_reduce_fusion
  477.8 0.9 slice.60
  478.7 1.5 convert_bitcast_fusion
  480.2 1.2 copy.75
  482.0 1.2 slice_bitcast_fusion
  483.8 0.7 copy.77
  485.2 3.9 fusion.4
  489.2 1.3 copy.88
  491.1 1.0 copy.89
  (69 shorter events, 6.1 us)
Async XLA Ops:
  7.2 214.0 %all-gather.3.cloned.1.call-start = ((), (), s32[]{:S(2)}) async-start(), calls=%async_computation.3 | async-start | bytes 9437184 | tf_op jit(solution)/shard_map/all_gather | solution.py:1028
  10.8 2.1 copy-start.12
  10.8 2.8 copy-start.10
  10.9 2.9 copy-start.11
  10.9 3.1 copy-start.13
  10.9 3.2 copy-start.14
  10.9 3.3 copy-start.15
  10.9 3.5 copy-start.7
  11.3 4.5 copy-start.16
  11.3 4.5 copy-start.17
  11.4 4.6 copy-start.2
  12.9 3.7 copy-start
  16.0 0.6 copy-start.8
  125.3 194.3 %reduce-scatter.2.cloned.1.call-start = ((), (), s32[]{:S(2)}) async-start(), calls=%async_computation.2 | async-start | bytes 9437184 | tf_op jit(solution)/shard_map/reduce_scatter | solution.py:987
  322.4 29.2 %all-to-all-start = ((bf16[4,8,8,2048]{3,1,2,0:T(8,128)(2,1)}), bf16[4,8,8,2048]{3,1,2,0:T(8,128)(2,1)}, u32[]{:S(2)}, u32[]{:S(2)}) async-start(bf16[4,8,8,2048]{3,1,2,0:T(8,128)(2,1)} %copy.74), calls=%async_computation.1 | async-start | bytes 2097152 | tf_op jit(solution)/shard_map/all_to_all | solution.py:988
  480.2 1.3 copy-start.1
  480.2 1.3 copy-start.6
  481.4 2.4 copy-start.5
  481.4 3.8 copy-start.9
  485.2 4.0 copy-start.3
  489.2 2.0 copy-start.4
Sparse Core Ops, SparseCore 0:
  125.4 95.6 all-gather.2
  223.5 96.1 reduce-scatter.1

commit v5 on v4

--- a/solution.py
+++ b/solution.py
@@ -7,9 +7,10 @@
 from jax.sharding import PartitionSpec as P
 
 EPSILON = 1e-05
-STEPS = 32
+ROWS = 256
 PAIR = 2
 LAG = 4
+HOP = jnp.bfloat16
 LANES = 8
 TOGETHER = 8
 LOG2E = 1.4426950408889634
@@ -39,11 +40,46 @@
 
 
 def front_kernel(
-    x_ref, gain_ref, win_ref, xw_ref, misc_ref, inner_ref, gate_ref, inp_ref, proj_ref, pad_ref, misc_scr, *, slots, length
+    x_ref, gain_ref, win_ref, xw_ref, misc_ref, ow_ref, inner_ref, gate_ref, inp_ref, dtl_ref, bc_ref, owf_ref,
+    pad_ref, misc_scr, ow_buf, ow_send, ow_recv, ow_local, *scratch, slots, length, n_dp, n_f
 ):
+    d = lax.axis_index("dp")
+    f = lax.axis_index("fsdp")
+
+    def ow(k):
+        return remote(ow_ref, owf_ref.at[d], ow_send.at[k], ow_recv.at[k], ((d + k) % n_dp, f))
+
+    def ow_arrival(k):
+        src = (d - k + n_dp) % n_dp
+        return remote(ow_ref, owf_ref.at[src], ow_send.at[k], ow_recv.at[k], (src, f))
+
+    ow_get = pltpu.make_async_copy(ow_ref, ow_buf, ow_local.at[0])
+    ow_put = pltpu.make_async_copy(ow_buf, owf_ref.at[d], ow_local.at[1])
+    enter, send, relay, close = combiner(scratch, dtl_ref, bc_ref, n_f)
+    i = pl.program_id(0)
+    last = pl.num_programs(0) - 1
     rows = x_ref.shape[0]
     width = inner_ref.shape[1]
     halo = 3 * slots
+    parts = rows // length
+
+    @pl.when(i == 0)
+    def _():
+        enter([((d + k) % n_dp, f) for k in range(1, n_dp)])
+        for k in range(1, n_dp):
+            ow(k).start()
+        ow_get.start()
+
+    @pl.when(i == 1)
+    def _():
+        ow_get.wait()
+        ow_put.start()
+
+    @pl.when(i > 0)
+    def _():
+        for a in range(parts):
+            send((i - 1) * parts + a)
+
     normed = rms_normed(x_ref[...].astype(F32), gain_ref[...])
     both = dot(normed, win_ref[...])
     gate_ref[...] = both[:, width:]
@@ -61,8 +97,25 @@
         total = total + misc_scr[TAPS + tap : TAPS + tap + 1, :] * pad_ref[tap * slots : tap * slots + rows, :]
     inp = (total * sigmoid(total)).astype(BF16)
     inp_ref[...] = inp
-    pack_rows(proj_ref, dot(inp, xw_ref[...]), dot(inp, misc_ref[...])[:, :DECAY], length)
+    pack_rows(scratch[0], i * parts, dot(inp, xw_ref[...]), dot(inp, misc_ref[...])[:, :DECAY], length)
     pad_ref[0:halo, :] = pad_ref[rows : rows + halo, :]
+
+    @pl.when(i > 0)
+    def _():
+        for a in range(parts):
+            relay((i - 1) * parts + a)
+
+    @pl.when(i == last)
+    def _():
+        for a in range(parts):
+            send(i * parts + a)
+        for a in range(parts):
+            relay(i * parts + a)
+        close()
+        ow_put.wait()
+        for k in range(1, n_dp):
+            ow_arrival(k).wait_recv()
+            ow(k).wait_send()
 
 
 def spread_lanes(bc_ref, out_ref, k, slots, steps):
@@ -158,16 +211,124 @@
 
 
 def back_kernel(
-    gb_ref, dtl_ref, bc_ref, inp_ref, gate_ref, y_ref, ck_ref, dtw_ref, misc_ref, ow_ref,
-    gis_ref, ggate_ref, gproj_ref, gout_ref, gmisc_ref,
+    gb_ref, dtl_ref, bc_ref, inp_ref, gate_ref, y_ref, ck_ref, dtw_ref, misc_ref, ow_ref, br_ref,
+    gis_ref, ggate_ref, gdtl_ref, gbcs_ref, gout_ref, gmisc_ref, brr_ref,
     lam_scr, dacc_scr, sacc_scr, bacc_scr, rate_scr, delta_scr, u_scr, gy_scr, gu_scr, gd_scr, h_scr, a_scr, gbt_scr,
-    even_scr, odd_scr, sums_scr, h_now, gbc_ref, misc_scr, back_scr, gout_scr, *, slots, length
+    even_scr, odd_scr, sums_scr, h_now, gbc_ref, misc_scr, back_scr, gout_scr,
+    mine, theirs, passed, b_local, b_done, one_send, one_recv, up_send, up_recv, down_send, down_recv, *scratch,
+    slots, length, n_dp, n_f
 ):
+    enter, send, relay, close = combiner(scratch, gdtl_ref, gbcs_ref, n_f)
+    d = lax.axis_index("dp")
+    f = lax.axis_index("fsdp")
+    n_z = n_f // 2
+    z = f // 2
+    core = f % 2
+    other = 1 - core
+
+    def one(to, j):
+        return remote(
+            br_ref.at[to * 2 + other, j], theirs.at[to, j], one_send.at[to, j], one_recv.at[to, j], (d, z * 2 + other)
+        )
+
+    def up(to, j):
+        return remote(mine.at[to, j], passed.at[to + 1, j], up_send.at[to, j], up_recv.at[to, j], (d, f + 2))
+
+    def down(to, j):
+        return remote(mine.at[to, j], passed.at[to, j], down_send.at[to, j], down_recv.at[to, j], (d, f - 2))
+
+    def load(to, j):
+        return pltpu.make_async_copy(br_ref.at[to * 2 + core, j], mine.at[to, j], b_local.at[to, j])
+
+    done = pltpu.make_async_copy(mine.at[z], brr_ref, b_done.at[0])
+
+    def pair(to, j):
+        one(to, j).wait_recv()
+        load(to, j).wait()
+        mine[to, j] = (mine[to, j].astype(F32) + theirs[to, j].astype(F32)).astype(mine.dtype)
+
+    def take(to, j, slot):
+        mine[to, j] = (mine[to, j].astype(F32) + passed[slot, j].astype(F32)).astype(mine.dtype)
+
+    def hop(u):
+        above = z + n_z - 1 - u
+        below = u - (n_z - 1 - z)
+
+        @pl.when((above > z) & (above < n_z))
+        def _():
+            def block(j, carry):
+                pair(above, j)
+
+                @pl.when(z > 0)
+                def _():
+                    up(above, j).wait_recv()
+                    take(above, j, above + 1)
+
+                up(above, j).start()
+                return carry
+
+            lax.fori_loop(0, n_dp, block, 0)
+
+        @pl.when((below < z) & (below >= 0))
+        def _():
+            def block(j, carry):
+                pair(below, j)
+
+                @pl.when(z < n_z - 1)
+                def _():
+                    down(below, j).wait_recv()
+                    take(below, j, below)
+
+                down(below, j).start()
+                return carry
+
+            lax.fori_loop(0, n_dp, block, 0)
+
+    def settle():
+        def block(j, carry):
+            pair(z, j)
+
+            @pl.when(z > 0)
+            def _():
+                up(z, j).wait_recv()
+                take(z, j, z + 1)
+
+            @pl.when(z < n_z - 1)
+            def _():
+                down(z, j).wait_recv()
+                take(z, j, z)
+
+            return carry
+
+        lax.fori_loop(0, n_dp, block, 0)
+        done.start()
+
     rows, width = inp_ref.shape
     steps = rows // slots
     states = lam_scr.shape[0]
     rank = dtl_ref.shape[1]
     step_id = pl.program_id(0)
+    final = pl.num_programs(0) - 1
+    parts = rows // length
+
+    @pl.when(step_id == 0)
+    def _():
+        enter()
+        for to in range(n_z):
+            for j in range(n_dp):
+                one(to, j).start()
+                load(to, j).start()
+
+    for u in range(n_z - 1):
+
+        @pl.when(step_id == 1 + 2 * u)
+        def _():
+            hop(u)
+
+    @pl.when(step_id > 0)
+    def _():
+        for a in range(parts):
+            send((final - step_id + 1) * parts + a)
 
     @pl.when(step_id == 0)
     def _():
@@ -193,8 +354,8 @@
     ggate_ref[...] = (g_gated * y * (sig * (1.0 + gate * (1.0 - sig)))).astype(BF16)
     gout_scr[...] += dot((y * silu).astype(BF16), gb, ((0,), (0,)))
     sacc_scr[...] += jnp.sum((g_y * inp).reshape(steps, slots, width), axis=0)
-    z = dot(dtl_ref[...], dtw_ref[...], ((1,), (1,))) + misc_scr[DT_BIAS : DT_BIAS + 1, :]
-    delta = softplus(z)
+    pre = dot(dtl_ref[...], dtw_ref[...], ((1,), (1,))) + misc_scr[DT_BIAS : DT_BIAS + 1, :]
+    delta = softplus(pre)
     delta_scr[...] = delta
     u_scr[...] = delta * inp
 
@@ -282,11 +443,16 @@
     gbc_ref[...] = jnp.transpose(sums_scr[...])
     gu = gu_scr[...]
     gis_ref[...] = gu * delta_scr[...] + misc_scr[SKIP : SKIP + 1, :] * gy_scr[...]
-    g_pre = (gd_scr[...] * (1.0 / LOG2E) + gu * inp) * sigmoid(z)
+    g_pre = (gd_scr[...] * (1.0 / LOG2E) + gu * inp) * sigmoid(pre)
     bacc_scr[...] += jnp.sum(g_pre.reshape(steps, slots, width), axis=0)
     g_low = g_pre.astype(BF16)
     gmisc_ref[:, :rank] += dot(g_low, dtl_ref[...], ((0,), (0,)))
-    pack_rows(gproj_ref, dot(g_low, dtw_ref[...]), gbc_ref[...], length)
+    pack_rows(scratch[0], (final - step_id) * parts, dot(g_low, dtw_ref[...]), gbc_ref[...], length)
+
+    @pl.when(step_id > 0)
+    def _():
+        for a in range(parts):
+            relay((final - step_id + 1) * parts + a)
 
     @pl.when(step_id == pl.num_programs(0) - 1)
     def _():
@@ -296,8 +462,28 @@
             back_scr[DECAY + n : DECAY + n + 1, :] = jnp.sum(dacc_scr[n], axis=0, keepdims=True) * rate
         back_scr[SKIP : SKIP + 1, :] = jnp.sum(sacc_scr[...], axis=0, keepdims=True)
         back_scr[DT_BIAS : DT_BIAS + 1, :] = jnp.sum(bacc_scr[...], axis=0, keepdims=True)
+        for a in range(parts):
+            send(a)
         gmisc_ref[:, rank:] = jnp.transpose(back_scr[...])
         gout_ref[...] = gout_scr[...].astype(gout_ref.dtype)
+        for a in range(parts):
+            relay(a)
+        steps_run = pl.num_programs(0)
+        lax.fori_loop(jnp.minimum(steps_run // 2, n_z - 1), n_z - 1, lambda u, c: (hop(u), c)[1], 0)
+        settle()
+        close()
+        done.wait()
+        for to in range(n_z):
+            for j in range(n_dp):
+                one(to, j).wait_send()
+
+                @pl.when(z < to)
+                def _():
+                    up(to, j).wait_send()
+
+                @pl.when(z > to)
+                def _():
+                    down(to, j).wait_send()
 
 
 def remote(src, dst, send, recv, where):
@@ -512,20 +698,20 @@
         g1(k).wait_send()
 
 
-def pack_rows(out_ref, main, rest, chunk):
+def pack_rows(out_ref, base, main, rest, chunk):
     part = chunk // 4
     for q in range(main.shape[0] // chunk):
-        out_ref[q, 0:chunk, :] = main[q * chunk : (q + 1) * chunk, :]
+        out_ref[base + q, 0:chunk, :] = main[q * chunk : (q + 1) * chunk, :]
         for j in range(4):
             first = q * chunk + j * part
-            out_ref[q, chunk : chunk + part, j * 32 : (j + 1) * 32] = rest[first : first + part, :]
-
-
-def combine_kernel(
-    part_ref, main_ref, rest_ref, one, sums, two, tops, rests,
-    one_send, one_recv, two_send, two_recv, top_send, top_recv, rest_send, rest_recv,
-    ctop_send, ctop_recv, crest_send, crest_recv, *, n_dp, n_f
-):
+            out_ref[base + q, chunk : chunk + part, j * 32 : (j + 1) * 32] = rest[first : first + part, :]
+
+
+def combiner(scratch, main_ref, rest_ref, n_f):
+    (
+        part, own, one, sums, two, tops, rests, one_send, one_recv, two_send, two_recv, top_send, top_recv,
+        rest_send, rest_recv, ctop_send, ctop_recv, crest_send, crest_recv,
+    ) = scratch
     d = lax.axis_index("dp")
     f = lax.axis_index("fsdp")
     n_z = n_f // 2
@@ -535,20 +721,10 @@
     partner = z * 2 + other
     chunk = tops.shape[2]
 
-    barrier = pltpu.get_barrier_semaphore()
-    pl.semaphore_signal(barrier, inc=1, device_id=(d, partner), device_id_type=pl.DeviceIdType.MESH)
-    for k in range(1, n_z):
-        pl.semaphore_signal(
-            barrier, inc=1, device_id=(d, (z + k) % n_z * 2 + core), device_id_type=pl.DeviceIdType.MESH
-        )
-    pl.semaphore_wait(barrier, n_z)
-
-    def first(k):
-        to = (z + k) % n_z
-        return remote(part_ref.at[to, other], one.at[to], one_send.at[k], one_recv.at[k], (d, partner))
-
-    def second(k):
-        to = (z + k) % n_z
+    def first(q):
+        return remote(part.at[q], one.at[q // 2], one_send.at[q // 2], one_recv.at[q // 2], (d, partner))
+
+    def second(to, k):
         return remote(sums.at[to], two.at[k], two_send.at[k], two_recv.at[k], (d, to * 2 + core))
 
     def third(k):
@@ -573,60 +749,97 @@
             remote(rests.at[src, side], rests.at[src, side], crest_send.at[k], crest_recv.at[k], (d, partner)),
         )
 
-    order = list(range(1, n_z)) + [0]
-    for k in order:
-        first(k).start()
-    for k in order:
-        to = (z + k) % n_z
-        first(k).wait_recv()
-        sums[to] = (part_ref[to, core] + one[to]).astype(sums.dtype)
-        if k:
-            second(k).start()
-    total = part_ref[z, core] + one[z]
-    for k in range(1, n_z):
-        second(k).wait_recv()
-        total = total + two[k].astype(F32)
-    tops[z, core] = total[0:chunk, :].astype(tops.dtype)
-    rests[z, core] = total[chunk:, :].astype(rests.dtype)
-    for k in range(1, n_z):
-        for copy in third(k):
+    def enter(peers=()):
+        barrier = pltpu.get_barrier_semaphore()
+        for peer in peers:
+            pl.semaphore_signal(barrier, inc=1, device_id=peer, device_id_type=pl.DeviceIdType.MESH)
+        pl.semaphore_signal(barrier, inc=1, device_id=(d, partner), device_id_type=pl.DeviceIdType.MESH)
+        for k in range(1, n_z):
+            pl.semaphore_signal(
+                barrier, inc=1, device_id=(d, (z + k) % n_z * 2 + core), device_id_type=pl.DeviceIdType.MESH
+            )
+        pl.semaphore_wait(barrier, n_z + len(peers))
+
+    def send(q):
+        @pl.when(q % 2 == other)
+        def _():
+            first(q).start()
+
+    def relay(q):
+        @pl.when(q % 2 == core)
+        def _():
+            to = q // 2
+            first(q).wait_recv()
+            total = part[q] + one[to]
+
+            @pl.when(to == z)
+            def _():
+                own[...] = total
+
+            @pl.when(to != z)
+            def _():
+                sums[to] = total.astype(sums.dtype)
+                second(to, (to - z + n_z) % n_z).start()
+
+    def close():
+        total = own[...]
+        for k in range(1, n_z):
+            second(z, k).wait_recv()
+            total = total + two[k].astype(F32)
+        tops[z, core] = total[0:chunk, :].astype(tops.dtype)
+        rests[z, core] = total[chunk:, :].astype(rests.dtype)
+        for k in range(1, n_z):
+            for copy in third(k):
+                copy.start()
+        for copy in fourth(0, core):
             copy.start()
-    for copy in fourth(0, core):
-        copy.start()
-    for k in range(1, n_z):
-        for copy in third_arrival(k):
-            copy.wait_recv()
-        for copy in fourth(k, core):
-            copy.start()
-    for k in range(n_z):
-        for copy in fourth(k, other):
-            copy.wait_recv()
-    part = chunk // 4
-    for a in range(n_z):
-        for b in range(2):
-            at = (a * 2 + b) * chunk
-            main_ref[at : at + chunk, :] = tops[a, b]
-            rest = rests[a, b]
-            for j in range(4):
-                rest_ref[at + j * part : at + (j + 1) * part, :] = rest[:, j * 32 : (j + 1) * 32]
-    for k in range(n_z):
-        first(k).wait_send()
-        for copy in fourth(k, core):
-            copy.wait_send()
-        if k:
-            second(k).wait_send()
-            for copy in third(k):
+        for k in range(1, n_z):
+            for copy in third_arrival(k):
+                copy.wait_recv()
+            for copy in fourth(k, core):
+                copy.start()
+        for k in range(n_z):
+            for copy in fourth(k, other):
+                copy.wait_recv()
+        quarter = chunk // 4
+        for a in range(n_z):
+            for b in range(2):
+                at = (a * 2 + b) * chunk
+                main_ref[at : at + chunk, :] = tops[a, b]
+                rest = rests[a, b]
+                for j in range(4):
+                    rest_ref[at + j * quarter : at + (j + 1) * quarter, :] = rest[:, j * 32 : (j + 1) * 32]
+        for k in range(n_z):
+            first(k * 2 + other).wait_send()
+            for copy in fourth(k, core):
                 copy.wait_send()
+            if k:
+                second((z + k) % n_z, k).wait_send()
+                for copy in third(k):
+                    copy.wait_send()
+
+    return enter, send, relay, close
+
+
+def combine_scratch(n_f, length, rest_type):
+    n_z = n_f // 2
+    packed_rows = length + length // 4
+    return [
+        pltpu.VMEM((n_f, packed_rows, 128), F32), pltpu.VMEM((packed_rows, 128), F32),
+        pltpu.VMEM((n_z, packed_rows, 128), F32), pltpu.VMEM((n_z, packed_rows, 128), HOP),
+        pltpu.VMEM((n_z, packed_rows, 128), HOP), pltpu.VMEM((n_z, 2, length, 128), BF16),
+        pltpu.VMEM((n_z, 2, length // 4, 128), rest_type),
+    ] + [pltpu.SemaphoreType.DMA((n_z,))] * 12
 
 
 def finish_kernel(
     gdtl_ref, gbc_ref, inp_ref, gis_ref, ggate_ref, inner_ref, before_ref, x_ref, gain_ref, win_ref, xw_ref, misc_ref,
-    gout_ref, gback_ref, out_ref, gin_out, gout_out, gback_out, gtail_out, gg_out,
+    gout_ref, gback_ref, br_ref, out_ref, brout_ref, gin_out, gout_out, gback_out, gtail_out, gg_out,
     misc_scr, tail_scr, gin_scr, gsel_scr, grest_scr, ggain_scr, pad_scr, gpad_scr, wacc_scr, cacc_scr,
     mine, theirs, passed, gin_low, gin_got, gin_sum, gin_all, gout_got, gback_got, gtail_low, gtail_got,
-    gg_low, gg_got, gg_sum, gg_all, local_sem,
+    gg_low, gg_got, gg_sum, gg_all, br_buf, local_sem,
     one_send, one_recv, up_send, up_recv, down_send, down_recv, dp_send, dp_recv,
-    w_send, w_recv, o_send, o_recv, b_send, b_recv, t_send, t_recv, g_send, g_recv,
+    r_send, r_recv, w_send, w_recv, o_send, o_recv, b_send, b_recv, t_send, t_recv, g_send, g_recv,
     w2_send, w2_recv, g2_send, g2_recv, *, slots, n_dp, n_f
 ):
     d = lax.axis_index("dp")
@@ -689,6 +902,16 @@
         to = (f - k + n_f) % n_f
         return remote(src.at[to], dst.at[to], send.at[k], recv.at[k], (d, to))
 
+    def branch(k):
+        to = (d + k) % n_dp
+        return remote(br_ref.at[to], brout_ref.at[d], r_send.at[k], r_recv.at[k], (to, f))
+
+    def branch_arrival(k):
+        src = (d - k + n_dp) % n_dp
+        return remote(br_ref.at[src], brout_ref.at[src], r_send.at[k], r_recv.at[k], (src, f))
+
+    get_branch = pltpu.make_async_copy(br_ref.at[d], br_buf, local_sem.at[3])
+    put_branch = pltpu.make_async_copy(br_buf, brout_ref.at[d], local_sem.at[4])
     outs = lambda: over_dp(gout_ref, gout_got, o_send, o_recv)
     backs = lambda: over_dp(gback_ref, gback_got, b_send, b_recv)
     ins = lambda: over_dp(gin_low, gin_got, w_send, w_recv)
@@ -795,6 +1018,9 @@
         pl.semaphore_wait(barrier, n_f + n_dp - 2)
         for copy in outs() + backs():
             copy.start()
+        for k in range(1, n_dp):
+            branch(k).start()
+        get_branch.start()
         own_out.start()
         own_back.start()
         gpad_scr[rows : rows + halo, :] = jnp.zeros((halo, width), F32)
@@ -866,9 +1092,11 @@
             gtail_low[a, :, :rank] = gsel_scr[at : at + inner_rows, :]
             gtail_low[a, :, rank:] = grest_scr[at : at + inner_rows, :]
         send_halves(last)
-        hops(blocks)
         for copy in ins() + tails() + gains():
             copy.start()
+        hops(blocks)
+        get_branch.wait()
+        put_branch.start()
         own_out.wait()
         own_back.wait()
         for copy in outs() + backs():
@@ -929,6 +1157,10 @@
             dp_arrival(k).wait_recv()
             dp(k).wait_send()
         put.wait()
+        put_branch.wait()
+        for k in range(1, n_dp):
+            branch_arrival(k).wait_recv()
+            branch(k).wait_send()
         for copy in outs() + backs() + ins() + tails() + gains():
             copy.wait_send()
         for k in range(1, n_f):
@@ -955,8 +1187,12 @@
     return pl.CostEstimate(flops=int(micros * 1.15e9), bytes_accessed=1 << 20, transcendentals=0)
 
 
-def params():
-    return pltpu.CompilerParams(vmem_limit_bytes=VMEM_BYTES, dimension_semantics=("arbitrary",))
+def params(number=None):
+    if number is None:
+        return pltpu.CompilerParams(vmem_limit_bytes=VMEM_BYTES, dimension_semantics=("arbitrary",))
+    return pltpu.CompilerParams(
+        vmem_limit_bytes=FULL_VMEM, dimension_semantics=("arbitrary",), collective_id=number, has_side_effects=True
+    )
 
 
 def body(
@@ -983,10 +1219,8 @@
     def by_group(v):
         return v.reshape(n_dp, slots, own, model).transpose(0, 2, 1, 3).reshape(n_dp, own * slots, model)
 
-    def collect(v):
-        v = lax.psum_scatter(v.reshape(total_rows, model), "fsdp", scatter_dimension=0, tiled=True)
-        v = lax.all_to_all(v.reshape(n_dp, own, slots, model), "dp", 0, 0, tiled=True)
-        return v.transpose(0, 2, 1, 3).reshape(seqs, own, model)
+    def by_seq(v):
+        return v.reshape(n_dp, own, slots, model).transpose(0, 2, 1, 3).reshape(seqs, own, model).astype(F32)
 
     masked = by_group(jnp.where(own_mask[:, :, None], cotangent, jnp.zeros_like(cotangent)))
 
@@ -998,7 +1232,8 @@
         [x_weight[:, rank:], decay_log, conv_weight, conv_bias[:, None], dt_bias[:, None], skip_gain[:, None]], axis=1
     )
     misc = jnp.pad(misc, ((0, 0), (0, 128 - misc.shape[1])))
-    packed = low(jnp.concatenate([out_weight, x_weight[:, :rank], misc, dt_weight], axis=1))
+    packed = low(jnp.concatenate([x_weight[:, :rank], misc, dt_weight], axis=1))
+    ow = low(out_weight)
     n_z = n_f // 2
     dma = pltpu.SemaphoreType.DMA
     hbm = pl.BlockSpec(memory_space=pl.ANY)
@@ -1030,69 +1265,51 @@
     win = win.reshape(model, 2 * width)
     gain = gain[:, :, 0, :d_rows].reshape(1, model)
     packed = packed.reshape(width, -1)
-    rows = STEPS * slots
-    blocks = length // STEPS
+    span = ROWS // slots
+    rows = span * slots
+    blocks = length // span
     grid = (blocks,)
     row_spec = lambda cols: pl.BlockSpec((rows, cols), lambda i: (i, 0))
     rev_spec = lambda cols: pl.BlockSpec((rows, cols), lambda i: (blocks - 1 - i, 0))
     once = dict(pipeline_mode=pl.Buffered(1))
     ow_spec = pl.BlockSpec((width, model), lambda i: (0, 0), **once)
-    xw_spec = pl.BlockSpec((width, 128), lambda i: (0, model // 128), **once)
-    misc_spec = pl.BlockSpec((width, 128), lambda i: (0, model // 128 + 1), **once)
-    dtw_spec = pl.BlockSpec((width, 128), lambda i: (0, model // 128 + 2), **once)
+    xw_spec = pl.BlockSpec((width, 128), lambda i: (0, 0), **once)
+    misc_spec = pl.BlockSpec((width, 128), lambda i: (0, 1), **once)
+    dtw_spec = pl.BlockSpec((width, 128), lambda i: (0, 2), **once)
     win_spec = pl.BlockSpec((model, 2 * width), lambda i: (0, 0), **once)
     misc_shape = pltpu.VMEM((128, width), F32)
     like = jax.ShapeDtypeStruct
-    held = STEPS // own
+    held = span // own
     per = n_f // held
     piece = (held, 1, own * slots, model)
     piece_spec = pl.BlockSpec(piece, lambda i: (i % per, i // per, 0, 0))
     rev_piece_spec = pl.BlockSpec(piece, lambda i: ((blocks - 1 - i) % per, (blocks - 1 - i) // per, 0, 0))
     pieces_shape = like((n_f, n_dp, own * slots, model), BF16)
-    packed_rows = length + length // 4
-    parts = rows // length
-    part_spec = pl.BlockSpec((parts, packed_rows, 128), lambda i: (i, 0, 0))
-    rev_part_spec = pl.BlockSpec((parts, packed_rows, 128), lambda i: (blocks - 1 - i, 0, 0))
-    parts_shape = like((n_f, packed_rows, 128), F32)
-
-    def combine(v, rest_type, number):
-        vmem = pl.BlockSpec(memory_space=pltpu.VMEM)
-        return pl.pallas_call(
-            functools.partial(combine_kernel, n_dp=n_dp, n_f=n_f),
-            in_specs=[vmem],
-            out_specs=[vmem, vmem],
-            out_shape=[like((total_rows, rank), BF16), like((total_rows, 2 * states), rest_type)],
-            scratch_shapes=[
-                pltpu.VMEM((n_z, packed_rows, 128), F32), pltpu.VMEM((n_z, packed_rows, 128), BF16),
-                pltpu.VMEM((n_z, packed_rows, 128), BF16), pltpu.VMEM((n_z, 2, length, 128), BF16),
-                pltpu.VMEM((n_z, 2, length // 4, 128), rest_type),
-            ]
-            + [dma((n_z,))] * 12,
-            compiler_params=pltpu.CompilerParams(
-                collective_id=number, has_side_effects=True, vmem_limit_bytes=VMEM_BYTES
-            ),
-            cost_estimate=cost(28),
-        name="combine",
-        )(v.reshape(n_z, 2, packed_rows, 128))
-
-    inner, gate, inp, proj = pl.pallas_call(
-        functools.partial(front_kernel, slots=slots, length=length),
+    inner, gate, inp, dtl, bc, ow = pl.pallas_call(
+        functools.partial(front_kernel, slots=slots, length=length, n_dp=n_dp, n_f=n_f),
         grid=grid,
         in_specs=[
-            row_spec(model), whole((1, model)), win_spec, xw_spec, misc_spec,
+            row_spec(model), whole((1, model)), win_spec, xw_spec, misc_spec, hbm,
         ],
-        out_specs=[row_spec(width), row_spec(width), row_spec(width), part_spec],
+        out_specs=[
+            row_spec(width), row_spec(width), row_spec(width), whole((total_rows, rank)), whole((total_rows, 2 * states)),
+            hbm,
+        ],
         out_shape=[
             like((total_rows, width), F32), like((total_rows, width), F32), like((total_rows, width), BF16),
-            parts_shape,
+            like((total_rows, rank), BF16), like((total_rows, 2 * states), F32), like((n_dp,) + ow.shape, BF16),
         ],
-        scratch_shapes=[pltpu.VMEM((rows + 3 * slots, width), F32), misc_shape],
-        compiler_params=params(),
-        cost_estimate=cost(20),
+        scratch_shapes=[
+            pltpu.VMEM((rows + 3 * slots, width), F32), misc_shape, pltpu.VMEM(ow.shape, BF16),
+            dma((n_dp,)), dma((n_dp,)), dma((2,)),
+        ]
+        + combine_scratch(n_f, length, F32),
+        compiler_params=params(2),
+        cost_estimate=cost(42),
         name="front",
-    )(x, gain, win, packed, packed)
-
-    dtl, bc = combine(proj, F32, 2)
+    )(x, gain, win, packed, packed, ow)
+    ow = ow.reshape(width, model)
+
 
     y, ck, branch = pl.pallas_call(
         functools.partial(mix_kernel, slots=slots),
@@ -1114,21 +1331,24 @@
         compiler_params=params(),
         cost_estimate=cost(36),
         name="mix",
-    )(dtl, bc, inp, gate, packed, packed, packed)
-
-    gis, ggate, gproj, gout, gmisc = pl.pallas_call(
-        functools.partial(back_kernel, slots=slots, length=length),
+    )(dtl, bc, inp, gate, packed, packed, ow)
+
+    gis, ggate, gdtl, gbc, gout, gmisc, branch = pl.pallas_call(
+        functools.partial(back_kernel, slots=slots, length=length, n_dp=n_dp, n_f=n_f),
         grid=grid,
         in_specs=[
             rev_piece_spec, rev_spec(rank), rev_spec(2 * states), rev_spec(width), rev_spec(width), rev_spec(width),
             pl.BlockSpec((1, states, slots, width), lambda i: (blocks - 1 - i, 0, 0, 0)), dtw_spec, misc_spec, ow_spec,
+            hbm,
         ],
         out_specs=[
-            rev_spec(width), rev_spec(width), rev_part_spec, whole((width, model)), whole((width, 256)),
+            rev_spec(width), rev_spec(width), whole((total_rows, rank)), whole((total_rows, 2 * states)),
+            whole((width, model)), whole((width, 256)), hbm,
         ],
         out_shape=[
-            like((total_rows, width), F32), like((total_rows, width), BF16), parts_shape,
-            like((width, model), BF16), like((width, 256), F32),
+            like((total_rows, width), F32), like((total_rows, width), BF16), like((total_rows, rank), BF16),
+            like((total_rows, 2 * states), BF16), like((width, model), BF16), like((width, 256), F32),
+            like((n_dp, own * slots, model), BF16),
         ],
         scratch_shapes=[
             pltpu.VMEM((states, slots, width), F32), pltpu.VMEM((states, slots, width), F32),
@@ -1136,37 +1356,38 @@
         ]
         + [pltpu.VMEM((rows, width), F32)] * 5
         + [
-            pltpu.VMEM((STEPS, states, slots, width), F32), pltpu.VMEM((STEPS, states, slots, width), F32),
+            pltpu.VMEM((span, states, slots, width), F32), pltpu.VMEM((span, states, slots, width), F32),
             pltpu.VMEM((2 * states, rows, 128), F32), pltpu.VMEM((PAIR, 2 * states, slots, 128), F32),
             pltpu.VMEM((PAIR, 2 * states, slots, 128), F32), pltpu.VMEM((2 * states, rows), F32),
             pltpu.VMEM((states, slots, width), F32), pltpu.VMEM((rows, 2 * states), F32), misc_shape, misc_shape,
-            pltpu.VMEM((width, model), F32),
-        ],
-        compiler_params=params(),
-        cost_estimate=cost(95),
+            pltpu.VMEM((width, model), F32), pltpu.VMEM((n_z, n_dp, own * slots, model), BF16),
+            pltpu.VMEM((n_z, n_dp, own * slots, model), BF16), pltpu.VMEM((n_z + 1, n_dp, own * slots, model), BF16),
+            dma((n_z, n_dp)), dma((1,)),
+        ]
+        + [dma((n_z, n_dp))] * 6
+        + combine_scratch(n_f, length, BF16),
+        compiler_params=params(3),
+        cost_estimate=cost(100),
         name="back",
-    )(g_branch, dtl, bc, inp, gate, y, ck, packed, packed, packed)
-
-    gdtl, gbc = combine(gproj, BF16, 3)
-
-    branch = collect(branch)
-    branch, gdtl = lax.optimization_barrier((branch, gdtl))
+    )(g_branch, dtl, bc, inp, gate, y, ck, packed, packed, ow, branch)
+
+
     tile = own * slots
     vmem = pltpu.VMEM
-    g_normed, gin, gout, gback, gtail, ggain = pl.pallas_call(
+    g_normed, branch, gin, gout, gback, gtail, ggain = pl.pallas_call(
         functools.partial(finish_kernel, slots=slots, n_dp=n_dp, n_f=n_f),
         grid=grid,
         in_specs=[
             rev_spec(rank), rev_spec(2 * states), rev_spec(width), rev_spec(width), rev_spec(width), rev_spec(width),
-            pl.BlockSpec((4 * slots, width), lambda i: (jnp.maximum((blocks - 1 - i) * (STEPS // 4) - 1, 0), 0)),
-            rev_spec(model), whole((1, model)), win_spec, xw_spec, misc_spec, hbm, hbm,
+            pl.BlockSpec((4 * slots, width), lambda i: (jnp.maximum((blocks - 1 - i) * (span // 4) - 1, 0), 0)),
+            rev_spec(model), whole((1, model)), win_spec, xw_spec, misc_spec, hbm, hbm, hbm,
         ],
         out_specs=[
-            hbm, whole((d_rows, 2 * width * n_f)), whole((inner_rows, model)), whole((inner_rows, 256)),
+            hbm, hbm, whole((d_rows, 2 * width * n_f)), whole((inner_rows, model)), whole((inner_rows, 256)),
             whole((inner_rows, 256)), whole((8, 128)),
         ],
         out_shape=[
-            like((n_dp, tile, model), BF16), like((d_rows, 2 * width * n_f), F32), like((inner_rows, model), F32),
+            like((n_dp, tile, model), BF16), like((n_dp, tile, model), BF16), like((d_rows, 2 * width * n_f), F32), like((inner_rows, model), F32),
             like((inner_rows, 256), F32), like((inner_rows, 256), F32), like((8, 128), F32),
         ],
         scratch_shapes=[
@@ -1180,25 +1401,23 @@
             vmem((n_dp, inner_rows, model), BF16), vmem((n_dp, inner_rows, 256), F32),
             vmem((n_dp, inner_rows, 256), F32), vmem((n_dp, inner_rows, 256), F32),
             vmem((n_dp, n_f, 8, 128), F32), vmem((n_dp, n_f, 8, 128), F32), vmem((n_f, 8, 128), F32),
-            vmem((n_f, 8, 128), F32), dma((3,)),
+            vmem((n_f, 8, 128), F32), vmem((tile, model), BF16), dma((5,)),
         ]
         + [dma((n_z, n_dp))] * 6
-        + [dma((n_dp,))] * 12
+        + [dma((n_dp,))] * 14
         + [dma((n_f,))] * 4,
-        compiler_params=pltpu.CompilerParams(
-            collective_id=4, has_side_effects=True, vmem_limit_bytes=FULL_VMEM, dimension_semantics=("arbitrary",)
-        ),
+        compiler_params=params(4),
         cost_estimate=cost(105),
         name="finish",
     )(
         gdtl, gbc, inp, gis, ggate, inner, inner, x, gain, win, packed, packed,
-        gout.reshape(n_dp, inner_rows, model), gmisc.reshape(n_dp, inner_rows, 256),
+        gout.reshape(n_dp, inner_rows, model), gmisc.reshape(n_dp, inner_rows, 256), branch,
     )
 
     hidden = tokens.astype(F32)
     upstream = cotangent.astype(F32)
-    output = (hidden + jnp.where(own_mask[:, :, None], branch.astype(F32), 0.0)).astype(BF16)
-    g_normed = g_normed.reshape(n_dp, own, slots, model).transpose(0, 2, 1, 3).reshape(seqs, own, model).astype(F32)
+    output = (hidden + jnp.where(own_mask[:, :, None], by_seq(branch), 0.0)).astype(BF16)
+    g_normed = by_seq(g_normed)
     factor = lax.rsqrt(jnp.mean(hidden * hidden, axis=-1, keepdims=True) + EPSILON)
     weighted = gain * g_normed
     input_grad = (

time: 507 us -> 488 us (0.963)
  Pallas kernels: 436 us -> 420 us
    pallas_call x3 -> x1, Pallas kernels: 154 us -> 115 us  [body(): pl.pallas_call(functools.partial(back_kernel, slots=slots, length=length,...]
    pallas_call x1, Pallas kernels: 20.5 us -> 49.8 us  [body(): pl.pallas_call(functools.partial(front_kernel, slots=slots, length=length...]
    pallas_call x1, Pallas kernels: 105 us -> 94.9 us  [body(): pl.pallas_call(functools.partial(gather_kernel, n_dp=n_dp, n_f=n_f), in_s...]
    all_gather x1, waiting for transfers between devices: 0.2 us -> 8.53 us  [body(): g_branch = lax.all_gather(g_branch, 'fsdp', axis=0, tiled=False)]
    reduce_scatter x1 -> x0, waiting for transfers between devices: 6.43 us -> none  [collect(): lax.psum_scatter(v.reshape(total_rows, model), 'fsdp', scatter_dimension=...]
  transfers between devices with their start and end apart: 3 -> 1, of which waited for: 2 -> 1; matrix products, arithmetic and copies ran while one was open for 0% -> 1% of each run, Pallas kernels for 42% -> 18%
where the time goes in v5:
time: 488 us; the launch traced here: 482 us
  Pallas kernels  420 us (86%)
  local copies, waits for them, and re-layouts  26.2 us (5%)
  between operations  14.3 us (3%)
  other arithmetic  13.5 us (3%)
  waiting for transfers between devices  8.55 us (2%)
    pallas_call x1, Pallas kernels, body(): pl.pallas_call(functools.partial(finish_kernel, slots=slots, n_dp=n_dp, n...  125 us
    pallas_call x1, Pallas kernels, body(): pl.pallas_call(functools.partial(back_kernel, slots=slots, length=length,...  115 us
    pallas_call x1, Pallas kernels, body(): pl.pallas_call(functools.partial(gather_kernel, n_dp=n_dp, n_f=n_f), in_s...  94.9 us
    pallas_call x1, Pallas kernels, body(): pl.pallas_call(functools.partial(front_kernel, slots=slots, length=length...  49.8 us
    pallas_call x1, Pallas kernels, body(): pl.pallas_call(functools.partial(mix_kernel, slots=slots), grid=grid, in_...  35.2 us
  transfers between devices with their start and end apart: 1, of which 1 were waited for; matrix products, arithmetic and copies ran while one was open for 1% of the time, Pallas kernels for 18%

profile of v5, /device:TPU:0, one launch (start us, length us, event | category | flops | bytes accessed | tf_op | source)
XLA Modules:
  0.0 482.3 jit_solution(4354033627705986202)
XLA Ops:
  7.2 0.7 slice.63
  8.0 0.8 slice.62
  11.4 0.7 convert.41
  12.7 0.7 convert.40
  14.2 0.9 convert.45
  15.2 1.8 convert_bitcast_fusion.2
  17.7 1.5 reshape.161.win_ref
  19.6 2.5 copy_bitcast_fusion.1
  22.9 94.9 %gather.1 = (bf16[4,8,64,2048]{3,2,1,0:T(8,128)(2,1)}, bf16[4,64,2048]{2,1,0:T(8,128)(2,1)}, bf16[4,8,64,1024]{3,2,1,0:T(8,128)(2,1)}, f32[4,8,8,128]{3,2,1,0:T(8,128)}, bf16[4,128,384]{2,1,0:T(8,128)(2,1)}) custom-call(bf16[4,64,2048]{2,1,0:T(8,128)(2,1)} %get-tuple-element.139.tok_ref, bf16[4,64,2048]{2,1,0:T(8,128)(2,1)} %get-tuple-element.138.cot_ref, ...), custom_call_target="tpu_custom_call" | custom-call | flops 103499997184 | bytes 1048576 | tf_op jit(solution)/shard_map/gather/pallas_call | solution.py:1240
  117.8 0.9 convert_element_type.52.ow_ref
  118.7 1.0 fusion.10
  119.6 0.7 mul.50
  120.3 0.7 reshape_squeeze.3.gain_ref
  121.0 49.8 %front.1 = (f32[2048,512]{1,0:T(8,128)}, f32[2048,512]{1,0:T(8,128)}, bf16[2048,512]{1,0:T(8,128)(2,1)}, bf16[2048,128]{1,0:T(8,128)(2,1)}, f32[2048,32]{1,0:T(8,128)}, /*index=5*/bf16[4,128,2048]{2,1,0:T(8,128)(2,1)}) custom-call(bf16[2048,2048]{1,0:T(8,128)(2,1)} %bitcast.60, f32[1,2048]{1,0:T(1,128)} %reshape_squeeze.3.gain_ref, ...), custom_call_target="tpu_custom_call" | custom-call | flops 48299999232 | bytes 1048576 | tf_op jit(solution)/shard_map/front/pallas_call | solution.py:1288
  170.7 35.2 %mix.1 = (f32[2048,512]{1,0:T(8,128)}, f32[8,16,8,512]{3,2,1,0:T(8,128)}, bf16[8,4,64,2048]{3,2,1,0:T(8,128)(2,1)}) custom-call(bf16[2048,128]{1,0:T(8,128)(2,1)} %get-tuple-element.57.dtl_ref, f32[2048,32]{1,0:T(8,128)} %get-tuple-element.58.bc_ref, bf16[2048,512]{1,0:T(8,128)(2,1)} %get-tuple-element.59.inp_ref, f32[2048,512]{1,0:T(8,128)} %get-tuple-element.60.gate_ref, ...), custom_call_target="tpu_custom_call" | custom-call | flops 41400000512 | bytes 1048576 | tf_op jit(solution)/shard_map/mix/pallas_call | solution.py:1314
  205.9 8.5 %all-gather.3.cloned.1.call-done = bf16[32,64,2048]{2,1,0:T(8,128)(2,1)} async-done(((bf16[4,64,2048]{2,1,0:T(8,128)(2,1)}), bf16[32,64,2048]{2,1,0:T(8,128)(2,1)}) %all-gather.3.cloned.1.call-update) | async-done | bytes 8388624 | tf_op jit(solution)/shard_map/all_gather | solution.py:1263
  214.5 115.1 %back.1 = (f32[2048,512]{1,0:T(8,128)}, bf16[2048,512]{1,0:T(8,128)(2,1)}, bf16[2048,128]{1,0:T(8,128)(2,1)}, bf16[2048,32]{1,0:T(8,128)(2,1)}, bf16[512,2048]{1...) custom-call(bf16[8,4,64,2048]{3,2,1,0:T(8,128)(2,1)} %bitcast.59, ...), custom_call_target="tpu_custom_call" | custom-call | flops 115000000512 | bytes 1048576 | tf_op jit(solution)/shard_map/back/pallas_call | solution.py:1336
  329.6 124.7 %finish.1 = (bf16[4,64,2048]{2,1,0:T(8,128)(2,1)}, bf16[4,64,2048]{2,1,0:T(8,128)(2,1)}, f32[64,8192]{1,0:T(8,128)}, f32[128,2048]{1,0:T(8,128)}, f32[128,256]{1...) custom-call(bf16[2048,128]{1,0:T(8,128)(2,1)} %get-tuple-element.65.gdtl_ref, ...), custom_call_target="tpu_custom_call" | custom-call | flops 120749998080 | bytes 1048576 | tf_op jit(solution)/shard_map/finish/pallas_call | solution.py:1377
  454.3 1.5 slice_reduce_fusion.2
  455.8 0.9 slice.55
  456.7 1.6 slice_reduce_fusion
  458.3 0.9 slice.60
  459.2 1.5 slice.58
  460.7 1.2 slice_bitcast_fusion
  462.6 0.7 copy.78
  463.2 1.6 copy.77
  464.9 1.5 convert_bitcast_fusion.1
  466.4 1.2 copy.74
  467.9 1.2 copy.75
  470.3 2.2 fusion.4
  472.5 1.3 copy.88
  474.5 1.0 copy.89
  (53 shorter events, 8.7 us)
Async XLA Ops:
  7.2 207.3 %all-gather.3.cloned.1.call-start = ((), (), s32[]{:S(2)}) async-start(), calls=%async_computation | async-start | bytes 9437184 | tf_op jit(solution)/shard_map/all_gather | solution.py:1263
  17.2 2.0 copy-start.11
  17.2 2.0 copy-start.12
  17.2 2.2 copy-start.2
  17.7 1.9 copy-start
  19.4 2.7 copy-start.9
  22.9 94.9 %copy-start.6 = (f32[128,2048]{1,0:T(8,128)S(1)}, f32[128,2048]{1,0:T(8,128)}, u32[]{:S(2)}) copy-start(f32[128,2048]{1,0:T(8,128)} %param.29) | copy-start | bytes 3145732
  466.3 1.2 copy-start.5
  467.8 1.3 copy-start.1
  467.8 1.3 copy-start.8
  469.1 1.2 copy-start.3
  469.1 1.2 copy-start.10
  470.3 2.2 copy-start.4
  472.5 2.0 copy-start.7
Sparse Core Ops, SparseCore 0:
  117.9 96.5 all-gather.2

commit v6 on v5

--- a/solution.py
+++ b/solution.py
@@ -10,6 +10,7 @@
 ROWS = 256
 PAIR = 2
 LAG = 4
+MID = 3
 HOP = jnp.bfloat16
 LANES = 8
 TOGETHER = 8
@@ -40,20 +41,36 @@
 
 
 def front_kernel(
-    x_ref, gain_ref, win_ref, xw_ref, misc_ref, ow_ref, inner_ref, gate_ref, inp_ref, dtl_ref, bc_ref, owf_ref,
-    pad_ref, misc_scr, ow_buf, ow_send, ow_recv, ow_local, *scratch, slots, length, n_dp, n_f
+    x_ref, gain_ref, win_ref, xw_ref, misc_ref, ow_ref, cin_ref, inner_ref, gate_ref, inp_ref, dtl_ref, bc_ref, owf_ref, c_ref,
+    pad_ref, misc_scr, ow_raw, ow_buf, ow_send, ow_recv, ow_local, c_buf, c_local,
+    cu_send, cu_recv, cd_send, cd_recv, ca_send, ca_recv, *scratch, slots, length, n_dp, n_f
 ):
     d = lax.axis_index("dp")
     f = lax.axis_index("fsdp")
 
     def ow(k):
-        return remote(ow_ref, owf_ref.at[d], ow_send.at[k], ow_recv.at[k], ((d + k) % n_dp, f))
+        return remote(ow_buf, owf_ref.at[d], ow_send.at[k], ow_recv.at[k], ((d + k) % n_dp, f))
 
     def ow_arrival(k):
         src = (d - k + n_dp) % n_dp
-        return remote(ow_ref, owf_ref.at[src], ow_send.at[k], ow_recv.at[k], (src, f))
-
-    ow_get = pltpu.make_async_copy(ow_ref, ow_buf, ow_local.at[0])
+        return remote(ow_buf, owf_ref.at[src], ow_send.at[k], ow_recv.at[k], (src, f))
+
+    n_z = n_f // 2
+    z = f // 2
+    partner = z * 2 + 1 - f % 2
+
+    def c_up(j, src):
+        return remote(cin_ref.at[j], c_ref.at[src, j], cu_send.at[j], cu_recv.at[j], (d, f + 2))
+
+    def c_down(j, src):
+        return remote(cin_ref.at[j], c_ref.at[src, j], cd_send.at[j], cd_recv.at[j], (d, f - 2))
+
+    def c_across(j, src):
+        return remote(cin_ref.at[j], c_ref.at[src, j], ca_send.at[j], ca_recv.at[j], (d, partner))
+
+    c_get = pltpu.make_async_copy(cin_ref, c_buf, c_local.at[0])
+    c_put = pltpu.make_async_copy(c_buf, c_ref.at[f], c_local.at[1])
+    ow_get = pltpu.make_async_copy(ow_ref, ow_raw, ow_local.at[0])
     ow_put = pltpu.make_async_copy(ow_buf, owf_ref.at[d], ow_local.at[1])
     enter, send, relay, close = combiner(scratch, dtl_ref, bc_ref, n_f)
     i = pl.program_id(0)
@@ -66,14 +83,32 @@
     @pl.when(i == 0)
     def _():
         enter([((d + k) % n_dp, f) for k in range(1, n_dp)])
+        ow_get.start()
+        c_get.start()
+        for j in range(n_dp):
+
+            @pl.when(z < n_z - 1)
+            def _():
+                c_up(j, f).start()
+
+            @pl.when(z > 0)
+            def _():
+                c_down(j, f).start()
+
+            c_across(j, f).start()
+
+    @pl.when(i == 1)
+    def _():
+        ow_get.wait()
+        ow_buf[...] = ow_raw[...].astype(BF16)
+        c_get.wait()
+        c_put.start()
+
+    @pl.when(i == 2)
+    def _():
+        ow_put.start()
         for k in range(1, n_dp):
             ow(k).start()
-        ow_get.start()
-
-    @pl.when(i == 1)
-    def _():
-        ow_get.wait()
-        ow_put.start()
 
     @pl.when(i > 0)
     def _():
@@ -112,6 +147,22 @@
         for a in range(parts):
             relay(i * parts + a)
         close()
+        c_put.wait()
+        for j in range(n_dp):
+
+            @pl.when(z > 0)
+            def _():
+                c_up(j, f - 2).wait_recv()
+                c_down(j, f).wait_send()
+
+            @pl.when(z < n_z - 1)
+            def _():
+                c_down(j, f + 2).wait_recv()
+                c_up(j, f).wait_send()
+
+            c_across(j, partner).wait_recv()
+            c_across(j, f).wait_send()
+
         ow_put.wait()
         for k in range(1, n_dp):
             ow_arrival(k).wait_recv()
@@ -138,9 +189,75 @@
 
 
 def mix_kernel(
-    dtl_ref, bc_ref, inp_ref, gate_ref, dtw_ref, misc_ref, ow_ref,
-    y_ref, ck_ref, br_ref, h_scr, delta_scr, u_scr, rate_scr, even_scr, odd_scr, misc_scr, *, slots
+    dtl_ref, bc_ref, inp_ref, gate_ref, dtw_ref, misc_ref, ow_ref, near_ref,
+    y_ref, ck_ref, br_ref, c_ref, h_scr, delta_scr, u_scr, rate_scr, even_scr, odd_scr, misc_scr,
+    up_send, up_recv, down_send, down_recv, core_send, core_recv, *, slots, n_dp, n_f
 ):
+    d = lax.axis_index("dp")
+    f = lax.axis_index("fsdp")
+    n_z = n_f // 2
+    z = f // 2
+    core = f % 2
+    partner = z * 2 + 1 - core
+    i = pl.program_id(0)
+    last = pl.num_programs(0) - 1
+
+    def up(j, o):
+        ref = c_ref.at[o * 2 + core, j]
+        return remote(ref, ref, up_send.at[o, j], up_recv.at[o, j], (d, f + 2))
+
+    def down(j, o):
+        ref = c_ref.at[o * 2 + core, j]
+        return remote(ref, ref, down_send.at[o, j], down_recv.at[o, j], (d, f - 2))
+
+    def across(j, o, side):
+        ref = c_ref.at[o * 2 + side, j]
+        return remote(ref, ref, core_send.at[o, j], core_recv.at[o, j], (d, partner))
+
+    def far(k, js):
+        for j in js:
+
+            @pl.when(z >= k)
+            def _():
+                if k > 1:
+                    up(j, z - k).wait_recv()
+
+                @pl.when(z < n_z - 1)
+                def _():
+                    up(j, z - k).start()
+
+                across(j, z - k, core).start()
+
+            @pl.when(z + k < n_z)
+            def _():
+                if k > 1:
+                    down(j, z + k).wait_recv()
+
+                @pl.when(z > 0)
+                def _():
+                    down(j, z + k).start()
+
+                across(j, z + k, core).start()
+
+    @pl.when(i == 0)
+    def _():
+        barrier = pltpu.get_barrier_semaphore()
+        pl.semaphore_signal(barrier, inc=1, device_id=(d, partner), device_id_type=pl.DeviceIdType.MESH)
+        for k in range(1, n_z):
+            pl.semaphore_signal(
+                barrier, inc=1, device_id=(d, (z + k) % n_z * 2 + core), device_id_type=pl.DeviceIdType.MESH
+            )
+        pl.semaphore_wait(barrier, n_z)
+        far(1, range(n_dp))
+
+    @pl.when(i == 3)
+    def _():
+        far(2, range(n_dp // 2))
+
+    @pl.when(i == 5)
+    def _():
+        far(2, range(n_dp // 2, n_dp))
+
     rows, width = inp_ref.shape
     steps = rows // slots
     states = h_scr.shape[0]
@@ -189,6 +306,26 @@
     gate = gate_ref[...]
     gated = (y * (gate * sigmoid(gate))).astype(BF16)
     br_ref[...] = dot(gated, ow_ref[...]).astype(br_ref.dtype).reshape(br_ref.shape)
+
+    @pl.when(i == last)
+    def _():
+        for k in range(3, n_z):
+            far(k, range(n_dp))
+        for o in range(n_z):
+            for j in range(n_dp):
+
+                @pl.when(o != z)
+                def _():
+                    across(j, o, 1 - core).wait_recv()
+                    across(j, o, core).wait_send()
+
+                @pl.when((o < z) & (z < n_z - 1))
+                def _():
+                    up(j, o).wait_send()
+
+                @pl.when((o > z) & (z > 0))
+                def _():
+                    down(j, o).wait_send()
 
 
 def lane_sums(parts):
@@ -834,12 +971,13 @@
 
 def finish_kernel(
     gdtl_ref, gbc_ref, inp_ref, gis_ref, ggate_ref, inner_ref, before_ref, x_ref, gain_ref, win_ref, xw_ref, misc_ref,
-    gout_ref, gback_ref, br_ref, out_ref, brout_ref, gin_out, gout_out, gback_out, gtail_out, gg_out,
+    gout_ref, gback_ref, br_ref, out_ref, brout_ref, gin_out, gout_out,
+    gx_out, gcw_out, gcb_out, gdt_out, gdtb_out, gdec_out, gskip_out, gg_out,
     misc_scr, tail_scr, gin_scr, gsel_scr, grest_scr, ggain_scr, pad_scr, gpad_scr, wacc_scr, cacc_scr,
-    mine, theirs, passed, gin_low, gin_got, gin_sum, gin_all, gout_got, gback_got, gtail_low, gtail_got,
+    mine, theirs, passed, gin_low, side_got, line_got, side_end, line_end, gin_sum, gin_all, gout_got, gback_got, gtail_low, gtail_got,
     gg_low, gg_got, gg_sum, gg_all, br_buf, local_sem,
     one_send, one_recv, up_send, up_recv, down_send, down_recv, dp_send, dp_recv,
-    r_send, r_recv, w_send, w_recv, o_send, o_recv, b_send, b_recv, t_send, t_recv, g_send, g_recv,
+    r_send, r_recv, s1_send, s1_recv, l1_send, l1_recv, s2_send, s2_recv, l2_send, l2_recv, o_send, o_recv, b_send, b_recv, t_send, t_recv, g_send, g_recv,
     w2_send, w2_recv, g2_send, g2_recv, *, slots, n_dp, n_f
 ):
     d = lax.axis_index("dp")
@@ -914,7 +1052,64 @@
     put_branch = pltpu.make_async_copy(br_buf, brout_ref.at[d], local_sem.at[4])
     outs = lambda: over_dp(gout_ref, gout_got, o_send, o_recv)
     backs = lambda: over_dp(gback_ref, gback_got, b_send, b_recv)
-    ins = lambda: over_dp(gin_low, gin_got, w_send, w_recv)
+
+    n_a = n_dp // 2
+    half = n_f // 2
+    mine_a = d // 2
+    mine_b = d % 2
+    front_half, back_half = pl.ds(0, half), pl.ds(half, half)
+
+    def side_first(a):
+        return remote(
+            gin_low.at[a * 2 + 1 - mine_b, front_half], side_got.at[a], s1_send.at[a], s1_recv.at[a],
+            (mine_a * 2 + 1 - mine_b, f),
+        )
+
+    def line_first(k, b):
+        to = (mine_a + k) % n_a
+        return remote(
+            gin_low.at[to * 2 + b, back_half], line_got.at[k, b], l1_send.at[k, b], l1_recv.at[k, b],
+            (to * 2 + mine_b, f),
+        )
+
+    def line_second(k):
+        to = (mine_a + k) % n_a
+        return remote(
+            gin_low.at[to * 2 + mine_b, front_half], line_end.at[k], l2_send.at[k], l2_recv.at[k], (to * 2 + mine_b, f)
+        )
+
+    def side_second():
+        return remote(
+            gin_low.at[mine_a * 2 + 1 - mine_b, back_half], side_end, s2_send.at[0], s2_recv.at[0],
+            (mine_a * 2 + 1 - mine_b, f),
+        )
+
+    def firsts():
+        return [side_first(a) for a in range(n_a)] + [line_first(k, b) for k in range(1, n_a) for b in range(2)]
+
+    def seconds():
+        return [line_second(k) for k in range(1, n_a)] + [side_second()]
+
+    def middle():
+        for copy in firsts():
+            copy.wait_recv()
+
+        def add(q, carry):
+            for a in range(n_a):
+                at = a * 2 + mine_b
+                gin_low[at, q] = (gin_low[at, q].astype(F32) + side_got[a, q].astype(F32)).astype(gin_low.dtype)
+            for b in range(2):
+                at = mine_a * 2 + b
+                total = gin_low[at, half + q].astype(F32)
+                for k in range(1, n_a):
+                    total = total + line_got[k, b, q].astype(F32)
+                gin_low[at, half + q] = total.astype(gin_low.dtype)
+            return carry
+
+        lax.fori_loop(0, half, add, 0)
+        for copy in seconds():
+            copy.start()
+
     tails = lambda: over_dp(gtail_low, gtail_got, t_send, t_recv)
     gains = lambda: over_dp(gg_low, gg_got, g_send, g_recv)
     own_out = pltpu.make_async_copy(gout_ref.at[d], gout_got.at[0], local_sem.at[0])
@@ -1092,7 +1287,7 @@
             gtail_low[a, :, :rank] = gsel_scr[at : at + inner_rows, :]
             gtail_low[a, :, rank:] = grest_scr[at : at + inner_rows, :]
         send_halves(last)
-        for copy in ins() + tails() + gains():
+        for copy in firsts() + tails() + gains():
             copy.start()
         hops(blocks)
         get_branch.wait()
@@ -1108,29 +1303,42 @@
         total = gback_got[0]
         for k in range(1, n_dp):
             total = total + gback_got[k]
-        gback_out[...] = total
+        gdt_out[...] = total[:, :rank]
+        total = jnp.transpose(total[:, rank:])
+        gdec_out[...] = total[DECAY:TAPS, :]
+        gdtb_out[...] = total[DT_BIAS : DT_BIAS + 1, :]
+        gskip_out[...] = total[SKIP : SKIP + 1, :]
 
         def drain(step, carry):
             hops(step)
             return carry
 
-        lax.fori_loop(blocks + 1, blocks + 1 + LAG * (n_z - 1), drain, 0)
-
-        for copy in ins() + tails() + gains():
+        lax.fori_loop(blocks + 1, blocks + 1 + MID, drain, 0)
+        middle()
+        lax.fori_loop(blocks + 1 + MID, blocks + 1 + LAG * (n_z - 1), drain, 0)
+
+        for copy in seconds() + tails() + gains():
             copy.wait_recv()
 
         def add(q, carry):
             total = gin_low[d, q].astype(F32)
-            for k in range(1, n_dp):
-                total = total + gin_got[k, q].astype(F32)
+            for k in range(1, n_a):
+                total = total + line_end[k, q].astype(F32)
             gin_sum[q] = total.astype(gin_sum.dtype)
+            total = gin_low[d, half + q].astype(F32) + side_end[q].astype(F32)
+            gin_sum[half + q] = total.astype(gin_sum.dtype)
+            return carry
+
+        lax.fori_loop(0, half, add, 0)
+
+        def add_gain(q, carry):
             total = gg_low[d, q]
             for k in range(1, n_dp):
                 total = total + gg_got[k, q]
             gg_sum[q] = total
             return carry
 
-        lax.fori_loop(0, n_f, add, 0)
+        lax.fori_loop(0, n_f, add_gain, 0)
         for k in range(1, n_f):
             over_f(gin_sum, gin_all, w2_send, w2_recv, k).start()
             over_f(gg_sum, gg_all, g2_send, g2_recv, k).start()
@@ -1139,14 +1347,18 @@
         total = gtail_low[d]
         for k in range(1, n_dp):
             total = total + gtail_got[k]
-        gtail_out[...] = total
+        gx_out[:rank, :] = jnp.transpose(total[:, :rank])
+        total = jnp.transpose(total[:, rank:])
+        gx_out[rank:, :] = total[:DECAY, :]
+        gcw_out[...] = total[TAPS:CONV_BIAS, :]
+        gcb_out[...] = total[CONV_BIAS : CONV_BIAS + 1, :]
         for k in range(1, n_f):
             over_f_arrival(gin_sum, gin_all, w2_send, w2_recv, k).wait_recv()
             over_f_arrival(gg_sum, gg_all, g2_send, g2_recv, k).wait_recv()
         total = gg_all[0]
         for b in range(1, n_f):
             total = total + gg_all[b]
-        gg_out[...] = total
+        gg_out[...] = total[0:1, 0:d_rows]
         for b in range(n_f):
             for h in range(2):
                 for a in range(n_dp):
@@ -1161,7 +1373,7 @@
         for k in range(1, n_dp):
             branch_arrival(k).wait_recv()
             branch(k).wait_send()
-        for copy in outs() + backs() + ins() + tails() + gains():
+        for copy in outs() + backs() + firsts() + seconds() + tails() + gains():
             copy.wait_send()
         for k in range(1, n_f):
             over_f(gin_sum, gin_all, w2_send, w2_recv, k).wait_send()
@@ -1233,7 +1445,7 @@
     )
     misc = jnp.pad(misc, ((0, 0), (0, 128 - misc.shape[1])))
     packed = low(jnp.concatenate([x_weight[:, :rank], misc, dt_weight], axis=1))
-    ow = low(out_weight)
+    ow = out_weight
     n_z = n_f // 2
     dma = pltpu.SemaphoreType.DMA
     hbm = pl.BlockSpec(memory_space=pl.ANY)
@@ -1260,7 +1472,6 @@
         cost_estimate=cost(90),
         name="gather",
     )(tok, masked, win, gain_tile, packed)
-    g_branch = lax.all_gather(g_branch, "fsdp", axis=0, tiled=False)
     x = x.reshape(total_rows, model)
     win = win.reshape(model, 2 * width)
     gain = gain[:, :, 0, :d_rows].reshape(1, model)
@@ -1285,53 +1496,57 @@
     piece_spec = pl.BlockSpec(piece, lambda i: (i % per, i // per, 0, 0))
     rev_piece_spec = pl.BlockSpec(piece, lambda i: ((blocks - 1 - i) % per, (blocks - 1 - i) // per, 0, 0))
     pieces_shape = like((n_f, n_dp, own * slots, model), BF16)
-    inner, gate, inp, dtl, bc, ow = pl.pallas_call(
+    inner, gate, inp, dtl, bc, ow, g_branch = pl.pallas_call(
         functools.partial(front_kernel, slots=slots, length=length, n_dp=n_dp, n_f=n_f),
         grid=grid,
         in_specs=[
-            row_spec(model), whole((1, model)), win_spec, xw_spec, misc_spec, hbm,
+            row_spec(model), whole((1, model)), win_spec, xw_spec, misc_spec, hbm, hbm,
         ],
         out_specs=[
             row_spec(width), row_spec(width), row_spec(width), whole((total_rows, rank)), whole((total_rows, 2 * states)),
-            hbm,
+            hbm, hbm,
         ],
         out_shape=[
             like((total_rows, width), F32), like((total_rows, width), F32), like((total_rows, width), BF16),
-            like((total_rows, rank), BF16), like((total_rows, 2 * states), F32), like((n_dp,) + ow.shape, BF16),
+            like((total_rows, rank), BF16), like((total_rows, 2 * states), F32), like((n_dp,) + ow.shape, BF16), pieces_shape,
         ],
         scratch_shapes=[
-            pltpu.VMEM((rows + 3 * slots, width), F32), misc_shape, pltpu.VMEM(ow.shape, BF16),
-            dma((n_dp,)), dma((n_dp,)), dma((2,)),
+            pltpu.VMEM((rows + 3 * slots, width), F32), misc_shape, pltpu.VMEM(ow.shape, F32), pltpu.VMEM(ow.shape, BF16),
+            dma((n_dp,)), dma((n_dp,)), dma((2,)), pltpu.VMEM((n_dp, own * slots, model), BF16), dma((2,)),
         ]
+        + [dma((n_dp,))] * 6
         + combine_scratch(n_f, length, F32),
         compiler_params=params(2),
         cost_estimate=cost(42),
         name="front",
-    )(x, gain, win, packed, packed, ow)
+    )(x, gain, win, packed, packed, ow, g_branch)
     ow = ow.reshape(width, model)
 
 
-    y, ck, branch = pl.pallas_call(
-        functools.partial(mix_kernel, slots=slots),
+    y, ck, branch, g_branch = pl.pallas_call(
+        functools.partial(mix_kernel, slots=slots, n_dp=n_dp, n_f=n_f),
         grid=grid,
         in_specs=[
-            row_spec(rank), row_spec(2 * states), row_spec(width), row_spec(width), dtw_spec, misc_spec, ow_spec,
+            row_spec(rank), row_spec(2 * states), row_spec(width), row_spec(width), dtw_spec, misc_spec, ow_spec, hbm,
         ],
         out_specs=[
-            row_spec(width), pl.BlockSpec((1, states, slots, width), lambda i: (i, 0, 0, 0)), piece_spec,
+            row_spec(width), pl.BlockSpec((1, states, slots, width), lambda i: (i, 0, 0, 0)), piece_spec, hbm,
         ],
         out_shape=[
             like((total_rows, width), F32), like((blocks, states, slots, width), F32), pieces_shape,
+            pieces_shape,
         ],
         scratch_shapes=[
             pltpu.VMEM((states, slots, width), F32), pltpu.VMEM((rows, width), F32), pltpu.VMEM((rows, width), F32),
             pltpu.VMEM((states, slots, width), F32), pltpu.VMEM((PAIR, 2 * states, slots, 128), F32),
             pltpu.VMEM((PAIR, 2 * states, slots, 128), F32), misc_shape,
-        ],
-        compiler_params=params(),
+        ]
+        + [dma((n_z, n_dp))] * 6,
+        input_output_aliases={7: 3},
+        compiler_params=params(5),
         cost_estimate=cost(36),
         name="mix",
-    )(dtl, bc, inp, gate, packed, packed, ow)
+    )(dtl, bc, inp, gate, packed, packed, ow, g_branch)
 
     gis, ggate, gdtl, gbc, gout, gmisc, branch = pl.pallas_call(
         functools.partial(back_kernel, slots=slots, length=length, n_dp=n_dp, n_f=n_f),
@@ -1374,7 +1589,7 @@
 
     tile = own * slots
     vmem = pltpu.VMEM
-    g_normed, branch, gin, gout, gback, gtail, ggain = pl.pallas_call(
+    g_normed, branch, gin, gout, gx, gcw, gcb, gdt, gdtb, gdec, gskip, ggain = pl.pallas_call(
         functools.partial(finish_kernel, slots=slots, n_dp=n_dp, n_f=n_f),
         grid=grid,
         in_specs=[
@@ -1383,12 +1598,16 @@
             rev_spec(model), whole((1, model)), win_spec, xw_spec, misc_spec, hbm, hbm, hbm,
         ],
         out_specs=[
-            hbm, hbm, whole((d_rows, 2 * width * n_f)), whole((inner_rows, model)), whole((inner_rows, 256)),
-            whole((inner_rows, 256)), whole((8, 128)),
+            hbm, hbm, whole((d_rows, 2 * width * n_f)), whole((inner_rows, model)),
+            whole((rank + 2 * states, inner_rows)), whole((4, inner_rows)), whole((1, inner_rows)),
+            whole((inner_rows, rank)), whole((1, inner_rows)), whole((states, inner_rows)), whole((1, inner_rows)),
+            whole((1, d_rows)),
         ],
         out_shape=[
             like((n_dp, tile, model), BF16), like((n_dp, tile, model), BF16), like((d_rows, 2 * width * n_f), F32), like((inner_rows, model), F32),
-            like((inner_rows, 256), F32), like((inner_rows, 256), F32), like((8, 128), F32),
+            like((rank + 2 * states, inner_rows), F32), like((4, inner_rows), F32), like((1, inner_rows), F32),
+            like((inner_rows, rank), F32), like((1, inner_rows), F32), like((states, inner_rows), F32),
+            like((1, inner_rows), F32), like((1, d_rows), F32),
         ],
         scratch_shapes=[
             misc_shape, misc_shape, vmem((model, 2 * width), F32), vmem((width, 128), F32), vmem((width, 128), F32),
@@ -1396,7 +1615,9 @@
             vmem((4, slots, width), F32), vmem((slots, width), F32),
             vmem((n_f, n_dp, tile, model), BF16), vmem((n_z, n_dp, tile, model), BF16),
             vmem((n_z + 1, n_dp, tile, model), BF16),
-            vmem((n_dp, n_f, d_rows, 2 * width), BF16), vmem((n_dp, n_f, d_rows, 2 * width), BF16),
+            vmem((n_dp, n_f, d_rows, 2 * width), BF16), vmem((n_dp // 2, n_z, d_rows, 2 * width), BF16),
+            vmem((n_dp // 2, 2, n_z, d_rows, 2 * width), BF16), vmem((n_z, d_rows, 2 * width), BF16),
+            vmem((n_dp // 2, n_z, d_rows, 2 * width), BF16),
             vmem((n_f, d_rows, 2 * width), BF16), vmem((n_f, d_rows, 2 * width), BF16),
             vmem((n_dp, inner_rows, model), BF16), vmem((n_dp, inner_rows, 256), F32),
             vmem((n_dp, inner_rows, 256), F32), vmem((n_dp, inner_rows, 256), F32),
@@ -1404,7 +1625,12 @@
             vmem((n_f, 8, 128), F32), vmem((tile, model), BF16), dma((5,)),
         ]
         + [dma((n_z, n_dp))] * 6
-        + [dma((n_dp,))] * 14
+        + [dma((n_dp,))] * 4
+        + [dma((n_dp // 2,))] * 2
+        + [dma((n_dp // 2, 2))] * 2
+        + [dma((1,))] * 2
+        + [dma((n_dp // 2,))] * 2
+        + [dma((n_dp,))] * 8
         + [dma((n_f,))] * 4,
         compiler_params=params(4),
         cost_estimate=cost(105),
@@ -1423,12 +1649,9 @@
     input_grad = (
         upstream + factor * weighted - hidden * factor**3 * jnp.mean(hidden * weighted, axis=-1, keepdims=True)
     ).astype(BF16)
-    conv_bias_grad = gtail[:, rank + CONV_BIAS]
-    x_grad = gtail[:, : rank + 2 * states]
     return (
-        output, input_grad, ggain[0, :d_rows], gin, gtail[:, rank + TAPS : rank + TAPS + 4], conv_bias_grad, x_grad,
-        gback[:, :rank], gback[:, rank + DT_BIAS], gback[:, rank + DECAY : rank + DECAY + states],
-        gback[:, rank + SKIP], gout,
+        output, input_grad, ggain.reshape(d_rows), gin, gcw.T, gcb.reshape(inner_rows), gx.T, gdt,
+        gdtb.reshape(inner_rows), gdec.T, gskip.reshape(inner_rows), gout,
     )
 
 

time: 488 us -> 474 us (0.971)
  Pallas kernels: 420 us -> 434 us
  between operations: 14.3 us -> 0.94 us
  waiting for transfers between devices: 8.55 us -> 0 us
  local copies, waits for them, and re-layouts: 26.2 us -> 19.5 us
    pallas_call x1, Pallas kernels: 35.2 us -> 56.7 us  [body(): pl.pallas_call(functools.partial(mix_kernel, slots=slots, n_dp=n_dp, n_f=...]
    all_gather x1 -> x0, waiting for transfers between devices: 8.53 us -> none  [body(): g_branch = lax.all_gather(g_branch, 'fsdp', axis=0, tiled=False)]
    slice x5 -> x0, local copies, waits for them, and re-layouts: 6.47 us -> none  [the longest x1 1.62 us: body(): gback[:, rank + SKIP]]
  transfers between devices with their start and end apart: 1 -> 0, of which waited for: 1 -> 0; matrix products, arithmetic and copies ran while one was open for 1% -> 0% of each run, Pallas kernels for 18% -> 0%
where the time goes in v6:
time: 474 us; the launch traced here: 468 us
  Pallas kernels  434 us (92%)
  local copies, waits for them, and re-layouts  19.5 us (4%)
  other arithmetic  13.1 us (3%)
    pallas_call x1, Pallas kernels, body(): pl.pallas_call(functools.partial(finish_kernel, slots=slots, n_dp=n_dp, n...  122 us
    pallas_call x1, Pallas kernels, body(): pl.pallas_call(functools.partial(back_kernel, slots=slots, length=length,...  114 us
    pallas_call x1, Pallas kernels, body(): pl.pallas_call(functools.partial(gather_kernel, n_dp=n_dp, n_f=n_f), in_s...  94.9 us
    pallas_call x1, Pallas kernels, body(): pl.pallas_call(functools.partial(mix_kernel, slots=slots, n_dp=n_dp, n_f=...  56.7 us
    pallas_call x1, Pallas kernels, body(): pl.pallas_call(functools.partial(front_kernel, slots=slots, length=length...  47.3 us

profile of v6, /device:TPU:0, one launch (start us, length us, event | category | flops | bytes accessed | tf_op | source)
XLA Modules:
  0.0 467.8 jit_solution(2668476425748615514)
XLA Ops:
  0.7 0.9 select_reduce_fusion
  1.6 0.7 convert_bitcast_fusion.6
  2.2 0.7 convert_bitcast_fusion.5
  2.9 0.7 convert_bitcast_fusion.4
  3.6 0.7 convert_bitcast_fusion.3
  4.2 0.7 convert.41
  5.0 0.6 pad_convert_fusion.gain_ref
  5.6 0.7 convert.40
  6.3 0.7 slice.31
  7.9 0.8 convert.45
  8.8 0.8 slice.30
  9.7 0.7 fusion.9.pk_ref
  10.4 1.4 broadcast_select_fusion
  12.7 1.5 reshape.173.win_ref
  14.2 2.5 copy_bitcast_fusion.1
  16.7 94.9 %gather.1 = (bf16[4,8,64,2048]{3,2,1,0:T(8,128)(2,1)}, bf16[4,64,2048]{2,1,0:T(8,128)(2,1)}, bf16[4,8,64,1024]{3,2,1,0:T(8,128)(2,1)}, f32[4,8,8,128]{3,2,1,0:T(8,128)}, bf16[4,128,384]{2,1,0:T(8,128)(2,1)}) custom-call(bf16[4,64,2048]{2,1,0:T(8,128)(2,1)} %get-tuple-element.103.tok_ref, bf16[4,64,2048]{2,1,0:T(8,128)(2,1)} %get-tuple-element.102.cot_ref, ...), custom_call_target="tpu_custom_call" | custom-call | flops 103499997184 | bytes 1048576 | tf_op jit(solution)/shard_map/gather/pallas_call | solution.py:1452
  111.6 1.0 fusion.10
  112.6 0.7 mul.50
  113.2 0.7 reshape_squeeze.3.gain_ref
  113.9 47.3 %front.1 = (f32[2048,512]{1,0:T(8,128)}, f32[2048,512]{1,0:T(8,128)}, bf16[2048,512]{1,0:T(8,128)(2,1)}, bf16[2048,128]{1,0:T(8,128)(2,1)}, f32[2048,32]{1,0:T(8...) custom-call(bf16[2048,2048]{1,0:T(8,128)(2,1)} %bitcast.64, f32[1,2048]{1,0:T(1,128)} %reshape_squeeze.3.gain_ref, ...), custom_call_target="tpu_custom_call" | custom-call | flops 48299999232 | bytes 1048576 | tf_op jit(solution)/shard_map/front/pallas_call | solution.py:1499
  161.2 56.7 %mix.1 = (f32[2048,512]{1,0:T(8,128)}, f32[8,16,8,512]{3,2,1,0:T(8,128)}, bf16[8,4,64,2048]{3,2,1,0:T(8,128)(2,1)}, bf16[8,4,64,2048]{3,2,1,0:T(8,128)(2,1)}) custom-call(bf16[2048,128]{1,0:T(8,128)(2,1)} %get-tuple-element.64.dtl_ref, f32[2048,32]{1,0:T(8,128)} %get-tuple-element.65.bc_ref, ...), custom_call_target="tpu_custom_call", output_to_operand_aliasing={{3}: (7, {})} | custom-call | flops 41400000512 | bytes 1048576 | tf_op jit(solution)/shard_map/mix/pallas_call | solution.py:1526
  217.9 113.7 %back.1 = (f32[2048,512]{1,0:T(8,128)}, bf16[2048,512]{1,0:T(8,128)(2,1)}, bf16[2048,128]{1,0:T(8,128)(2,1)}, bf16[2048,32]{1,0:T(8,128)(2,1)}, bf16[512,2048]{1...) custom-call(bf16[8,4,64,2048]{3,2,1,0:T(8,128)(2,1)} %get-tuple-element.70.gb_ref, ...), custom_call_target="tpu_custom_call" | custom-call | flops 115000000512 | bytes 1048576 | tf_op jit(solution)/shard_map/back/pallas_call | solution.py:1551
  331.7 121.6 %finish.1 = (bf16[4,64,2048]{2,1,0:T(8,128)(2,1)}, bf16[4,64,2048]{2,1,0:T(8,128)(2,1)}, f32[64,8192]{1,0:T(8,128)}, f32[128,2048]{1,0:T(8,128)}, f32[160,128]{1...) custom-call(bf16[2048,128]{1,0:T(8,128)(2,1)} %get-tuple-element.74., ...), custom_call_target="tpu_custom_call" | custom-call | flops 120749998080 | bytes 1048576 | tf_op jit(solution)/shard_map/finish/pallas_call | solution.py:1592
  453.3 1.5 convert_bitcast_fusion.1
  454.7 1.2 copy.55
  456.2 1.2 copy.56
  458.7 2.2 fusion.4
  461.5 1.3 copy.76
  463.9 0.6 copy.79
  464.5 0.6 copy.80
  465.7 0.6 copy.82
  466.8 1.0 copy.84
  (58 shorter events, 6.1 us)
Async XLA Ops:
  0.6 11.1 %copy-start.3 = (f32[64,8192]{1,0:T(8,128)S(1)}, f32[64,8192]{1,0:T(8,128)}, u32[]{:S(2)}) copy-start(f32[64,8192]{1,0:T(8,128)} %param.21) | copy-start | bytes 6291460
  5.0 7.0 %copy-start.10 = (pred[32,8]{1,0:T(8,128)(4,1)}, pred[32,8]{1,0:T(8,128)(4,1)S(1)}, u32[]{:S(2)}) copy-start(pred[32,8]{1,0:T(8,128)(4,1)S(1)} %broadcast_compare_fusion) | copy-start | bytes 772
  12.2 2.0 copy-start
  454.7 1.2 copy-start.5
  456.2 1.3 copy-start.1
  456.2 1.3 copy-start.8
  457.5 1.2 copy-start.2
  457.5 1.2 copy-start.11
  458.7 2.2 copy-start.17
  458.7 2.7 copy-start.4
  461.4 1.4 copy-start.13
  461.4 2.0 copy-start.16
  461.4 2.5 copy-start.7
  461.4 3.1 copy-start.9
  461.4 3.7 copy-start.15
  461.5 4.2 copy-start.12
  461.5 4.8 %copy-start.14 = (f32[1,128]{1,0:T(1,128)S(1)}, f32[1,128]{1,0:T(1,128)}, u32[]{:S(2)}) copy-start(f32[1,128]{1,0:T(1,128)} %get-tuple-element.92) | copy-start | bytes 1540
  461.5 5.3 %copy-start.6 = (f32[128,2048]{1,0:T(8,128)S(1)}, f32[128,2048]{1,0:T(8,128)}, u32[]{:S(2)}) copy-start(f32[128,2048]{1,0:T(8,128)} %get-tuple-element.127) | copy-start | bytes 3145732

commit v7 on v6

--- a/solution.py
+++ b/solution.py
@@ -764,8 +764,6 @@
         g1(k).start()
     for k in range(1, n_dp):
         pk(k).start()
-    for k in range(1, n_dp):
-        cot_dp(k).start()
     for load, store in zip(loads, stores):
         load.wait()
         store.start()
@@ -780,6 +778,8 @@
     for k in range(1, n_dp):
         w2(k).start()
         g2(k).start()
+    for k in range(1, n_dp):
+        cot_dp(k).start()
     for far in range(1, n_z):
         for j in range(n_dp):
 

time: 474 us -> 476 us (level)
  no operation moved by 1% of the time
where the time goes in v7:
time: 476 us; the launch traced here: 469 us
  Pallas kernels  435 us (91%)
  local copies, waits for them, and re-layouts  19.5 us (4%)
  other arithmetic  13.1 us (3%)
    pallas_call x1, Pallas kernels, body(): pl.pallas_call(functools.partial(finish_kernel, slots=slots, n_dp=n_dp, n...  121 us
    pallas_call x1, Pallas kernels, body(): pl.pallas_call(functools.partial(back_kernel, slots=slots, length=length,...  114 us
    pallas_call x1, Pallas kernels, body(): pl.pallas_call(functools.partial(gather_kernel, n_dp=n_dp, n_f=n_f), in_s...  98 us
    pallas_call x1, Pallas kernels, body(): pl.pallas_call(functools.partial(mix_kernel, slots=slots, n_dp=n_dp, n_f=...  56.4 us
    pallas_call x1, Pallas kernels, body(): pl.pallas_call(functools.partial(front_kernel, slots=slots, length=length...  46.4 us

profile of v7, /device:TPU:0, one launch (start us, length us, event | category | flops | bytes accessed | tf_op | source)
XLA Modules:
  0.0 469.0 jit_solution(3968087176916626336)
XLA Ops:
  0.7 0.9 select_reduce_fusion
  1.6 0.7 convert_bitcast_fusion.6
  2.2 0.7 convert_bitcast_fusion.5
  2.9 0.7 convert_bitcast_fusion.4
  3.6 0.7 convert_bitcast_fusion.3
  4.2 0.7 convert.41
  5.0 0.6 pad_convert_fusion.gain_ref
  5.6 0.7 convert.40
  6.3 0.7 slice.31
  7.9 0.8 convert.45
  8.8 0.8 slice.30
  9.7 0.7 fusion.9.pk_ref
  10.4 1.4 broadcast_select_fusion
  12.7 1.5 reshape.173.win_ref
  14.2 2.5 copy_bitcast_fusion.1
  16.7 98.0 %gather.1 = (bf16[4,8,64,2048]{3,2,1,0:T(8,128)(2,1)}, bf16[4,64,2048]{2,1,0:T(8,128)(2,1)}, bf16[4,8,64,1024]{3,2,1,0:T(8,128)(2,1)}, f32[4,8,8,128]{3,2,1,0:T(8,128)}, bf16[4,128,384]{2,1,0:T(8,128)(2,1)}) custom-call(bf16[4,64,2048]{2,1,0:T(8,128)(2,1)} %get-tuple-element.103.tok_ref, bf16[4,64,2048]{2,1,0:T(8,128)(2,1)} %get-tuple-element.102.cot_ref, ...), custom_call_target="tpu_custom_call" | custom-call | flops 103499997184 | bytes 1048576 | tf_op jit(solution)/shard_map/gather/pallas_call | solution.py:1452
  114.7 1.0 fusion.10
  115.7 0.7 mul.50
  116.3 0.7 reshape_squeeze.3.gain_ref
  117.0 46.4 %front.1 = (f32[2048,512]{1,0:T(8,128)}, f32[2048,512]{1,0:T(8,128)}, bf16[2048,512]{1,0:T(8,128)(2,1)}, bf16[2048,128]{1,0:T(8,128)(2,1)}, f32[2048,32]{1,0:T(8...) custom-call(bf16[2048,2048]{1,0:T(8,128)(2,1)} %bitcast.64, f32[1,2048]{1,0:T(1,128)} %reshape_squeeze.3.gain_ref, ...), custom_call_target="tpu_custom_call" | custom-call | flops 48299999232 | bytes 1048576 | tf_op jit(solution)/shard_map/front/pallas_call | solution.py:1499
  163.4 56.4 %mix.1 = (f32[2048,512]{1,0:T(8,128)}, f32[8,16,8,512]{3,2,1,0:T(8,128)}, bf16[8,4,64,2048]{3,2,1,0:T(8,128)(2,1)}, bf16[8,4,64,2048]{3,2,1,0:T(8,128)(2,1)}) custom-call(bf16[2048,128]{1,0:T(8,128)(2,1)} %get-tuple-element.64.dtl_ref, f32[2048,32]{1,0:T(8,128)} %get-tuple-element.65.bc_ref, ...), custom_call_target="tpu_custom_call", output_to_operand_aliasing={{3}: (7, {})} | custom-call | flops 41400000512 | bytes 1048576 | tf_op jit(solution)/shard_map/mix/pallas_call | solution.py:1526
  219.9 113.7 %back.1 = (f32[2048,512]{1,0:T(8,128)}, bf16[2048,512]{1,0:T(8,128)(2,1)}, bf16[2048,128]{1,0:T(8,128)(2,1)}, bf16[2048,32]{1,0:T(8,128)(2,1)}, bf16[512,2048]{1...) custom-call(bf16[8,4,64,2048]{3,2,1,0:T(8,128)(2,1)} %get-tuple-element.70.gb_ref, ...), custom_call_target="tpu_custom_call" | custom-call | flops 115000000512 | bytes 1048576 | tf_op jit(solution)/shard_map/back/pallas_call | solution.py:1551
  333.6 120.8 %finish.1 = (bf16[4,64,2048]{2,1,0:T(8,128)(2,1)}, bf16[4,64,2048]{2,1,0:T(8,128)(2,1)}, f32[64,8192]{1,0:T(8,128)}, f32[128,2048]{1,0:T(8,128)}, f32[160,128]{1...) custom-call(bf16[2048,128]{1,0:T(8,128)(2,1)} %get-tuple-element.74., ...), custom_call_target="tpu_custom_call" | custom-call | flops 120749998080 | bytes 1048576 | tf_op jit(solution)/shard_map/finish/pallas_call | solution.py:1592
  454.5 1.5 convert_bitcast_fusion.1
  455.9 1.2 copy.55
  457.4 1.2 copy.56
  459.9 2.2 fusion.4
  462.7 1.3 copy.76
  465.1 0.6 copy.79
  465.7 0.6 copy.80
  466.9 0.6 copy.82
  468.0 1.0 copy.84
  (58 shorter events, 6.1 us)
Async XLA Ops:
  0.6 11.1 %copy-start.3 = (f32[64,8192]{1,0:T(8,128)S(1)}, f32[64,8192]{1,0:T(8,128)}, u32[]{:S(2)}) copy-start(f32[64,8192]{1,0:T(8,128)} %param.21) | copy-start | bytes 6291460
  5.0 7.0 %copy-start.10 = (pred[32,8]{1,0:T(8,128)(4,1)}, pred[32,8]{1,0:T(8,128)(4,1)S(1)}, u32[]{:S(2)}) copy-start(pred[32,8]{1,0:T(8,128)(4,1)S(1)} %broadcast_compare_fusion) | copy-start | bytes 772
  12.2 2.0 copy-start
  455.9 1.2 copy-start.5
  457.4 1.3 copy-start.1
  457.4 1.3 copy-start.8
  458.7 1.2 copy-start.2
  458.7 1.2 copy-start.11
  459.9 2.2 copy-start.17
  459.9 2.7 copy-start.4
  462.6 1.4 copy-start.13
  462.6 2.0 copy-start.16
  462.6 2.5 copy-start.7
  462.6 3.1 copy-start.9
  462.6 3.7 copy-start.15
  462.6 4.2 copy-start.12
  462.7 4.8 %copy-start.14 = (f32[1,128]{1,0:T(1,128)S(1)}, f32[1,128]{1,0:T(1,128)}, u32[]{:S(2)}) copy-start(f32[1,128]{1,0:T(1,128)} %get-tuple-element.92) | copy-start | bytes 1540
  462.7 5.3 %copy-start.6 = (f32[128,2048]{1,0:T(8,128)S(1)}, f32[128,2048]{1,0:T(8,128)}, u32[]{:S(2)}) copy-start(f32[128,2048]{1,0:T(8,128)} %get-tuple-element.127) | copy-start | bytes 3145732
